TPU v7x, 128 devices: a whole 4x4x4 slice. The times are simulated.
128 devices in a mesh: leaf: 128 (over y, z, x, core).
Axes of the slice: x: 4, y: 4, z: 4, core: 2. Of those that a mesh axis runs over, the one named last changes fastest.
Arguments:
- right_hand: float32 [2048, 32, 256], P('leaf')
- leaf_live: int32 [2048], P('leaf'), may hold values from 0 to 1, as said below
- near_index: int32 [2048, 6], P('leaf'), may hold values from 0 to 2047, as said below
- near_tile: bfloat16 [2048, 6, 256, 256], P('leaf'), may hold values from -1 to 5
- far_index: int32 [2048, 8], P('leaf'), may hold values from 0 to 2047, as said below
- far_couple: bfloat16 [2048, 8, 64, 64], P('leaf'), may hold values from -0.25 to 0.25
- leaf_basis: bfloat16 [2048, 64, 256], P('leaf'), may hold values from -0.375 to 0.375
- leaf_transfer: bfloat16 [2048, 64, 64], P('leaf'), may hold values from -0.1875 to 0.1875
- tree_up: bfloat16 [254, 64, 64], replicated, may hold values from -0.5 to 0.5
- tree_couple: bfloat16 [254, 64, 64], replicated, may hold values from -0.75 to 0.75
Outputs:
- basis_next: float32 [2048, 32, 256], P('leaf')
- hessenberg: float32 [6, 32], replicated
Inputs may be any that keep to these rules, and one draw needn't show every extreme that they name: `leaf_live`: each device's 16 slots hold between 5 and 16 live leaves, both counts reached on some device; which slots are live is arbitrary. `near_index`: entry 0 of each row is the row's own slot; every entry lies within 2 slots of its row's slot, and some entry lies exactly 2 away; entries may name dead slots. `far_index`: every entry lies within 16 slots of its row's slot, and some entry lies exactly 16 away; entries may name dead slots.
All inputs are finite; a program needn't handle non-finite values.
Results may differ from a plain program's by a relative error of at most 0.009.
Values may be sent and summed in bfloat16 or wider, within the bound.
No kernel may reach another device: no remote copies, remote signals or barrier semaphores. Data moves between devices by JAX's collectives and lax.ppermute only.
A program may use at most 128 MiB of HBM per device.

v0:
```python
import jax
import jax.numpy as jnp
from jax import lax
from jax.sharding import PartitionSpec as P

epsilon = 1e-06


def with_halo(array, sides, width):
    for axis, dim in sides:
        size, length = (lax.axis_size(axis), array.shape[dim])
        up = [(i, (i + 1) % size) for i in range(size - 1)]
        down = [(j, i) for i, j in up]
        last = lax.slice_in_dim(array, length - width, length, axis=dim)
        initial = lax.slice_in_dim(array, 0, width, axis=dim)
        before = lax.ppermute(last, axis, up)
        after = lax.ppermute(initial, axis, down)
        array = jnp.concatenate([before, array, after], axis=dim)
    return array


def swapped(array, axis, stride):
    return lax.ppermute(array, axis, [(i, i ^ 1 << stride) for i in range(lax.axis_size(axis))])


def apply_operator(
    vector,
    leaf_live,
    near_index,
    near_tile,
    far_index,
    far_couple,
    leaf_basis,
    leaf_transfer,
    tree_up,
    tree_couple,
):
    position = lax.axis_index("leaf")
    device_total = lax.axis_size("leaf")
    slot_count = vector.shape[0]
    live_mask = leaf_live.astype(jnp.float32)[:, None, None]
    inputs = (vector * live_mask).astype(jnp.bfloat16)
    padded = with_halo(inputs, (("leaf", 0),), slot_count)
    local_near = near_index - (position * slot_count - slot_count)
    columns = padded[local_near]
    near = jnp.einsum("inrp,inpq->irq", columns, near_tile, preferred_element_type=jnp.float32)
    moments = jnp.einsum(
        "irp,ikp->irk", inputs, leaf_basis, preferred_element_type=jnp.float32
    ).astype(jnp.bfloat16)
    moment_pad = with_halo(moments, (("leaf", 0),), slot_count)
    local_far = far_index - (position * slot_count - slot_count)
    far_term = jnp.einsum(
        "ifrk,ifkj->irj", moment_pad[local_far], far_couple, preferred_element_type=jnp.float32
    )
    box_moment = jnp.einsum(
        "irk,ikj->rj", moments, leaf_transfer, preferred_element_type=jnp.float32
    ).astype(jnp.bfloat16)
    levels = device_total.bit_length() - 1
    locals_list = []
    current = box_moment
    for level in range(levels):
        level_first = 2 * device_total - 2 * (device_total >> level)
        own_node = level_first + (position >> level)
        other_node = level_first + (position >> level ^ 1)
        sibling = swapped(current, "leaf", level)
        locals_list.append(
            jnp.dot(sibling, tree_couple[own_node], preferred_element_type=jnp.float32)
        )
        lifted = jnp.dot(current, tree_up[own_node], preferred_element_type=jnp.float32) + jnp.dot(
            sibling, tree_up[other_node], preferred_element_type=jnp.float32
        )
        current = lifted.astype(jnp.bfloat16)
    downward = jnp.zeros(box_moment.shape, jnp.bfloat16)
    for level in reversed(range(levels)):
        level_first = 2 * device_total - 2 * (device_total >> level)
        own_node = level_first + (position >> level)
        carried = jnp.einsum(
            "rj,kj->rk", downward, tree_up[own_node], preferred_element_type=jnp.float32
        )
        downward = (locals_list[level] + carried).astype(jnp.bfloat16)
    leaf_down = jnp.einsum(
        "rj,ikj->irk", downward, leaf_transfer, preferred_element_type=jnp.float32
    )
    local_total = (far_term + leaf_down).astype(jnp.bfloat16)
    spread = jnp.einsum("irk,ikp->irp", local_total, leaf_basis, preferred_element_type=jnp.float32)
    return live_mask * (near + spread)


def column_sums(first_field, second_field):
    return jnp.sum(first_field * second_field, axis=(0, 2))


def global_norm(field):
    return jnp.sqrt(lax.psum(column_sums(field, field), "leaf") + epsilon)


def inner_sums(stacked):
    return lax.psum(stacked, "leaf")


def on_device(
    right_hand,
    leaf_live,
    near_index,
    near_tile,
    far_index,
    far_couple,
    leaf_basis,
    leaf_transfer,
    tree_up,
    tree_couple,
):

    def operator(vector):
        return apply_operator(
            vector,
            leaf_live,
            near_index,
            near_tile,
            far_index,
            far_couple,
            leaf_basis,
            leaf_transfer,
            tree_up,
            tree_couple,
        )

    live_mask = leaf_live.astype(jnp.float32)[:, None, None]
    start_vec = right_hand * live_mask
    norm_start = global_norm(start_vec)
    basis_one = start_vec / norm_start[None, :, None]
    image_one = operator(basis_one)
    first_inner = inner_sums(column_sums(basis_one, image_one)[None])[0]
    residue_one = image_one - first_inner[None, :, None] * basis_one
    first_length = global_norm(residue_one)
    basis_two = residue_one / first_length[None, :, None]
    image_two = operator(basis_two)
    both_inner = inner_sums(
        jnp.stack([column_sums(basis_one, image_two), column_sums(basis_two, image_two)])
    )
    cross_inner = both_inner[0]
    self_inner = both_inner[1]
    residue_two = (
        image_two - cross_inner[None, :, None] * basis_one - self_inner[None, :, None] * basis_two
    )
    second_length = global_norm(residue_two)
    basis_next = residue_two / second_length[None, :, None]
    hessenberg = jnp.stack(
        [norm_start, first_inner, first_length, cross_inner, self_inner, second_length]
    )
    return (basis_next, hessenberg)


def solution(mesh):
    placed = (
        P("leaf", None, None),
        P("leaf"),
        P("leaf", None),
        P("leaf", None, None, None),
        P("leaf", None),
        P("leaf", None, None, None),
        P("leaf", None, None),
        P("leaf", None, None),
        P(),
        P(),
    )
    return jax.shard_map(
        on_device,
        mesh=mesh,
        in_specs=placed,
        out_specs=(P("leaf", None, None), P()),
        check_vma=False,
    )
```

profile of v0, /device:TPU:1, one launch (start us, length us, event | category | flops | bytes accessed | tf_op | source)
XLA Modules:
  0.0 563.7 jit_solution(7283835769958912221)
XLA Ops:
  2.7 68.7 %psum.35 = f32[32]{0:T(128)S(1)} all-reduce(f32[32]{0:T(128)S(1)} %multiply_reduce_fusion.5), channel_id=1, replica_groups=mesh['leaf'=128] {'leaf'}, use_global_device_ids=true, to_apply=%region_1.0 | all-reduce | flops 32 | bytes 256 | tf_op jit(solution)/shard_map/psum | solution.py:94
  75.2 2.6 collective-permute-start.2
  77.8 2.4 collective-permute-start.3
  80.2 3.2 collective-permute-start
  86.2 12.0 %constant_dynamic-slice_fusion.2 = (bf16[1,64,64]{0,2,1:T(8,128)(2,1)}, bf16[1,64,64]{0,2,1:T(8,128)(2,1)}, bf16[1,64,64]{0,2,1:T(8,128)(2,1)}, bf16[1,64,64]{0,...) fusion(bf16[254,64,64]{0,2,1:T(8,128)(2,1)} %param.18, ...), kind=kLoop, calls=%fused_computation.177 | loop fusion | bytes 213044 | tf_op jit(solution)/shard_map/dynamic_slice | solution.py:70
  103.8 9.0 %constant_dynamic-slice_fusion.19 = (bf16[1,64,64]{0,2,1:T(8,128)(2,1)S(1)}, bf16[1,64,64]{0,2,1:T(8,128)(2,1)}, bf16[1,64,64]{0,2,1:T(8,128)(2,1)}, bf16[1,64,6...) fusion(bf16[254,64,64]{0,2,1:T(8,128)(2,1)} %param.19, ...), kind=kLoop, calls=%fused_computation.194 | loop fusion | bytes 114716 | tf_op jit(solution)/shard_map/dynamic_slice | solution.py:67
  126.0 2.3 copy.47
  141.9 2.3 copy.57
  151.5 3.3 collective-permute-start.6
  156.7 4.8 collective-permute-start.7
  163.4 3.6 collective-permute-start.8
  168.9 5.7 %collective-permute-start.9 = (bf16[32,64]{1,0:T(8,128)(2,1)S(1)}, bf16[32,64]{1,0:T(8,128)(2,1)S(1)}, u32[]{:S(2)}, u32[]{:S(2)}) collective-permute-start(bf16[32,64]{1,0:T(8,128)(2,1)S(1)} %fusion.21), channel_id=1, source_target_pairs={{0,32},{1,33},{2,34},{3,35},{4,36},{5,37},{6,38},{7,39},{8,40},{9,... | collective-permute-start | bytes 12296 | tf_op jit(solution)/shard_map/ppermute | solution.py:23
  177.0 3.1 collective-permute-start.10
  183.6 2.3 copy.55
  211.0 3.0 gather_fusion
  214.0 8.1 %multiply_reduce_fusion.4 = (f32[32]{0:T(128)S(1)}, f32[16,32,256]{2,1,0:T(8,128)}) fusion(f32[32]{0:T(128)S(1)} %copy-done.19, f32[16,32,256]{2,1,0:T(8,128)S(1)} %copy-done.1, f32[16]{0:T(128)S(1)} %copy-done.11, f32[16,32,256]{2,1,0:T(8,128)} %fusion.9, bf16[16,6,32,256]{3,2,1,0:T(8,128)(2,1)} %bitcast.261, bf16[16,6,256,256]{3,2,1,0:T(8,128)(2,1)} %param.13), kind=kOutput, calls=%fused_computation.101 | convolution fusion | flops 403439584 | bytes 15728960 | tf_op jit(solution)/shard_map/inrp,inpq->irq/dot_general | solution.py:46
  222.2 67.2 %psum.36 = f32[1,32]{1,0:T(1,128)S(1)} all-reduce(f32[1,32]{1,0:T(1,128)S(1)} %bitcast.268), channel_id=1, replica_groups=mesh['leaf'=128] {'leaf'}, use_global_device_ids=true, to_apply=%region_3.0 | all-reduce | flops 32 | bytes 256 | tf_op jit(solution)/shard_map/psum | solution.py:98
  290.7 62.8 %psum.37 = f32[32]{0:T(128)S(1)} all-reduce(f32[32]{0:T(128)S(1)} %multiply_reduce_fusion.3), channel_id=1, replica_groups=mesh['leaf'=128] {'leaf'}, use_global_device_ids=true, to_apply=%region_5.0 | all-reduce | flops 32 | bytes 256 | tf_op jit(solution)/shard_map/psum | solution.py:94
  381.9 8.1 %collective-permute-start.11 = (bf16[16,32,256]{2,1,0:T(8,128)(2,1)}, bf16[16,32,256]{2,1,0:T(8,128)(2,1)}, u32[]{:S(2)}, u32[]{:S(2)}) collective-permute-start(bf16[16,32,256]{2,1,0:T(8,128)(2,1)} %get-tuple-element.6), channel_id=1, source_target_pairs={{0,1},{1,2},{2,3},{3,4},{4,5},{5,6},{6,7},{7,8},{8,9},{9,10},{10,1... | collective-permute-start | bytes 786440 | tf_op jit(solution)/shard_map/ppermute | solution.py:16
  391.9 3.6 collective-permute-start.13
  408.0 2.4 convolution_bitcast_fusion.3
  415.8 8.4 %multiply_reduce_fusion.2 = (f32[32]{0:T(128)S(1)}, f32[32]{0:T(128)S(1)}, f32[16,32,256]{2,1,0:T(8,128)}) fusion(f32[32]{0:T(128)S(1)} %copy-done.20, f32[16,32,256]{2,1,0:T(8,128)S(1)} %copy-done.1, f32[16]{0:T(128)S(1)} %copy-done.12, f32[16,32,256]{2,1,0:T(8,128)} %get-tuple-element.7, f32[16,32,256]{2,1,0:T(8,128)} %fusion.8, ...), kind=kOutput, calls=%fused_computation.97 | convolution fusion | flops 403701696 | bytes 16253376 | tf_op jit(solution)/shard_map/inrp,inpq->irq/dot_general | solution.py:46
  424.2 70.6 %psum.38 = f32[2,32]{1,0:T(2,128)S(1)} all-reduce(f32[2,32]{1,0:T(2,128)S(1)} %pad_maximum_fusion.4), channel_id=1, replica_groups=mesh['leaf'=128] {'leaf'}, use_global_device_ids=true, to_apply=%region_8.0 | all-reduce | flops 64 | bytes 512 | tf_op jit(solution)/shard_map/psum | solution.py:98
  497.0 64.1 %psum.39 = f32[32]{0:T(128)S(1)} all-reduce(f32[32]{0:T(128)S(1)} %get-tuple-element.4), channel_id=1, replica_groups=mesh['leaf'=128] {'leaf'}, use_global_device_ids=true, to_apply=%region_10.0 | all-reduce | flops 32 | bytes 256 | tf_op jit(solution)/shard_map/psum | solution.py:94
  (175 shorter events, 139.2 us)
Async XLA Ops:
  0.6 205.1 %copy-start = (bf16[16,8,64,64]{3,2,1,0:T(8,128)(2,1)S(1)}, bf16[16,8,64,64]{3,2,1,0:T(8,128)(2,1)}, u32[]{:S(2)}) copy-start(bf16[16,8,64,64]{3,2,1,0:T(8,128)(2,1)} %param.15) | copy-start | bytes 3145732
  75.2 127.6 %collective-permute-start.2 = (bf16[16,32,64]{2,1,0:T(8,128)(2,1)S(1)}, bf16[16,32,64]{2,1,0:T(8,128)(2,1)}, u32[]{:S(2)}, u32[]{:S(2)}) collective-permute-start(bf16[16,32,64]{2,1,0:T(8,128)(2,1)S(1)} %convolution_convert_fusion.1), channel_id=1, source_target_pairs={{0,1},{1,2},{2,3},{3,4},{4,5},{5,6},{6,7},{7,8},{8,9},{9,10},{10,1... | collective-permute-start | bytes 196616 | tf_op jit(solution)/shard_map/ppermute | solution.py:16
  77.8 125.0 %collective-permute-start.3 = (bf16[16,32,64]{2,1,0:T(8,128)(2,1)S(1)}, bf16[16,32,64]{2,1,0:T(8,128)(2,1)}, u32[]{:S(2)}, u32[]{:S(2)}) collective-permute-start(bf16[16,32,64]{2,1,0:T(8,128)(2,1)S(1)} %convolution_convert_fusion.1), channel_id=1, source_target_pairs={{1,0},{2,1},{3,2},{4,3},{5,4},{6,5},{7,6},{8,7},{9,8},{10,9},{11,1... | collective-permute-start | bytes 196616 | tf_op jit(solution)/shard_map/ppermute | solution.py:17
  80.2 128.6 %collective-permute-start = (bf16[16,32,256]{2,1,0:T(8,128)(2,1)}, bf16[16,32,256]{2,1,0:T(8,128)(2,1)}, u32[]{:S(2)}, u32[]{:S(2)}) collective-permute-start(bf16[16,32,256]{2,1,0:T(8,128)(2,1)} %multiply_convert_fusion.1), channel_id=1, source_target_pairs={{0,1},{1,2},{2,3},{3,4},{4,5},{5,6},{6,7},{7,8},{8,9},{9,10},{10,1... | collective-permute-start | bytes 786440 | tf_op jit(solution)/shard_map/ppermute | solution.py:16
  83.4 125.4 %collective-permute-start.1 = (bf16[16,32,256]{2,1,0:T(8,128)(2,1)}, bf16[16,32,256]{2,1,0:T(8,128)(2,1)}, u32[]{:S(2)}, u32[]{:S(2)}) collective-permute-start(bf16[16,32,256]{2,1,0:T(8,128)(2,1)} %multiply_convert_fusion.1), channel_id=1, source_target_pairs={{1,0},{2,1},{3,2},{4,3},{5,4},{6,5},{7,6},{8,7},{9,8},{10,9},{11,1... | collective-permute-start | bytes 786440 | tf_op jit(solution)/shard_map/ppermute | solution.py:17
  86.2 60.8 %collective-permute-start.4 = (bf16[32,64]{1,0:T(8,128)(2,1)}, bf16[32,64]{1,0:T(8,128)(2,1)}, u32[]{:S(2)}, u32[]{:S(2)}) collective-permute-start(bf16[32,64]{1,0:T(8,128)(2,1)} %fusion.10), channel_id=1, source_target_pairs={{0,1},{1,0},{2,3},{3,2},{4,5},{5,4},{6,7},{7,6},{8,9},{9,8},{10,11... | collective-permute-start | bytes 12296 | tf_op jit(solution)/shard_map/ppermute | solution.py:23
  147.8 2.9 collective-permute-start.5
  151.5 4.4 collective-permute-start.6
  156.7 5.8 %collective-permute-start.7 = (bf16[32,64]{1,0:T(8,128)(2,1)S(1)}, bf16[32,64]{1,0:T(8,128)(2,1)S(1)}, u32[]{:S(2)}, u32[]{:S(2)}) collective-permute-start(bf16[32,64]{1,0:T(8,128)(2,1)S(1)} %fusion.17), channel_id=1, source_target_pairs={{0,8},{1,9},{2,10},{3,11},{4,12},{5,13},{6,14},{7,15},{8,0},{9,1},... | collective-permute-start | bytes 12296 | tf_op jit(solution)/shard_map/ppermute | solution.py:23
  163.4 4.6 collective-permute-start.8
  168.9 6.7 %collective-permute-start.9 = (bf16[32,64]{1,0:T(8,128)(2,1)S(1)}, bf16[32,64]{1,0:T(8,128)(2,1)S(1)}, u32[]{:S(2)}, u32[]{:S(2)}) collective-permute-start(bf16[32,64]{1,0:T(8,128)(2,1)S(1)} %fusion.21), channel_id=1, source_target_pairs={{0,32},{1,33},{2,34},{3,35},{4,36},{5,37},{6,38},{7,39},{8,40},{9,... | collective-permute-start | bytes 12296 | tf_op jit(solution)/shard_map/ppermute | solution.py:23
  177.0 19.0 %collective-permute-start.10 = (bf16[32,64]{1,0:T(8,128)(2,1)}, bf16[32,64]{1,0:T(8,128)(2,1)}, u32[]{:S(2)}, u32[]{:S(2)}) collective-permute-start(bf16[32,64]{1,0:T(8,128)(2,1)} %fusion.23), channel_id=1, source_target_pairs={{0,64},{1,65},{2,66},{3,67},{4,68},{5,69},{6,70},{7,71},{8,72},{9,... | collective-permute-start | bytes 12296 | tf_op jit(solution)/shard_map/ppermute | solution.py:23
  357.7 1.5 collective-permute-start.15
  360.1 2.5 collective-permute-start.16
  363.5 4.0 collective-permute-start.17
  368.3 2.5 collective-permute-start.18
  371.6 4.1 collective-permute-start.19
  376.6 2.8 collective-permute-start.20
  380.2 17.5 %collective-permute-start.21 = (bf16[32,64]{1,0:T(8,128)(2,1)S(1)}, bf16[32,64]{1,0:T(8,128)(2,1)S(1)}, u32[]{:S(2)}, u32[]{:S(2)}) collective-permute-start(bf16[32,64]{1,0:T(8,128)(2,1)S(1)} %fusion.36), channel_id=1, source_target_pairs={{0,64},{1,65},{2,66},{3,67},{4,68},{5,69},{6,70},{7,71},{8,72},{9,... | collective-permute-start | bytes 12296 | tf_op jit(solution)/shard_map/ppermute | solution.py:23
  381.9 30.8 %collective-permute-start.11 = (bf16[16,32,256]{2,1,0:T(8,128)(2,1)}, bf16[16,32,256]{2,1,0:T(8,128)(2,1)}, u32[]{:S(2)}, u32[]{:S(2)}) collective-permute-start(bf16[16,32,256]{2,1,0:T(8,128)(2,1)} %get-tuple-element.6), channel_id=1, source_target_pairs={{0,1},{1,2},{2,3},{3,4},{4,5},{5,6},{6,7},{7,8},{8,9},{9,10},{10,1... | collective-permute-start | bytes 786440 | tf_op jit(solution)/shard_map/ppermute | solution.py:16
  390.0 22.7 %collective-permute-start.12 = (bf16[16,32,256]{2,1,0:T(8,128)(2,1)}, bf16[16,32,256]{2,1,0:T(8,128)(2,1)}, u32[]{:S(2)}, u32[]{:S(2)}) collective-permute-start(bf16[16,32,256]{2,1,0:T(8,128)(2,1)} %get-tuple-element.6), channel_id=1, source_target_pairs={{1,0},{2,1},{3,2},{4,3},{5,4},{6,5},{7,6},{8,7},{9,8},{10,9},{11,1... | collective-permute-start | bytes 786440 | tf_op jit(solution)/shard_map/ppermute | solution.py:17
  391.9 12.5 %collective-permute-start.13 = (bf16[16,32,64]{2,1,0:T(8,128)(2,1)S(1)}, bf16[16,32,64]{2,1,0:T(8,128)(2,1)S(1)}, u32[]{:S(2)}, u32[]{:S(2)}) collective-permute-start(bf16[16,32,64]{2,1,0:T(8,128)(2,1)S(1)} %convolution_convert_fusion), channel_id=1, source_target_pairs={{0,1},{1,2},{2,3},{3,4},{4,5},{5,6},{6,7},{7,8},{8,9},{9,10},{10,1... | collective-permute-start | bytes 196616 | tf_op jit(solution)/shard_map/ppermute | solution.py:16
  395.5 9.5 %collective-permute-start.14 = (bf16[16,32,64]{2,1,0:T(8,128)(2,1)S(1)}, bf16[16,32,64]{2,1,0:T(8,128)(2,1)}, u32[]{:S(2)}, u32[]{:S(2)}) collective-permute-start(bf16[16,32,64]{2,1,0:T(8,128)(2,1)S(1)} %convolution_convert_fusion), channel_id=1, source_target_pairs={{1,0},{2,1},{3,2},{4,3},{5,4},{6,5},{7,6},{8,7},{9,8},{10,9},{11,1... | collective-permute-start | bytes 196616 | tf_op jit(solution)/shard_map/ppermute | solution.py:17
  424.2 138.9 %copy-start.22 = (f32[1,32]{1,0:T(1,128)S(1)}, f32[1,32]{1,0:T(1,128)}, u32[]{:S(2)}) copy-start(f32[1,32]{1,0:T(1,128)} %copy-done.21) | copy-start | bytes 388
  (23 other events, 776.6 us)
where the time goes:
time: 570 us; the launch traced here: 564 us
  blocking collectives  333 us (58%)
  local copies, waits for them, and re-layouts  78.7 us (14%)
  matrix products  63.4 us (11%)
  starting transfers between devices  56.1 us (10%)
  other arithmetic  23.2 us (4%)
  waiting for transfers between devices  7.84 us (1%)
    psum x3, blocking collectives, global_norm(): return jnp.sqrt(lax.psum(column_sums(field, field), 'leaf') + epsilon)  196 us
    psum x2, blocking collectives, inner_sums(): return lax.psum(stacked, 'leaf')  138 us
    unnamed x70, local copies, waits for them, and re-layouts  43.1 us
    ppermute x14, starting transfers between devices, swapped(): lax.ppermute(array, axis, [(i, i ^ 1 << stride) for i in range(lax.axis_s...  30.2 us
    ppermute x4, starting transfers between devices, with_halo(): before = lax.ppermute(last, axis, up)  17.5 us
    dot_general x2, matrix products, apply_operator(): jnp.einsum('inrp,inpq->irq', columns, near_tile, preferred_element_type=j...  16.5 us
    dot_general x13, matrix products, apply_operator(): jnp.einsum('rj,kj->rk', downward, tree_up[own_node], preferred_element_ty...  13.2 us
    dynamic_slice x1, local copies, waits for them, and re-layouts, apply_operator(): tree_up[other_node]  12 us
  transfers between devices with their start and end apart: 22, of which 11 were waited for; matrix products, arithmetic and copies ran while one was open for 21% of the time, Pallas kernels for 0%

commit v1 on v0

v1 whole, which is shorter than its diff:
```python
import functools

import jax
import jax.numpy as jnp
from jax import lax
from jax.experimental import pallas as pl
from jax.experimental.pallas import tpu as pltpu
from jax.sharding import PartitionSpec as P

EPSILON = 1e-06
F32 = jnp.float32
BF16 = jnp.bfloat16
NT = (((1,), (1,)), ((), ()))

VMEM = pl.BlockSpec(memory_space=pltpu.VMEM)
SMEM = pl.BlockSpec(memory_space=pltpu.SMEM)
ANY = pl.BlockSpec(memory_space=pl.ANY)

SLOTS, RHS, POINTS, RANK = 16, 32, 256, 64
REACH = 2
HALF = SLOTS // 2
MOM_ROWS = HALF * RHS
NEAR_ROWS = REACH * 2 * RHS
BOX_AT = MOM_ROWS + NEAR_ROWS
PAIR_ROWS = BOX_AT + RHS
DEVICES = 128
LEVELS = 7
CHIPS = DEVICES // 2


def dot(a, b):
    return jnp.dot(a, b, preferred_element_type=F32)


def dot_nt(a, b):
    return lax.dot_general(a, b, NT, preferred_element_type=F32)


def row_sum(x):
    return jnp.sum(x, axis=1, keepdims=True)


def lanes(shape=(RHS, 128)):
    return lax.broadcasted_iota(jnp.int32, shape, 1)


def rows(shape=(RHS, 128)):
    return lax.broadcasted_iota(jnp.int32, shape, 0)


def level_start(level):
    return 2 * DEVICES - 2 * (DEVICES >> level)


def three_parts(column):
    high = column.astype(BF16).astype(F32)
    rest = column - high
    middle = rest.astype(BF16).astype(F32)
    low = (rest - middle).astype(BF16).astype(F32)
    return high, middle, low


def message(moment, sums):
    block = jnp.concatenate([moment.astype(F32), jnp.zeros((RHS, 128 - RANK), F32)], axis=1)
    at = lanes()
    for j, column in enumerate(sums):
        for k, part in enumerate(three_parts(column)):
            block = jnp.where(at == RANK + 3 * j + k, part, block)
    return block.astype(BF16)


def read_sum(block, j):
    at = lanes()
    first = RANK + 3 * j
    return row_sum(jnp.where((at >= first) & (at < first + 3), block, 0.0))


def pack_out(inputs, moments, box, sums, pa_ref, pb_ref, own_ref):
    block = message(box.astype(BF16), sums)
    own_ref[...] = block
    pa_ref[BOX_AT:PAIR_ROWS, :] = block
    for g in range(HALF):
        both = jnp.concatenate([moments[g], moments[g + HALF]], axis=1).astype(BF16)
        pa_ref[g * RHS : (g + 1) * RHS, :] = both
        pb_ref[g * RHS : (g + 1) * RHS, :] = both
    odd = lax.rem(lax.axis_index("leaf"), 2)

    def edge(ref, first):
        for j in range(REACH):
            x = inputs[first + j]
            for half in range(2):
                start = MOM_ROWS + (2 * j + half) * RHS
                ref[start : start + RHS, :] = x[:, half * 128 : (half + 1) * 128]

    @pl.when(odd == 0)
    def _():
        edge(pa_ref, SLOTS - REACH)
        edge(pb_ref, 0)

    @pl.when(odd == 1)
    def _():
        edge(pa_ref, 0)
        edge(pb_ref, SLOTS - REACH)


def up_moments(inputs, basis_ref, transfer_ref):
    moments = []
    box = jnp.zeros((RHS, RANK), F32)
    for g in range(SLOTS):
        moment = dot_nt(inputs[g], basis_ref[g]).astype(BF16)
        moments.append(moment.astype(F32))
        box = box + dot(moment, transfer_ref[g])
    return moments, box


def first_kernel(live_ref, rh_ref, basis_ref, transfer_ref, pa_ref, pb_ref, own_ref, sb_ref):
    inputs = []
    square = jnp.zeros((RHS, POINTS), F32)
    for g in range(SLOTS):
        s = rh_ref[g] * live_ref[g].astype(F32)
        square = square + s * s
        sb = s.astype(BF16)
        sb_ref[g] = sb
        inputs.append(sb)
    moments, box = up_moments(inputs, basis_ref, transfer_ref)
    pack_out(inputs, moments, box, [row_sum(square)], pa_ref, pb_ref, own_ref)


def pair_kernel(n_sums, own_ref, ra_ref, up_ref, out_ref, up_vmem, sem):
    position = lax.axis_index("leaf")
    odd = lax.rem(position, 2)
    first = pl.multiple_of((position - odd) * RANK, 2 * RANK)
    copy = pltpu.make_async_copy(up_ref.at[pl.ds(first, 2 * RANK)], up_vmem, sem)
    copy.start()
    own = own_ref[...].astype(F32)
    other = ra_ref[BOX_AT:PAIR_ROWS, :].astype(F32)
    even_side = jnp.where(odd == 0, own, other)
    odd_side = jnp.where(odd == 0, other, own)
    both = own + other
    sums = [read_sum(both, j) for j in range(n_sums)]
    joined = jnp.concatenate([even_side[:, :RANK], odd_side[:, :RANK]], axis=1).astype(BF16)
    copy.wait()
    block = message(dot(joined, up_vmem[...]).astype(BF16), sums)
    for c in range(CHIPS):
        out_ref[c] = block


def near_far_kernel(
    step_leaves,
    near_index_ref,
    far_index_ref,
    sb_ref,
    own_ref,
    ra_ref,
    rb_ref,
    tile_ref,
    couple_ref,
    near_ref,
    far_ref,
    x_ref,
    left_ref,
    right_ref,
):
    step = pl.program_id(0)
    position = lax.axis_index("leaf")
    odd = lax.rem(position, 2)

    @pl.when(step == 0)
    def _():
        at = lanes()

        def spread_moments(source, first):
            for g in range(HALF):
                both = source[g * RHS : (g + 1) * RHS, :].astype(F32)
                turned = pltpu.roll(both, RANK, 1)
                low = at < RANK
                left_ref[first + g] = jnp.where(low, both, 0.0).astype(BF16)
                right_ref[first + g] = jnp.where(low, 0.0, turned).astype(BF16)
                left_ref[first + HALF + g] = jnp.where(low, turned, 0.0).astype(BF16)
                right_ref[first + HALF + g] = jnp.where(low, 0.0, both).astype(BF16)

        def edges(source, first):
            for j in range(REACH):
                for half in range(2):
                    start = MOM_ROWS + (2 * j + half) * RHS
                    x_ref[first + j, :, half * 128 : (half + 1) * 128] = source[
                        start : start + RHS, :
                    ]

        spread_moments(own_ref, SLOTS)
        for g in range(SLOTS):
            x_ref[REACH + g] = sb_ref[g]

        @pl.when(odd == 0)
        def _():
            spread_moments(rb_ref, 0)
            spread_moments(ra_ref, 2 * SLOTS)
            edges(rb_ref, 0)
            edges(ra_ref, REACH + SLOTS)

        @pl.when(odd == 1)
        def _():
            spread_moments(ra_ref, 0)
            spread_moments(rb_ref, 2 * SLOTS)
            edges(ra_ref, 0)
            edges(rb_ref, REACH + SLOTS)

    near_base = position * SLOTS - REACH
    far_base = position * SLOTS - SLOTS
    for j in range(step_leaves):
        g = step * step_leaves + j
        columns = [x_ref[near_index_ref[g, k] - near_base] for k in range(6)]
        near_ref[j] = dot(jnp.concatenate(columns, axis=1), tile_ref[j])
        pairs = [
            left_ref[far_index_ref[g, 2 * f] - far_base]
            + right_ref[far_index_ref[g, 2 * f + 1] - far_base]
            for f in range(4)
        ]
        far_ref[j] = dot(jnp.concatenate(pairs, axis=1), couple_ref[j])


def tree_sweep(own_ref, ra_ref, gathered_ref, up_ref, couple_ref, nodes_ref, couple_vmem, sems):
    position = lax.axis_index("leaf")
    copies = []
    for level in range(LEVELS):
        node = level_start(level) + (position >> level)
        start = pl.multiple_of(node * RANK, RANK)
        copy = pltpu.make_async_copy(
            couple_ref.at[pl.ds(start, RANK)], couple_vmem.at[level], sems.at[level]
        )
        copy.start()
        copies.append(copy)
    total = gathered_ref[0].astype(F32)
    for c in range(1, CHIPS):
        total = total + gathered_ref[c].astype(F32)
    current = [gathered_ref[c][:, :RANK] for c in range(CHIPS)]
    for level in range(1, LEVELS):
        first = level_start(level) - DEVICES
        for n in range(len(current)):
            nodes_ref[first + n] = current[n]
        if level + 1 < LEVELS:
            following = []
            for m in range(len(current) // 2):
                start = (level_start(level) + 2 * m) * RANK
                joined = jnp.concatenate([current[2 * m], current[2 * m + 1]], axis=1)
                following.append(dot(joined, up_ref[start : start + 2 * RANK, :]).astype(BF16))
            current = following
    locals_list = []
    for level in range(LEVELS):
        if level == 0:
            sibling = ra_ref[BOX_AT:PAIR_ROWS, :][:, :RANK]
        else:
            sibling = nodes_ref[level_start(level) - DEVICES + ((position >> level) ^ 1)]
        copies[level].wait()
        locals_list.append(dot(sibling, couple_vmem[level]))
    downward = locals_list[LEVELS - 1].astype(BF16)
    for level in reversed(range(LEVELS - 1)):
        node = level_start(level) + (position >> level)
        up = up_ref[pl.ds(pl.multiple_of(node * RANK, RANK), RANK), :]
        downward = (locals_list[level] + dot_nt(downward, up)).astype(BF16)
    return downward, total


def image_of(g, downward, live_ref, near_ref, far_ref, basis_ref, transfer_ref):
    leaf_down = dot_nt(downward, transfer_ref[g])
    local_total = (far_ref[g] + leaf_down).astype(BF16)
    return live_ref[g].astype(F32) * (near_ref[g] + dot(local_total, basis_ref[g]))


def middle_kernel(
    live_ref,
    rh_ref,
    basis_ref,
    transfer_ref,
    own_in_ref,
    ra_ref,
    gathered_ref,
    up_ref,
    couple_ref,
    near_ref,
    far_ref,
    pa_ref,
    pb_ref,
    own_ref,
    sb_ref,
    image_ref,
    scal_ref,
    nodes_ref,
    couple_vmem,
    sems,
):
    downward, total = tree_sweep(
        own_in_ref, ra_ref, gathered_ref, up_ref, couple_ref, nodes_ref, couple_vmem, sems
    )
    square = read_sum(total, 0)
    norm = jnp.sqrt(square + EPSILON)
    scal_ref[...] = jnp.where(lanes() == 0, norm, square)
    inputs = []
    inner = jnp.zeros((RHS, POINTS), F32)
    length = jnp.zeros((RHS, POINTS), F32)
    for g in range(SLOTS):
        image = image_of(g, downward, live_ref, near_ref, far_ref, basis_ref, transfer_ref) / norm
        image_ref[g] = image
        basis_one = rh_ref[g] * live_ref[g].astype(F32) / norm
        inner = inner + basis_one * image
        length = length + image * image
        sb = image.astype(BF16)
        sb_ref[g] = sb
        inputs.append(sb)
    moments, box = up_moments(inputs, basis_ref, transfer_ref)
    pack_out(inputs, moments, box, [row_sum(inner), row_sum(length)], pa_ref, pb_ref, own_ref)


def as_row(column, shift):
    return jnp.sum(jnp.where(lanes() == rows() + shift, column, 0.0), axis=0, keepdims=True)


def as_column(row, shift):
    return row_sum(jnp.where(lanes() == rows() + shift, row, 0.0))


def last_operator_kernel(
    live_ref,
    rh_ref,
    basis_ref,
    transfer_ref,
    own_in_ref,
    ra_ref,
    gathered_ref,
    up_ref,
    couple_ref,
    near_ref,
    far_ref,
    image_ref,
    scal_in_ref,
    one_ref,
    two_ref,
    v_ref,
    send_ref,
    scal_ref,
    nodes_ref,
    couple_vmem,
    sems,
):
    downward, total = tree_sweep(
        own_in_ref, ra_ref, gathered_ref, up_ref, couple_ref, nodes_ref, couple_vmem, sems
    )
    norm = scal_in_ref[:, 0:1]
    one_one = (scal_in_ref[:, 1:2] / norm) / norm
    first_inner = read_sum(total, 0)
    image_square = read_sum(total, 1)
    residue = image_square - 2.0 * first_inner * first_inner + first_inner * first_inner * one_one
    residue = jnp.maximum(residue, 0.0)
    first_length = jnp.sqrt(residue + EPSILON)
    one_two = (first_inner - first_inner * one_one) / first_length
    two_two = (residue / first_length) / first_length
    at = lanes()
    scal = jnp.zeros((RHS, 128), F32)
    for j, column in enumerate((norm, first_inner, first_length, one_one, one_two, two_two)):
        scal = jnp.where(at == j, column, scal)
    scal_ref[...] = scal
    cross = jnp.zeros((RHS, POINTS), F32)
    own = jnp.zeros((RHS, POINTS), F32)
    square = jnp.zeros((RHS, POINTS), F32)
    for g in range(SLOTS):
        image = image_ref[g]
        y = image_of(g, downward, live_ref, near_ref, far_ref, basis_ref, transfer_ref)
        basis_one = rh_ref[g] * live_ref[g].astype(F32) / norm
        basis_two = (image - first_inner * basis_one) / first_length
        v = (y - first_inner * image) / first_length
        one_ref[g] = basis_one
        two_ref[g] = basis_two
        v_ref[g] = v
        cross = cross + basis_one * v
        own = own + basis_two * v
        square = square + v * v
    row = as_row(row_sum(cross), 0) + as_row(row_sum(own), 32) + as_row(row_sum(square), 64)
    for d in range(DEVICES):
        send_ref[d] = row


def final_kernel(one_ref, two_ref, v_ref, scal_ref, gathered_ref, next_ref, hess_ref):
    row = jnp.sum(gathered_ref[...], axis=0)
    cross, own, square = as_column(row, 0), as_column(row, 32), as_column(row, 64)
    norm, first_inner, first_length, one_one, one_two, two_two = (
        scal_ref[:, j : j + 1] for j in range(6)
    )
    residue = (
        square
        - 2.0 * cross * cross
        - 2.0 * own * own
        + cross * cross * one_one
        + own * own * two_two
        + 2.0 * cross * own * one_two
    )
    second_length = jnp.sqrt(jnp.maximum(residue, 0.0) + EPSILON)
    for j, column in enumerate((norm, first_inner, first_length, cross, own, second_length)):
        hess_ref[j : j + 1, :] = as_row(column, 0)[:, :RHS]
    for g in range(SLOTS):
        next_ref[g] = (v_ref[g] - cross * one_ref[g] - own * two_ref[g]) / second_length


def shape(dims, dtype):
    return jax.ShapeDtypeStruct(dims, dtype)


FIELD = (SLOTS, RHS, POINTS)
PACKED = [shape((PAIR_ROWS, 128), BF16), shape((BOX_AT, 128), BF16), shape((RHS, 128), BF16)]
TREE_SCRATCH = [
    pltpu.VMEM((DEVICES - 2, RHS, RANK), BF16),
    pltpu.VMEM((LEVELS, RANK, RANK), BF16),
    pltpu.SemaphoreType.DMA((LEVELS,)),
]
MIB = 1 << 20


def params(mib):
    return pltpu.CompilerParams(vmem_limit_bytes=mib * MIB)


def on_device(
    right_hand,
    leaf_live,
    near_index,
    near_tile,
    far_index,
    far_couple,
    leaf_basis,
    leaf_transfer,
    tree_up,
    tree_couple,
):
    up_rows = tree_up.reshape(-1, RANK)
    couple_rows = tree_couple.reshape(-1, RANK)
    tiles = near_tile.reshape(SLOTS, 6 * POINTS, POINTS)
    couples = far_couple.reshape(SLOTS, 8 * RANK, RANK)
    same = [(i, i ^ 1) for i in range(DEVICES)]
    across = [(i, i + 1) for i in range(1, DEVICES - 1, 2)]
    across += [(j, i) for i, j in across]
    groups = [[2 * c + core for c in range(CHIPS)] for core in range(2)]

    def exchange(pa, pb, own, n_sums):
        ra = lax.ppermute(pa, "leaf", same)
        rb = lax.ppermute(pb, "leaf", across)
        sent = pl.pallas_call(
            functools.partial(pair_kernel, n_sums),
            out_shape=shape((CHIPS, RHS, 128), BF16),
            in_specs=[VMEM, VMEM, ANY],
            out_specs=VMEM,
            scratch_shapes=[pltpu.VMEM((2 * RANK, RANK), BF16), pltpu.SemaphoreType.DMA],
            compiler_params=params(4),
            name="pair",
        )(own, ra, up_rows)
        gathered = lax.all_to_all(sent, "leaf", 0, 0, axis_index_groups=groups)
        return ra, rb, gathered

    def near_far(sb, pb, ra, rb):
        leaves = 2
        whole = lambda dims: pl.BlockSpec(dims, lambda i: (0,) * len(dims))
        part = lambda dims: pl.BlockSpec((leaves, *dims), lambda i: (i, 0, 0))
        return pl.pallas_call(
            functools.partial(near_far_kernel, leaves),
            grid=(SLOTS // leaves,),
            out_shape=[shape(FIELD, F32), shape((SLOTS, RHS, RANK), F32)],
            in_specs=[
                SMEM,
                SMEM,
                whole(FIELD),
                whole((BOX_AT, 128)),
                whole((PAIR_ROWS, 128)),
                whole((BOX_AT, 128)),
                part((6 * POINTS, POINTS)),
                part((8 * RANK, RANK)),
            ],
            out_specs=[part((RHS, POINTS)), part((RHS, RANK))],
            scratch_shapes=[
                pltpu.VMEM((SLOTS + 2 * REACH, RHS, POINTS), BF16),
                pltpu.VMEM((3 * SLOTS, RHS, 128), BF16),
                pltpu.VMEM((3 * SLOTS, RHS, 128), BF16),
            ],
            compiler_params=params(16),
            cost_estimate=pl.CostEstimate(
                flops=1_000_000_000, bytes_accessed=16_000_000, transcendentals=0
            ),
            name="near_far",
        )(near_index, far_index, sb, pb, ra, rb, tiles, couples)

    pa, pb, own, sb = pl.pallas_call(
        first_kernel,
        out_shape=[*PACKED, shape(FIELD, BF16)],
        in_specs=[SMEM, VMEM, VMEM, VMEM],
        out_specs=[VMEM] * 4,
        compiler_params=params(8),
        name="first",
    )(leaf_live, right_hand, leaf_basis, leaf_transfer)
    ra, rb, gathered = exchange(pa, pb, own, 1)
    near, far = near_far(sb, pb, ra, rb)
    pa, pb, own, sb, image, scal = pl.pallas_call(
        middle_kernel,
        out_shape=[*PACKED, shape(FIELD, BF16), shape(FIELD, F32), shape((RHS, 128), F32)],
        in_specs=[SMEM] + [VMEM] * 7 + [ANY] + [VMEM] * 2,
        out_specs=[VMEM] * 6,
        scratch_shapes=TREE_SCRATCH,
        compiler_params=params(24),
        name="middle",
    )(
        leaf_live, right_hand, leaf_basis, leaf_transfer, own, ra, gathered,
        up_rows, couple_rows, near, far,
    )
    ra, rb, gathered = exchange(pa, pb, own, 2)
    near, far = near_far(sb, pb, ra, rb)
    one, two, v, sent, scal = pl.pallas_call(
        last_operator_kernel,
        out_shape=[shape(FIELD, F32)] * 3
        + [shape((DEVICES, 1, 128), F32), shape((RHS, 128), F32)],
        in_specs=[SMEM] + [VMEM] * 7 + [ANY] + [VMEM] * 4,
        out_specs=[VMEM] * 5,
        scratch_shapes=TREE_SCRATCH,
        compiler_params=params(24),
        name="last_operator",
    )(
        leaf_live, right_hand, leaf_basis, leaf_transfer, own, ra, gathered,
        up_rows, couple_rows, near, far, image, scal,
    )
    gathered = lax.all_to_all(sent, "leaf", 0, 0)
    return pl.pallas_call(
        final_kernel,
        out_shape=[shape(FIELD, F32), shape((6, RHS), F32)],
        in_specs=[VMEM] * 5,
        out_specs=[VMEM] * 2,
        compiler_params=params(8),
        name="final",
    )(one, two, v, scal, gathered)


def solution(mesh):
    placed = (
        P("leaf", None, None),
        P("leaf"),
        P("leaf", None),
        P("leaf", None, None, None),
        P("leaf", None),
        P("leaf", None, None, None),
        P("leaf", None, None),
        P("leaf", None, None),
        P(),
        P(),
    )
    return jax.shard_map(
        on_device,
        mesh=mesh,
        in_specs=placed,
        out_specs=(P("leaf", None, None), P()),
        check_vma=False,
    )
```

time: 570 us -> 137 us (0.24)
  blocking collectives: 333 us -> 19.2 us
  matrix products: 63.4 us -> 0 us
  starting transfers between devices: 56.1 us -> 29.7 us
  Pallas kernels: 0 us -> 24.9 us
  local copies, waits for them, and re-layouts: 78.7 us -> 54.5 us
  other arithmetic: 23.2 us -> 0 us
    psum x5 -> x0, blocking collectives: 333 us -> none  [the longest x3 196 us: global_norm(): return jnp.sqrt(lax.psum(column_sums(field, field), 'leaf') + epsilon)]
    dot_general x49 -> x0, matrix products: 63.4 us -> none  [the longest x2 16.5 us: apply_operator(): jnp.einsum('inrp,inpq->irq', columns, near_tile, preferred_element_type=j...]
    ppermute x22 -> x4, starting transfers between devices: 56.1 us -> 8.15 us  [the longest x2 6.77 us: exchange(): rb = lax.ppermute(pb, 'leaf', across)]
    pallas_call x0 -> x8, Pallas kernels: none -> 24.9 us  [the longest x2 8.92 us: near_far(): pl.pallas_call(functools.partial(near_far_kernel, leaves), grid=(SLOTS //...]
    all_to_all x0 -> x2, starting transfers between devices: none -> 21.6 us  [exchange(): gathered = lax.all_to_all(sent, 'leaf', 0, 0, axis_index_groups=groups)]
    dynamic_slice x2 -> x0, local copies, waits for them, and re-layouts: 21 us -> none  [the longest x1 12 us: apply_operator(): tree_up[other_node]]
    all_to_all x0 -> x1, blocking collectives: none -> 19.2 us  [on_device(): gathered = lax.all_to_all(sent, 'leaf', 0, 0)]
    unnamed x70 -> x88, local copies, waits for them, and re-layouts: 43.1 us -> 54.5 us
  transfers between devices with their start and end apart: 22 -> 6, of which waited for: 11 -> 2; matrix products, arithmetic and copies ran while one was open for 21% -> 9% of each run, Pallas kernels for 0% -> 7%
where the time goes in v1:
time: 137 us; the launch traced here: 136 us
  local copies, waits for them, and re-layouts  54.5 us (40%)
  starting transfers between devices  29.7 us (22%)
  Pallas kernels  24.9 us (18%)
  blocking collectives  19.2 us (14%)
  waiting for transfers between devices  6.48 us (5%)
    unnamed x88, local copies, waits for them, and re-layouts  54.5 us
    all_to_all x2, starting transfers between devices, exchange(): gathered = lax.all_to_all(sent, 'leaf', 0, 0, axis_index_groups=groups)  21.6 us
    all_to_all x1, blocking collectives, on_device(): gathered = lax.all_to_all(sent, 'leaf', 0, 0)  19.2 us
    pallas_call x2, Pallas kernels, near_far(): pl.pallas_call(functools.partial(near_far_kernel, leaves), grid=(SLOTS //...  8.92 us
    ppermute x2, starting transfers between devices, exchange(): rb = lax.ppermute(pb, 'leaf', across)  6.77 us
    pallas_call x1, Pallas kernels, on_device(): pl.pallas_call(middle_kernel, out_shape=[*PACKED, shape(FIELD, BF16), sha...  6.27 us
    pallas_call x1, Pallas kernels, on_device(): pl.pallas_call(last_operator_kernel, out_shape=[shape(FIELD, F32)] * 3 +...  5.74 us
    ppermute x2, waiting for transfers between devices, exchange(): rb = lax.ppermute(pb, 'leaf', across)  5.16 us
  transfers between devices with their start and end apart: 6, of which 2 were waited for; matrix products, arithmetic and copies ran while one was open for 9% of the time, Pallas kernels for 7%

profile of v1, /device:TPU:1, one launch (start us, length us, event | category | flops | bytes accessed | tf_op | source)
XLA Modules:
  0.0 135.7 jit_solution(6506748244959214013)
XLA Ops:
  4.3 1.3 first.1
  6.4 1.4 %collective-permute-start = (bf16[416,128]{1,0:T(8,128)(2,1)S(1)}, bf16[416,128]{1,0:T(8,128)(2,1)S(1)}, u32[]{:S(2)}, u32[]{:S(2)}) collective-permute-start(bf16[416,128]{1,0:T(8,128)(2,1)S(1)} %get-tuple-element.22), channel_id=1, source_target_pairs={{0,1},{1,0},{2,3},{3,2},{4,5},{5,4},{6,7},{7,6},{8,9},{9,8},{10,11... | collective-permute-start | bytes 319496 | tf_op jit(solution)/shard_map/ppermute | solution.py:443
  7.7 6.2 %copy.12 = bf16[254,64,64]{2,1,0:T(8,128)(2,1)} copy(bf16[254,64,64]{0,2,1:T(8,128)(2,1)} %param.18) | data formatting | bytes 4161536 | tf_op args[8]
  14.0 2.2 %copy-done = bf16[254,64,64]{2,1,0:T(8,128)(2,1)S(1)} copy-done((bf16[254,64,64]{2,1,0:T(8,128)(2,1)S(1)}, bf16[254,64,64]{2,1,0:T(8,128)(2,1)}, u32[]{:S(2)}) %copy-start) | copy-done | bytes 2080792
  16.2 1.1 pair.2
  17.2 11.7 %all-to-all-start = ((bf16[64,32,128]{2,1,0:T(8,128)(2,1)}), bf16[64,32,128]{2,1,0:T(8,128)(2,1)}, u32[]{:S(2)}, u32[]{:S(2)}) async-start(bf16[64,32,128]{2,1,0:T(8,128)(2,1)} %pair.2), calls=%async_computation | async-start | bytes 1048576 | tf_op jit(solution)/shard_map/all_to_all | solution.py:454
  28.9 3.3 %collective-permute-start.1 = (bf16[384,128]{1,0:T(8,128)(2,1)S(1)}, bf16[384,128]{1,0:T(8,128)(2,1)S(1)}, u32[]{:S(2)}, u32[]{:S(2)}) collective-permute-start(bf16[384,128]{1,0:T(8,128)(2,1)S(1)} %get-tuple-element.24.own_ref), channel_id=1, source_target_pairs={{1,2},{3,4},{5,6},{7,8},{9,10},{11,12},{13,14},{15,16},{17,18},{19... | collective-permute-start | bytes 294920 | tf_op jit(solution)/shard_map/ppermute | solution.py:444
  32.4 6.3 %copy.13 = bf16[254,64,64]{2,1,0:T(8,128)(2,1)} copy(bf16[254,64,64]{0,2,1:T(8,128)(2,1)} %param.19) | data formatting | bytes 4161536 | tf_op args[9]
  39.3 4.6 %copy-done.3 = bf16[16,6,256,256]{3,2,1,0:T(8,128)(2,1)S(1)} copy-done((bf16[16,6,256,256]{3,2,1,0:T(8,128)(2,1)S(1)}, bf16[16,6,256,256]{3,2,1,0:T(8,128)(2,1)}, u32[]{:S(2)}) %copy-start.3) | copy-done | bytes 12582936
  46.7 4.5 %near_far.2 = (f32[16,32,256]{2,1,0:T(8,128)S(1)}, f32[16,32,64]{2,1,0:T(8,128)S(1)}) custom-call(s32[16,6]{1,0:T(8,128)S(1)} %copy.14.near_index_ref, s32[16,8]{1,0:T(8,128)S(1)} %copy.15.far_index_ref, bf16[16,32,256]{2,1,0:T(8,128)(2,1)S(1)} %copy-done.24, bf16[384,128]{1,0:T(8,128)(2,1)S(1)} %copy-done.32, ...), custom_call_target="tpu_custom_call" | custom-call | flops 1000000000 | bytes 16000000 | tf_op jit(solution)/shard_map/near_far/pallas_call | solution.py:461
  52.7 2.2 %copy-done.1 = bf16[254,64,64]{2,1,0:T(8,128)(2,1)S(1)} copy-done((bf16[254,64,64]{2,1,0:T(8,128)(2,1)S(1)}, bf16[254,64,64]{2,1,0:T(8,128)(2,1)}, u32[]{:S(2)}) %copy-start.1) | copy-done | bytes 2080792
  54.9 2.2 %copy-done.5 = bf16[254,64,64]{2,1,0:T(8,128)(2,1)S(1)} copy-done((bf16[254,64,64]{2,1,0:T(8,128)(2,1)S(1)}, bf16[254,64,64]{2,1,0:T(8,128)(2,1)}, u32[]{:S(2)}) %copy-start.5) | copy-done | bytes 2080792
  59.0 6.3 %middle.1 = (bf16[416,128]{1,0:T(8,128)(2,1)S(1)}, bf16[384,128]{1,0:T(8,128)(2,1)S(1)}, bf16[32,128]{1,0:T(8,128)(2,1)S(1)}, bf16[16,32,256]{2,1,0:T(8,128)(2,1...) custom-call(s32[16]{0:T(128)S(1)} %copy-done.38, f32[16,32,256]{2,1,0:T(8,128)S(1)} %copy-done.9, ...), custom_call_target="tpu_custom_call" | custom-call | tf_op jit(solution)/shard_map/middle/pallas_call | solution.py:498
  68.1 1.3 collective-permute-done.2.ra_ref
  70.5 9.9 %all-to-all-start.1 = ((bf16[64,32,128]{2,1,0:T(8,128)(2,1)}), bf16[64,32,128]{2,1,0:T(8,128)(2,1)}, u32[]{:S(2)}, u32[]{:S(2)}) async-start(bf16[64,32,128]{2,1,0:T(8,128)(2,1)} %copy-done.14), calls=%async_computation.1 | async-start | bytes 1048576 | tf_op jit(solution)/shard_map/all_to_all | solution.py:454
  80.4 3.4 %collective-permute-start.3 = (bf16[384,128]{1,0:T(8,128)(2,1)}, bf16[384,128]{1,0:T(8,128)(2,1)S(1)}, u32[]{:S(2)}, u32[]{:S(2)}) collective-permute-start(bf16[384,128]{1,0:T(8,128)(2,1)} %copy-done.29), channel_id=1, source_target_pairs={{1,2},{3,4},{5,6},{7,8},{9,10},{11,12},{13,14},{15,16},{17,18},{19... | collective-permute-start | bytes 294920 | tf_op jit(solution)/shard_map/ppermute | solution.py:444
  83.8 5.2 %collective-permute-done.3.rb_ref = bf16[384,128]{1,0:T(8,128)(2,1)S(1)} collective-permute-done((bf16[384,128]{1,0:T(8,128)(2,1)}, bf16[384,128]{1,0:T(8,128)(2,1)S(1)}, u32[]{:S(2)}, u32[]{:S(2)}) %collective-permute-start.3) | collective-permute-done | bytes 98336 | tf_op jit(solution)/shard_map/ppermute | solution.py:444
  89.0 4.6 %copy-done.4 = bf16[16,6,256,256]{3,2,1,0:T(8,128)(2,1)S(1)} copy-done((bf16[16,6,256,256]{3,2,1,0:T(8,128)(2,1)S(1)}, bf16[16,6,256,256]{3,2,1,0:T(8,128)(2,1)}, u32[]{:S(2)}) %copy-start.4) | copy-done | bytes 12582936
  95.4 4.5 %near_far.3 = (f32[16,32,256]{2,1,0:T(8,128)S(1)}, f32[16,32,64]{2,1,0:T(8,128)S(1)}) custom-call(s32[16,6]{1,0:T(8,128)S(1)} %copy.14.near_index_ref, s32[16,8]{1,0:T(8,128)S(1)} %copy.15.far_index_ref, bf16[16,32,256]{2,1,0:T(8,128)(2,1)S(1)} %copy-done.22, bf16[384,128]{1,0:T(8,128)(2,1)S(1)} %copy-done.30, ...), custom_call_target="tpu_custom_call" | custom-call | flops 1000000000 | bytes 16000000 | tf_op jit(solution)/shard_map/near_far/pallas_call | solution.py:461
  101.4 2.2 %copy-done.2 = bf16[254,64,64]{2,1,0:T(8,128)(2,1)S(1)} copy-done((bf16[254,64,64]{2,1,0:T(8,128)(2,1)S(1)}, bf16[254,64,64]{2,1,0:T(8,128)(2,1)}, u32[]{:S(2)}) %copy-start.2) | copy-done | bytes 2080792
  103.6 2.2 %copy-done.6 = bf16[254,64,64]{2,1,0:T(8,128)(2,1)S(1)} copy-done((bf16[254,64,64]{2,1,0:T(8,128)(2,1)S(1)}, bf16[254,64,64]{2,1,0:T(8,128)(2,1)}, u32[]{:S(2)}) %copy-start.6) | copy-done | bytes 2080792
  109.5 5.7 %last_operator.1 = (f32[16,32,256]{2,1,0:T(8,128)S(1)}, f32[16,32,256]{2,1,0:T(8,128)S(1)}, f32[16,32,256]{2,1,0:T(8,128)S(1)}, f32[128,1,128]{2,1,0:T(1,128)S(1)}, f32[32,128]{1,0:T(8,128)S(1)}) custom-call(s32[16]{0:T(128)S(1)} %copy-done.39, f32[16,32,256]{2,1,0:T(8,128)S(1)} %copy-done.9, bf16[16,64,256]{2,1,0:T(8,128)(2,1)S(1)} %copy-done.11, ...), custom_call_target="tpu_custom_call" | custom-call | tf_op jit(solution)/shard_map/last_operator/pallas_call | solution.py:512
  115.2 19.2 %all_to_all.15.gathered_ref = f32[128,1,128]{2,1,0:T(1,128)S(1)} all-to-all(f32[128,1,128]{2,1,0:T(1,128)S(1)} %get-tuple-element.39), channel_id=1, replica_groups=mesh['leaf'=128] {'leaf'}, dimensions={0} | all-to-all | bytes 131072 | tf_op jit(solution)/shard_map/all_to_all | solution.py:525
  134.4 1.2 final.1
  (85 shorter events, 22.3 us)
Async XLA Ops:
  0.6 1.0 copy-start.8
  1.7 1.0 copy-start.10
  6.4 22.5 %copy-start.31 = (bf16[384,128]{1,0:T(8,128)(2,1)}, bf16[384,128]{1,0:T(8,128)(2,1)S(1)}, u32[]{:S(2)}) copy-start(bf16[384,128]{1,0:T(8,128)(2,1)S(1)} %get-tuple-element.24.own_ref) | copy-start | bytes 294916
  6.4 7.6 %collective-permute-start = (bf16[416,128]{1,0:T(8,128)(2,1)S(1)}, bf16[416,128]{1,0:T(8,128)(2,1)S(1)}, u32[]{:S(2)}, u32[]{:S(2)}) collective-permute-start(bf16[416,128]{1,0:T(8,128)(2,1)S(1)} %get-tuple-element.22), channel_id=1, source_target_pairs={{0,1},{1,0},{2,3},{3,2},{4,5},{5,4},{6,7},{7,6},{8,9},{9,8},{10,11... | collective-permute-start | bytes 319496 | tf_op jit(solution)/shard_map/ppermute | solution.py:443
  7.7 24.5 %copy-start.40 = (s32[16,6]{0,1:T(8,128)S(1)}, s32[16,6]{0,1:T(8,128)}, u32[]{:S(2)}) copy-start(s32[16,6]{0,1:T(8,128)} %param.12) | copy-start | bytes 1156
  7.7 24.6 %copy-start.41 = (s32[16,8]{0,1:T(8,128)S(1)}, s32[16,8]{0,1:T(8,128)}, u32[]{:S(2)}) copy-start(s32[16,8]{0,1:T(8,128)} %param.14) | copy-start | bytes 1540
  14.0 2.2 %copy-start = (bf16[254,64,64]{2,1,0:T(8,128)(2,1)S(1)}, bf16[254,64,64]{2,1,0:T(8,128)(2,1)}, u32[]{:S(2)}) copy-start(bf16[254,64,64]{2,1,0:T(8,128)(2,1)} %copy.12) | copy-start | bytes 6242308
  17.2 22.1 %copy-start.7 = (bf16[16,8,64,64]{3,2,1,0:T(8,128)(2,1)S(1)}, bf16[16,8,64,64]{3,2,1,0:T(8,128)(2,1)}, u32[]{:S(2)}) copy-start(bf16[16,8,64,64]{3,2,1,0:T(8,128)(2,1)} %param.15) | copy-start | bytes 3145732
  17.2 35.4 %all-to-all-start = ((bf16[64,32,128]{2,1,0:T(8,128)(2,1)}), bf16[64,32,128]{2,1,0:T(8,128)(2,1)}, u32[]{:S(2)}, u32[]{:S(2)}) async-start(bf16[64,32,128]{2,1,0:T(8,128)(2,1)} %pair.2), calls=%async_computation | async-start | bytes 1048576 | tf_op jit(solution)/shard_map/all_to_all | solution.py:454
  28.9 9.8 %collective-permute-start.1 = (bf16[384,128]{1,0:T(8,128)(2,1)S(1)}, bf16[384,128]{1,0:T(8,128)(2,1)S(1)}, u32[]{:S(2)}, u32[]{:S(2)}) collective-permute-start(bf16[384,128]{1,0:T(8,128)(2,1)S(1)} %get-tuple-element.24.own_ref), channel_id=1, source_target_pairs={{1,2},{3,4},{5,6},{7,8},{9,10},{11,12},{13,14},{15,16},{17,18},{19... | collective-permute-start | bytes 294920 | tf_op jit(solution)/shard_map/ppermute | solution.py:444
  39.3 4.6 %copy-start.3 = (bf16[16,6,256,256]{3,2,1,0:T(8,128)(2,1)S(1)}, bf16[16,6,256,256]{3,2,1,0:T(8,128)(2,1)}, u32[]{:S(2)}) copy-start(bf16[16,6,256,256]{3,2,1,0:T(8,128)(2,1)} %param.13) | copy-start | bytes 37748740
  46.7 6.0 %copy-start.9 = (f32[16,32,256]{2,1,0:T(8,128)S(1)}, f32[16,32,256]{2,1,0:T(8,128)}, u32[]{:S(2)}) copy-start(f32[16,32,256]{2,1,0:T(8,128)} %rh_ref.5) | copy-start | bytes 1572868
  46.7 6.0 %copy-start.11 = (bf16[16,64,256]{2,1,0:T(8,128)(2,1)S(1)}, bf16[16,64,256]{2,1,0:T(8,128)(2,1)}, u32[]{:S(2)}) copy-start(bf16[16,64,256]{2,1,0:T(8,128)(2,1)} %basis_ref.5) | copy-start | bytes 1572868
  46.7 6.0 %copy-start.13 = (bf16[16,64,64]{2,1,0:T(8,128)(2,1)S(1)}, bf16[16,64,64]{2,1,0:T(8,128)(2,1)}, u32[]{:S(2)}) copy-start(bf16[16,64,64]{2,1,0:T(8,128)(2,1)} %transfer_ref.5) | copy-start | bytes 393220
  46.7 6.0 %copy-start.38 = (s32[16]{0:T(128)S(1)}, s32[16]{0:T(128)}, u32[]{:S(2)}) copy-start(s32[16]{0:T(128)} %live_ref.5) | copy-start | bytes 196
  52.7 2.2 %copy-start.1 = (bf16[254,64,64]{2,1,0:T(8,128)(2,1)S(1)}, bf16[254,64,64]{2,1,0:T(8,128)(2,1)}, u32[]{:S(2)}) copy-start(bf16[254,64,64]{2,1,0:T(8,128)(2,1)} %copy.12) | copy-start | bytes 6242308
  54.9 2.2 %copy-start.5 = (bf16[254,64,64]{2,1,0:T(8,128)(2,1)S(1)}, bf16[254,64,64]{2,1,0:T(8,128)(2,1)}, u32[]{:S(2)}) copy-start(bf16[254,64,64]{2,1,0:T(8,128)(2,1)} %copy.13) | copy-start | bytes 6242308
  68.1 1.3 collective-permute-start.2
  70.5 30.9 %all-to-all-start.1 = ((bf16[64,32,128]{2,1,0:T(8,128)(2,1)}), bf16[64,32,128]{2,1,0:T(8,128)(2,1)}, u32[]{:S(2)}, u32[]{:S(2)}) async-start(bf16[64,32,128]{2,1,0:T(8,128)(2,1)} %copy-done.14), calls=%async_computation.1 | async-start | bytes 1048576 | tf_op jit(solution)/shard_map/all_to_all | solution.py:454
  80.4 8.6 %collective-permute-start.3 = (bf16[384,128]{1,0:T(8,128)(2,1)}, bf16[384,128]{1,0:T(8,128)(2,1)S(1)}, u32[]{:S(2)}, u32[]{:S(2)}) collective-permute-start(bf16[384,128]{1,0:T(8,128)(2,1)} %copy-done.29), channel_id=1, source_target_pairs={{1,2},{3,4},{5,6},{7,8},{9,10},{11,12},{13,14},{15,16},{17,18},{19... | collective-permute-start | bytes 294920 | tf_op jit(solution)/shard_map/ppermute | solution.py:444
  89.0 4.6 %copy-start.4 = (bf16[16,6,256,256]{3,2,1,0:T(8,128)(2,1)S(1)}, bf16[16,6,256,256]{3,2,1,0:T(8,128)(2,1)}, u32[]{:S(2)}) copy-start(bf16[16,6,256,256]{3,2,1,0:T(8,128)(2,1)} %param.13) | copy-start | bytes 37748740
  95.4 6.0 %copy-start.36 = (f32[32,128]{1,0:T(8,128)S(1)}, f32[32,128]{1,0:T(8,128)}, u32[]{:S(2)}) copy-start(f32[32,128]{1,0:T(8,128)} %copy-done.35) | copy-start | bytes 49156
  101.4 2.2 %copy-start.2 = (bf16[254,64,64]{2,1,0:T(8,128)(2,1)S(1)}, bf16[254,64,64]{2,1,0:T(8,128)(2,1)}, u32[]{:S(2)}) copy-start(bf16[254,64,64]{2,1,0:T(8,128)(2,1)} %copy.12) | copy-start | bytes 6242308
  103.6 2.2 %copy-start.6 = (bf16[254,64,64]{2,1,0:T(8,128)(2,1)S(1)}, bf16[254,64,64]{2,1,0:T(8,128)(2,1)}, u32[]{:S(2)}) copy-start(bf16[254,64,64]{2,1,0:T(8,128)(2,1)} %copy.13) | copy-start | bytes 6242308
  (24 other events, 19.8 us)

commit v2 on v1

v2 whole, which is shorter than its diff:
```python
import functools

import jax
import jax.numpy as jnp
from jax import lax
from jax.experimental import pallas as pl
from jax.experimental.pallas import tpu as pltpu
from jax.sharding import PartitionSpec as P


EPSILON = 1e-06
F32 = jnp.float32
BF16 = jnp.bfloat16
NT = (((1,), (1,)), ((), ()))

SMEM = pl.BlockSpec(memory_space=pltpu.SMEM)
ANY = pl.BlockSpec(memory_space=pl.ANY)
VMEM = pl.BlockSpec(memory_space=pltpu.VMEM)
HBM = pl.BlockSpec(memory_space=pltpu.HBM)

SLOTS, RHS, POINTS, RANK = 16, 32, 256, 64
REACH = 2
HALF = SLOTS // 2
MOM_ROWS = HALF * RHS
NEAR_ROWS = REACH * 2 * RHS
BOX_AT = MOM_ROWS + NEAR_ROWS
PAIR_ROWS = BOX_AT + RHS
DEVICES = 128
LEVELS = 7
CHIPS = DEVICES // 2
NODES = 254
TURN = 16
DEPTH = 4
COPIES = 8
UP_NODES = 16
UP_PARTS = CHIPS // UP_NODES + 1


def dot(a, b):
    return jnp.dot(a, b, preferred_element_type=F32)


def dot_nt(a, b):
    return lax.dot_general(a, b, NT, preferred_element_type=F32)


def row_sum(x):
    return jnp.sum(x, axis=1, keepdims=True)


def lanes(shape=(RHS, 128)):
    return lax.broadcasted_iota(jnp.int32, shape, 1)


def rows(shape=(RHS, 128)):
    return lax.broadcasted_iota(jnp.int32, shape, 0)


def level_start(level):
    return 2 * DEVICES - 2 * (DEVICES >> level)


def three_parts(column):
    high = column.astype(BF16).astype(F32)
    rest = column - high
    middle = rest.astype(BF16).astype(F32)
    low = (rest - middle).astype(BF16).astype(F32)
    return high, middle, low


def message(moment, sums):
    block = jnp.concatenate([moment.astype(F32), jnp.zeros((RHS, 128 - RANK), F32)], axis=1)
    at = lanes()
    for j, column in enumerate(sums):
        for k, part in enumerate(three_parts(column)):
            block = jnp.where(at == RANK + 3 * j + k, part, block)
    return block.astype(BF16)


def read_sum(block, j):
    at = lanes()
    first = RANK + 3 * j
    return row_sum(jnp.where((at >= first) & (at < first + 3), block, 0.0))


def pack_out(inputs, moments, box, sums, pa_ref, pb_ref, own_ref):
    block = message(box.astype(BF16), sums)
    own_ref[...] = block
    pa_ref[BOX_AT:PAIR_ROWS, :] = block
    for j in range(HALF):
        both = moments[:, j * 128 : (j + 1) * 128]
        pa_ref[j * RHS : (j + 1) * RHS, :] = both
        pb_ref[j * RHS : (j + 1) * RHS, :] = both
    odd = lax.rem(lax.axis_index("leaf"), 2)

    def edge(ref, first):
        for j in range(REACH):
            x = inputs[first + j]
            for half in range(2):
                start = MOM_ROWS + (2 * j + half) * RHS
                ref[start : start + RHS, :] = x[:, half * 128 : (half + 1) * 128]

    @pl.when(odd == 0)
    def _():
        edge(pa_ref, SLOTS - REACH)
        edge(pb_ref, 0)

    @pl.when(odd == 1)
    def _():
        edge(pa_ref, 0)
        edge(pb_ref, SLOTS - REACH)


def block_of_lane():
    return lanes((RHS, 4 * RANK)) // RANK


def up_moments(inputs, basis_ref, transfer_ref):
    block = block_of_lane()
    groups = []
    for q in range(SLOTS // 4):
        four = jnp.concatenate(inputs[4 * q : 4 * q + 4], axis=0)
        crossed = dot_nt(four, basis_ref[4 * q * RANK : 4 * (q + 1) * RANK, :])
        group = crossed[0:RHS, :]
        for j in range(1, 4):
            group = jnp.where(block == j, crossed[j * RHS : (j + 1) * RHS, :], group)
        groups.append(group.astype(BF16))
    moments = jnp.concatenate(groups, axis=1)
    return moments, dot(moments, transfer_ref[...])


def start_copies(sources, targets, sems):
    copies = [
        pltpu.make_async_copy(source, target, sems.at[i])
        for i, (source, target) in enumerate(zip(sources, targets, strict=True))
    ]
    for copy in copies:
        copy.start()
    return copies


def one_hot(count, nodes):
    at, row = lanes((count, NODES)), rows((count, NODES))
    block = jnp.zeros((count, NODES), F32)
    for i, node in enumerate(nodes):
        block = jnp.where((row == i) & (at == node), 1.0, block)
    return block.astype(BF16)


def first_kernel(
    live_hbm,
    rh_hbm,
    basis_hbm,
    transfer_hbm,
    up_hbm,
    pa_ref,
    pb_ref,
    own_ref,
    sb_hbm,
    mom_hbm,
    pair_ref,
    live_ref,
    rh_ref,
    basis_ref,
    transfer_ref,
    up_ref,
    sb_ref,
    turn_ref,
    sems,
    out_sems,
):
    live_in, *copies = start_copies(
        (live_hbm, rh_hbm, basis_hbm, transfer_hbm, up_hbm),
        (live_ref, rh_ref, basis_ref, transfer_ref, up_ref),
        sems,
    )
    live_in.wait()
    copies[0].wait()
    inputs = []
    square = jnp.zeros((RHS, POINTS), F32)
    for g in range(SLOTS):
        s = rh_ref[g] * live_ref[g].astype(F32)
        square = square + s * s
        sb = s.astype(BF16)
        sb_ref[g] = sb
        inputs.append(sb)
    sb_out = pltpu.make_async_copy(sb_ref, sb_hbm, out_sems.at[0])
    sb_out.start()
    copies[1].wait()
    copies[2].wait()
    moments, box = up_moments(inputs, basis_ref, transfer_ref)
    pack_out(inputs, moments, box, [row_sum(square)], pa_ref, pb_ref, own_ref)
    mom_out = pltpu.make_async_copy(pb_ref.at[pl.ds(0, MOM_ROWS)], mom_hbm, out_sems.at[1])
    mom_out.start()
    position = lax.axis_index("leaf")
    first = position - lax.rem(position, 2)
    pick = one_hot(8, (first, first + 1))
    copies[3].wait()
    for k in range(0, RANK, 4):
        four = dot_nt(pick, up_ref[k * RANK : (k + 4) * RANK, :])
        for j in range(4):
            turn_ref[pl.ds(k + j, 8, stride=RANK), :] = four[:, j * RANK : (j + 1) * RANK]
    pair_ref[...] = turn_ref[0 : 2 * RANK, :].astype(BF16)
    for copy in (sb_out, mom_out):
        copy.wait()


def pair_kernel(n_sums, own_ref, ra_ref, up_ref, out_hbm, block_ref, out_sems):
    odd = lax.rem(lax.axis_index("leaf"), 2)
    own = own_ref[...].astype(F32)
    other = ra_ref[BOX_AT:PAIR_ROWS, :].astype(F32)
    even_side = jnp.where(odd == 0, own, other)
    odd_side = jnp.where(odd == 0, other, own)
    both = own + other
    sums = [read_sum(both, j) for j in range(n_sums)]
    joined = jnp.concatenate([even_side[:, :RANK], odd_side[:, :RANK]], axis=1).astype(BF16)
    block = message(dot(joined, up_ref[...]).astype(BF16), sums)
    for c in range(COPIES):
        block_ref[c] = block
    outs = [
        pltpu.make_async_copy(block_ref, out_hbm.at[pl.ds(c * COPIES, COPIES)], out_sems.at[c])
        for c in range(CHIPS // COPIES)
    ]
    for out in outs:
        out.start()
    for out in outs:
        out.wait()


def turn_part(t, up_ref, couple_ref, nodes_ref, own_couple_ref, nodes_turn, couple_turn):
    position = lax.axis_index("leaf")
    pick = (lanes((DEVICES, NODES)) == rows((DEVICES, NODES)) + DEVICES).astype(F32).astype(BF16)
    own = one_hot(8, [level_start(level) + (position >> level) for level in range(LEVELS)])
    for k in range(0, TURN, 4):
        start = (t * TURN + k) * RANK
        turned = dot_nt(pick, up_ref[start : start + 4 * RANK, :])
        own_turned = dot_nt(own, couple_ref[start : start + 4 * RANK, :])
        for j in range(4):
            part = slice(j * RANK, (j + 1) * RANK)
            nodes_turn[pl.ds(k + j, DEVICES, stride=TURN), :] = turned[:, part]
            couple_turn[pl.ds(k + j, 8, stride=TURN), :] = own_turned[:, part]
    to = slice(t * TURN, (t + 1) * TURN)
    for n in range(DEVICES):
        nodes_ref[n, to, :] = nodes_turn[n * TURN : (n + 1) * TURN, :].astype(BF16)
    for n in range(8):
        own_couple_ref[n, to, :] = couple_turn[n * TURN : (n + 1) * TURN, :].astype(BF16)


def near_far_kernel(turn, near_index_ref, far_index_ref, *refs):
    sb_hbm, mom_hbm, ra_any, rb_any, tile_hbm, couple_ref, *refs = refs
    if turn:
        up_hbm, couple_t_hbm, near_hbm, far_hbm, nodes_hbm, own_couple_hbm, *refs = refs
    else:
        near_hbm, far_hbm, *refs = refs
    x_ref, mom_ref, ra_ref, rb_ref, left_ref, right_ref, tile_ref, *refs = refs
    near_ref, far_ref, in_sems, tile_sems, near_sems, far_sem, *refs = refs
    small = start_copies(
        (mom_hbm, rb_any, ra_any, sb_hbm),
        (mom_ref, rb_ref, ra_ref, x_ref.at[pl.ds(REACH, SLOTS)]),
        in_sems,
    )
    tiles = [
        pltpu.make_async_copy(tile_hbm.at[g], tile_ref.at[g], tile_sems.at[g])
        for g in range(SLOTS)
    ]
    for g in range(DEPTH):
        tiles[g].start()
    parts = []
    if turn:
        up_ref, couple_t_ref, nodes_ref, own_couple_ref, nodes_turn, couple_turn, *refs = refs
        turn_sems, turn_out_sems = refs
        chunk = TURN * RANK
        for t in range(RANK // TURN):
            part = pl.ds(t * chunk, chunk)
            parts.append(
                [
                    pltpu.make_async_copy(source.at[part], to.at[part], turn_sems.at[t, i])
                    for i, (source, to) in enumerate(
                        ((up_hbm, up_ref), (couple_t_hbm, couple_t_ref))
                    )
                ]
            )
    position = lax.axis_index("leaf")
    odd = lax.rem(position, 2)
    at = lanes()

    def spread_moments(source, first):
        for j in range(HALF):
            both = source[j * RHS : (j + 1) * RHS, :].astype(F32)
            turned = pltpu.roll(both, RANK, 1)
            low = at < RANK
            left_ref[first + 2 * j] = jnp.where(low, both, 0.0).astype(BF16)
            right_ref[first + 2 * j] = jnp.where(low, 0.0, turned).astype(BF16)
            left_ref[first + 2 * j + 1] = jnp.where(low, turned, 0.0).astype(BF16)
            right_ref[first + 2 * j + 1] = jnp.where(low, 0.0, both).astype(BF16)

    def edges(source, first):
        for j in range(REACH):
            for half in range(2):
                start = MOM_ROWS + (2 * j + half) * RHS
                x_ref[first + j, :, half * 128 : (half + 1) * 128] = source[start : start + RHS, :]

    small[0].wait()
    spread_moments(mom_ref, SLOTS)
    for copy in small[1:]:
        copy.wait()
    spread_moments(rb_ref, odd * (2 * SLOTS))
    spread_moments(ra_ref, (1 - odd) * (2 * SLOTS))
    edges(rb_ref, odd * (REACH + SLOTS))
    edges(ra_ref, (1 - odd) * (REACH + SLOTS))
    near_base = position * SLOTS - REACH
    far_base = position * SLOTS - SLOTS
    outs = []
    for g in range(SLOTS):
        if g + DEPTH < SLOTS:
            tiles[g + DEPTH].start()
        if turn and g % 4 == 0:
            for copy in parts[g // 4]:
                copy.start()
        tiles[g].wait()
        columns = [x_ref[near_index_ref[k, g] - near_base] for k in range(6)]
        near_ref[g] = dot(jnp.concatenate(columns, axis=1), tile_ref[g])
        out = pltpu.make_async_copy(near_ref.at[g], near_hbm.at[g], near_sems.at[g])
        out.start()
        outs.append(out)
        pairs = [
            left_ref[far_index_ref[2 * f, g] - far_base]
            + right_ref[far_index_ref[2 * f + 1, g] - far_base]
            for f in range(4)
        ]
        far_ref[:, g * RANK : (g + 1) * RANK] = dot(jnp.concatenate(pairs, axis=1), couple_ref[g])
        if turn and g % 4 == 3:
            t = g // 4
            for copy in parts[t]:
                copy.wait()
            turn_part(
                t, up_ref, couple_t_ref, nodes_ref, own_couple_ref, nodes_turn, couple_turn
            )
            to = pl.ds(t * TURN, TURN)
            for i, (source, target) in enumerate(
                ((nodes_ref, nodes_hbm), (own_couple_ref, own_couple_hbm))
            ):
                out = pltpu.make_async_copy(
                    source.at[:, to], target.at[:, to], turn_out_sems.at[t, i]
                )
                out.start()
                outs.append(out)
    out = pltpu.make_async_copy(far_ref, far_hbm, far_sem)
    out.start()
    outs.append(out)
    for out in outs:
        out.wait()


def tree_sweep(copies, ra_ref, gathered_ref, up_ref, pair_ref, couple_ref, nodes_ref):
    position = lax.axis_index("leaf")
    total = gathered_ref[0].astype(F32)
    for c in range(1, CHIPS):
        total = total + gathered_ref[c].astype(F32)
    current = [gathered_ref[c][:, :RANK] for c in range(CHIPS)]
    for level in range(1, LEVELS):
        if level == 2:
            copies[UP_PARTS - 1].wait()
        first = level_start(level) - DEVICES
        for n in range(len(current)):
            nodes_ref[first + n] = current[n]
        if level + 1 < LEVELS:
            following = []
            for m in range(len(current) // 2):
                start = (first + 2 * m) * RANK
                if level == 1 and 2 * m % UP_NODES == 0:
                    copies[2 * m // UP_NODES].wait()
                joined = jnp.concatenate([current[2 * m], current[2 * m + 1]], axis=1)
                following.append(dot(joined, up_ref[start : start + 2 * RANK, :]).astype(BF16))
            current = following
    copies[UP_PARTS].wait()
    sibling = ra_ref[BOX_AT:PAIR_ROWS, :][:, :RANK]
    locals_list = [dot(sibling, couple_ref[0:RANK, :])]
    for level in range(1, LEVELS):
        sibling = nodes_ref[level_start(level) - DEVICES + ((position >> level) ^ 1)]
        locals_list.append(dot(sibling, couple_ref[level * RANK : (level + 1) * RANK, :]))
    downward = locals_list[LEVELS - 1].astype(BF16)
    for level in reversed(range(LEVELS - 1)):
        if level == 0:
            up = pair_ref[pl.ds(pl.multiple_of(lax.rem(position, 2) * RANK, RANK), RANK), :]
        else:
            node = level_start(level) - DEVICES + (position >> level)
            up = up_ref[pl.ds(pl.multiple_of(node * RANK, RANK), RANK), :]
        downward = (locals_list[level] + dot_nt(downward, up)).astype(BF16)
    return downward, total


def spread_of(downward, far_ref, basis_ref, transfer_ref):
    block = block_of_lane()
    local_total = far_ref[...] + dot_nt(downward, transfer_ref[...])
    spread = []
    for q in range(SLOTS // 4):
        group = local_total[:, 4 * q * RANK : 4 * (q + 1) * RANK]
        apart = jnp.concatenate(
            [jnp.where(block == j, group, 0.0).astype(BF16) for j in range(4)], axis=0
        )
        four = dot(apart, basis_ref[4 * q * RANK : 4 * (q + 1) * RANK, :])
        spread += [four[j * RHS : (j + 1) * RHS, :] for j in range(4)]
    return spread


def start_tree(hbm, local, sems):
    up_hbm, up_ref = hbm[0], local[0]
    sizes = [UP_NODES] * (UP_PARTS - 1) + [CHIPS]
    cuts = [pl.ds(sum(sizes[:i]) * RANK, size * RANK) for i, size in enumerate(sizes)]
    sources = [up_hbm.at[cut] for cut in cuts] + list(hbm[1:])
    targets = [up_ref.at[cut] for cut in cuts] + list(local[1:])
    return start_copies(sources, targets, sems)


def middle_kernel(live_ref, ra_ref, gathered_ref, pair_ref, *refs):
    hbm, refs = refs[:7], refs[7:]
    pa_ref, pb_ref, own_ref, sb_hbm, mom_hbm, image_hbm, scal_hbm, *refs = refs
    local, refs = refs[:7], refs[7:]
    sb_ref, image_ref, scal_ref, nodes_ref, sems, out_sems, image_sems = refs
    copies = start_tree(hbm, local, sems)
    up_ref, couple_ref, near_ref, far_ref, transfer_ref, basis_ref, rh_ref = local
    downward, total = tree_sweep(
        copies, ra_ref, gathered_ref, up_ref, pair_ref, couple_ref, nodes_ref
    )
    for copy in copies[UP_PARTS + 1 :]:
        copy.wait()
    spread = spread_of(downward, far_ref, basis_ref, transfer_ref)
    outs = []
    square = read_sum(total, 0)
    norm = jnp.sqrt(square + EPSILON)
    scal_ref[...] = jnp.where(lanes() == 0, norm, square)
    inputs = []
    inner = jnp.zeros((RHS, POINTS), F32)
    length = jnp.zeros((RHS, POINTS), F32)
    for g in range(SLOTS):
        image = live_ref[g].astype(F32) * (near_ref[g] + spread[g]) / norm
        image_ref[g] = image
        if g % 4 == 3:
            four = pl.ds(g - 3, 4)
            out = pltpu.make_async_copy(
                image_ref.at[four], image_hbm.at[four], image_sems.at[g // 4]
            )
            out.start()
            outs.append(out)
        basis_one = rh_ref[g] * live_ref[g].astype(F32) / norm
        inner = inner + basis_one * image
        length = length + image * image
        sb = image.astype(BF16)
        sb_ref[g] = sb
        inputs.append(sb)
    outs += start_copies((sb_ref, scal_ref), (sb_hbm, scal_hbm), out_sems)
    moments, box = up_moments(inputs, basis_ref, transfer_ref)
    pack_out(inputs, moments, box, [row_sum(inner), row_sum(length)], pa_ref, pb_ref, own_ref)
    mom_out = pltpu.make_async_copy(pb_ref.at[pl.ds(0, MOM_ROWS)], mom_hbm, out_sems.at[2])
    mom_out.start()
    for out in (*outs, mom_out):
        out.wait()


def as_row(column, shift):
    return jnp.sum(jnp.where(lanes() == rows() + shift, column, 0.0), axis=0, keepdims=True)


def as_column(row, shift):
    return row_sum(jnp.where(lanes() == rows() + shift, row, 0.0))


def last_operator_kernel(live_ref, ra_ref, gathered_ref, pair_ref, *refs):
    hbm, refs = refs[:9], refs[9:]
    one_ref, two_ref, v_ref, send_ref, scal_ref, *refs = refs
    local, (nodes_ref, sems) = refs[:9], refs[9:]
    copies = start_tree(hbm, local, sems)
    up_ref, couple_ref, near_ref, far_ref, transfer_ref, basis_ref, rh_ref = local[:7]
    image_ref, scal_in_ref = local[7:]
    downward, total = tree_sweep(
        copies, ra_ref, gathered_ref, up_ref, pair_ref, couple_ref, nodes_ref
    )
    for copy in copies[UP_PARTS + 1 :]:
        copy.wait()
    spread = spread_of(downward, far_ref, basis_ref, transfer_ref)
    norm = scal_in_ref[:, 0:1]
    one_one = (scal_in_ref[:, 1:2] / norm) / norm
    first_inner = read_sum(total, 0)
    image_square = read_sum(total, 1)
    residue = image_square - 2.0 * first_inner * first_inner + first_inner * first_inner * one_one
    residue = jnp.maximum(residue, 0.0)
    first_length = jnp.sqrt(residue + EPSILON)
    one_two = (first_inner - first_inner * one_one) / first_length
    two_two = (residue / first_length) / first_length
    at = lanes()
    scal = jnp.zeros((RHS, 128), F32)
    for j, column in enumerate((norm, first_inner, first_length, one_one, one_two, two_two)):
        scal = jnp.where(at == j, column, scal)
    scal_ref[...] = scal
    cross = jnp.zeros((RHS, POINTS), F32)
    own = jnp.zeros((RHS, POINTS), F32)
    square = jnp.zeros((RHS, POINTS), F32)
    for g in range(SLOTS):
        image = image_ref[g]
        y = live_ref[g].astype(F32) * (near_ref[g] + spread[g])
        basis_one = rh_ref[g] * live_ref[g].astype(F32) / norm
        basis_two = (image - first_inner * basis_one) / first_length
        v = (y - first_inner * image) / first_length
        one_ref[g] = basis_one
        two_ref[g] = basis_two
        v_ref[g] = v
        cross = cross + basis_one * v
        own = own + basis_two * v
        square = square + v * v
    row = as_row(row_sum(cross), 0) + as_row(row_sum(own), 32) + as_row(row_sum(square), 64)
    for d in range(DEVICES):
        send_ref[d] = row


def final_kernel(one_ref, two_ref, v_ref, scal_ref, gathered_ref, next_ref, hess_ref):
    row = jnp.sum(gathered_ref[...], axis=0)
    cross, own, square = as_column(row, 0), as_column(row, 32), as_column(row, 64)
    norm, first_inner, first_length, one_one, one_two, two_two = (
        scal_ref[:, j : j + 1] for j in range(6)
    )
    residue = (
        square
        - 2.0 * cross * cross
        - 2.0 * own * own
        + cross * cross * one_one
        + own * own * two_two
        + 2.0 * cross * own * one_two
    )
    second_length = jnp.sqrt(jnp.maximum(residue, 0.0) + EPSILON)
    for j, column in enumerate((norm, first_inner, first_length, cross, own, second_length)):
        hess_ref[j : j + 1, :] = as_row(column, 0)[:, :RHS]
    for g in range(SLOTS):
        next_ref[g] = (v_ref[g] - cross * one_ref[g] - own * two_ref[g]) / second_length


def shape(dims, dtype):
    return jax.ShapeDtypeStruct(dims, dtype)


FIELD = (SLOTS, RHS, POINTS)
FAR_FIELD = (RHS, SLOTS * RANK)
PACKED = [shape((PAIR_ROWS, 128), BF16), shape((BOX_AT, 128), BF16), shape((RHS, 128), BF16)]
NODE_ROWS = DEVICES * RANK
BASIS = (SLOTS * RANK, POINTS)
TRANSFER = (SLOTS * RANK, RANK)
TURNED = (RANK * RANK, NODES)
GATHERED = (CHIPS, RHS, 128)
TREE_BUFFERS = [
    ((NODE_ROWS, RANK), BF16),
    ((8 * RANK, RANK), BF16),
    (FIELD, F32),
    (FAR_FIELD, F32),
    (TRANSFER, BF16),
    (BASIS, BF16),
    (FIELD, F32),
]
TREE_NODES = ((DEVICES - 2, RHS, RANK), BF16)
MIB = 1 << 20


def vmem(*kinds):
    return [pltpu.VMEM(*kind) for kind in kinds]


def sems(*dims):
    return [pltpu.SemaphoreType.DMA(dim) for dim in dims]


def in_hbm(*arrays):
    return [pltpu.with_memory_space_constraint(array, pltpu.HBM) for array in arrays]


def call(kernel, outs, in_specs, out_specs, scratch, mib, **more):
    return pl.pallas_call(
        kernel,
        out_shape=outs,
        in_specs=in_specs,
        out_specs=out_specs,
        scratch_shapes=scratch,
        compiler_params=pltpu.CompilerParams(vmem_limit_bytes=mib * MIB),
        **more,
    )


def on_device(
    right_hand,
    leaf_live,
    near_index,
    near_tile,
    far_index,
    far_couple,
    leaf_basis,
    leaf_transfer,
    tree_up,
    tree_couple,
):
    up_turned = tree_up.transpose(1, 2, 0).reshape(TURNED)
    couple_turned = tree_couple.transpose(1, 2, 0).reshape(TURNED)
    tiles = near_tile.reshape(SLOTS, 6 * POINTS, POINTS)
    couples = far_couple.reshape(SLOTS, 8 * RANK, RANK)
    indices = (near_index.T, far_index.T)
    leaf_basis = leaf_basis.reshape(BASIS)
    leaf_transfer = leaf_transfer.reshape(TRANSFER)
    same = [(i, i ^ 1) for i in range(DEVICES)]
    across = [(i, i + 1) for i in range(1, DEVICES - 1, 2)]
    across += [(j, i) for i, j in across]
    groups = [[2 * c + core for c in range(CHIPS)] for core in range(2)]

    def exchange(pa, pb, own, pair_up, n_sums):
        ra = lax.ppermute(pa, "leaf", same)
        rb = lax.ppermute(pb, "leaf", across)
        sent = call(
            functools.partial(pair_kernel, n_sums),
            pltpu.HBM(GATHERED, BF16),
            [VMEM, VMEM, VMEM],
            HBM,
            [*vmem(((COPIES, RHS, 128), BF16)), *sems((CHIPS // COPIES,))],
            4,
        )(own, ra, pair_up)
        gathered = lax.all_to_all(sent, "leaf", 0, 0, axis_index_groups=groups)
        return ra, rb, gathered

    def near_far(sb, mom, ra, rb, turn):
        outs = [pltpu.HBM(FIELD, F32), pltpu.HBM(FAR_FIELD, F32)]
        scratch = [
            *vmem(
                ((SLOTS + 2 * REACH, RHS, POINTS), BF16),
                ((MOM_ROWS, 128), BF16),
                ((PAIR_ROWS, 128), BF16),
                ((BOX_AT, 128), BF16),
                ((3 * SLOTS, RHS, 128), BF16),
                ((3 * SLOTS, RHS, 128), BF16),
                ((SLOTS, 6 * POINTS, POINTS), BF16),
                (FIELD, F32),
                (FAR_FIELD, F32),
            ),
            *sems((4,), (SLOTS,), (SLOTS,)),
            pltpu.SemaphoreType.DMA,
        ]
        more = []
        if turn:
            counts = (DEVICES, 8)
            outs += [pltpu.HBM((n, RANK, RANK), BF16) for n in counts]
            scratch += vmem(
                (TURNED, BF16),
                (TURNED, BF16),
                *(((n, RANK, RANK), BF16) for n in counts),
                *(((n * TURN, RANK), F32) for n in counts),
            )
            scratch += sems((RANK // TURN, 2), (RANK // TURN, 2))
            more = in_hbm(up_turned, couple_turned)
        return call(
            functools.partial(near_far_kernel, turn),
            outs,
            [SMEM, SMEM, HBM, HBM, ANY, ANY, HBM, VMEM, *([HBM] * len(more))],
            [HBM] * len(outs),
            scratch,
            40,
            cost_estimate=pl.CostEstimate(
                flops=1_000_000_000, bytes_accessed=16_000_000, transcendentals=0
            ),
        )(*indices, *in_hbm(sb, mom), ra, rb, *in_hbm(tiles), couples, *more)

    pa, pb, own, sb, mom, pair_up = call(
        first_kernel,
        [
            *PACKED,
            pltpu.HBM(FIELD, BF16),
            pltpu.HBM((MOM_ROWS, 128), BF16),
            shape((2 * RANK, RANK), BF16),
        ],
        [HBM] * 5,
        [VMEM] * 3 + [HBM] * 2 + [VMEM],
        [
            pltpu.SMEM((SLOTS,), jnp.int32),
            *vmem(
                (FIELD, F32),
                (BASIS, BF16),
                (TRANSFER, BF16),
                (TURNED, BF16),
                (FIELD, BF16),
                ((8 * RANK, RANK), F32),
            ),
            *sems((5,), (2,)),
        ],
        12,
    )(*in_hbm(leaf_live, right_hand, leaf_basis, leaf_transfer, up_turned))
    ra, rb, gathered = exchange(pa, pb, own, pair_up, 1)
    near, far, nodes, own_couple = near_far(sb, mom, ra, rb, True)
    up_nodes = nodes.reshape(NODE_ROWS, RANK)
    own_couple = own_couple.reshape(8 * RANK, RANK)
    count = len(TREE_BUFFERS)
    pa, pb, own, sb, mom, image, scal = call(
        middle_kernel,
        [
            *PACKED,
            pltpu.HBM(FIELD, BF16),
            pltpu.HBM((MOM_ROWS, 128), BF16),
            pltpu.HBM(FIELD, F32),
            pltpu.HBM((RHS, 128), F32),
        ],
        [SMEM, VMEM, VMEM, VMEM] + [HBM] * count,
        [VMEM] * 3 + [HBM] * 4,
        [
            *vmem(*TREE_BUFFERS, (FIELD, BF16), (FIELD, F32), ((RHS, 128), F32), TREE_NODES),
            *sems((count + UP_PARTS - 1,), (3,), (4,)),
        ],
        20,
    )(
        leaf_live, ra, gathered, pair_up,
        *in_hbm(up_nodes, own_couple, near, far, leaf_transfer, leaf_basis, right_hand),
    )
    ra, rb, gathered = exchange(pa, pb, own, pair_up, 2)
    near, far = near_far(sb, mom, ra, rb, False)
    one, two, v, sent, scal = call(
        last_operator_kernel,
        [shape(FIELD, F32)] * 3 + [shape((DEVICES, 1, 128), F32), shape((RHS, 128), F32)],
        [SMEM, VMEM, VMEM, VMEM] + [HBM] * (count + 2),
        [VMEM] * 5,
        [
            *vmem(*TREE_BUFFERS, (FIELD, F32), ((RHS, 128), F32), TREE_NODES),
            *sems((count + UP_PARTS + 1,)),
        ],
        20,
    )(
        leaf_live, ra, gathered, pair_up,
        *in_hbm(up_nodes, own_couple, near, far, leaf_transfer, leaf_basis, right_hand),
        *in_hbm(image, scal),
    )
    gathered = lax.all_to_all(sent, "leaf", 0, 0)
    return call(
        final_kernel, [shape(FIELD, F32), shape((6, RHS), F32)], [VMEM] * 5, [VMEM] * 2, [], 8
    )(one, two, v, scal, gathered)


def solution(mesh):
    placed = (
        P("leaf", None, None),
        P("leaf"),
        P("leaf", None),
        P("leaf", None, None, None),
        P("leaf", None),
        P("leaf", None, None, None),
        P("leaf", None, None),
        P("leaf", None, None),
        P(),
        P(),
    )
    return jax.shard_map(
        on_device,
        mesh=mesh,
        in_specs=placed,
        out_specs=(P("leaf", None, None), P()),
        check_vma=False,
    )
```

time: 137 us -> 102 us (0.74)
  local copies, waits for them, and re-layouts: 54.5 us -> 0.02 us
  Pallas kernels: 24.9 us -> 38.2 us
  waiting for transfers between devices: 6.48 us -> 12.4 us
    unnamed x88 -> x8, local copies, waits for them, and re-layouts: 54.5 us -> 0.02 us
    pallas_call x8, Pallas kernels: 24.9 us -> 38.2 us  [the longest x2 21.2 us: near_far(): call(functools.partial(near_far_kernel, turn), outs, [SMEM, SMEM, HBM, HB...]
    ppermute x2, waiting for transfers between devices: 5.16 us -> 10.1 us  [exchange(): rb = lax.ppermute(pb, 'leaf', across)]
  transfers between devices with their start and end apart: 6 -> 6, of which waited for: 2 -> 4; matrix products, arithmetic and copies ran while one was open for 9% -> 0% of each run, Pallas kernels for 7% -> 21%
where the time goes in v2:
time: 102 us; the launch traced here: 101 us
  Pallas kernels  38.2 us (37%)
  starting transfers between devices  30.9 us (30%)
  blocking collectives  19 us (19%)
  waiting for transfers between devices  12.4 us (12%)
    all_to_all x2, starting transfers between devices, exchange(): gathered = lax.all_to_all(sent, 'leaf', 0, 0, axis_index_groups=groups)  22 us
    pallas_call x2, Pallas kernels, near_far(): call(functools.partial(near_far_kernel, turn), outs, [SMEM, SMEM, HBM, HB...  21.2 us
    all_to_all x1, blocking collectives, on_device(): gathered = lax.all_to_all(sent, 'leaf', 0, 0)  19 us
    ppermute x2, waiting for transfers between devices, exchange(): rb = lax.ppermute(pb, 'leaf', across)  10.1 us
    ppermute x2, starting transfers between devices, exchange(): rb = lax.ppermute(pb, 'leaf', across)  7.42 us
    pallas_call x1, Pallas kernels, on_device(): call(middle_kernel, [*PACKED, pltpu.HBM(FIELD, BF16), pltpu.HBM((MOM_ROWS...  5.72 us
    pallas_call x1, Pallas kernels, on_device(): call(last_operator_kernel, [shape(FIELD, F32)] * 3 + [shape((DEVICES, 1,...  4.97 us
    pallas_call x1, Pallas kernels, on_device(): call(first_kernel, [*PACKED, pltpu.HBM(FIELD, BF16), pltpu.HBM((MOM_ROWS,...  2.94 us
  transfers between devices with their start and end apart: 6, of which 4 were waited for; matrix products, arithmetic and copies ran while one was open for 0% of the time, Pallas kernels for 21%

profile of v2, /device:TPU:1, one launch (start us, length us, event | category | flops | bytes accessed | tf_op | source)
XLA Modules:
  0.0 101.3 jit_solution(3522725710395138256)
XLA Ops:
  0.6 0.0 copy-start
  0.7 2.9 %shard_map.113 = (bf16[416,128]{1,0:T(8,128)(2,1)S(1)}, bf16[384,128]{1,0:T(8,128)(2,1)S(1)}, bf16[32,128]{1,0:T(8,128)(2,1)S(1)}, bf16[16,32,256]{2,1,0:T(8,128...) custom-call(s32[16]{0:T(128)} %live_ref.3, f32[16,32,256]{2,1,0:T(8,128)} %refs_6_.3, ...), custom_call_target="tpu_custom_call" | custom-call | tf_op jit(solution)/shard_map/pallas_call | solution.py:665
  3.6 1.5 %collective-permute-start = (bf16[416,128]{1,0:T(8,128)(2,1)S(1)}, bf16[416,128]{1,0:T(8,128)(2,1)S(1)}, u32[]{:S(2)}, u32[]{:S(2)}) collective-permute-start(bf16[416,128]{1,0:T(8,128)(2,1)S(1)} %get-tuple-element.26), channel_id=1, source_target_pairs={{0,1},{1,0},{2,3},{3,2},{4,5},{5,4},{6,7},{7,6},{8,9},{9,8},{10,11... | collective-permute-start | bytes 319496 | tf_op jit(solution)/shard_map/ppermute | solution.py:611
  5.1 1.0 collective-permute-done.ra_ref.refs_2_
  6.0 1.1 %shard_map.114 = bf16[64,32,128]{2,1,0:T(8,128)(2,1)} custom-call(bf16[32,128]{1,0:T(8,128)(2,1)S(1)} %get-tuple-element.27.own_ref, bf16[416,128]{1,0:T(8,128)(2,1)S(1)} %collective-permute-done.ra_ref.refs_2_, bf16[128,64]{1,0:T(8,128)(2,1)S(1)} %get-tuple-element.28.up_ref.pair_ref), custom_call_target="tpu_custom_call" | custom-call | tf_op jit(solution)/shard_map/pallas_call | solution.py:613
  7.1 11.3 %all-to-all-start = ((bf16[64,32,128]{2,1,0:T(8,128)(2,1)}), bf16[64,32,128]{2,1,0:T(8,128)(2,1)S(1)}, u32[]{:S(2)}, u32[]{:S(2)}) async-start(bf16[64,32,128]{2,1,0:T(8,128)(2,1)} %shard_map.114), calls=%async_computation | async-start | bytes 1048576 | tf_op jit(solution)/shard_map/all_to_all | solution.py:621
  18.4 3.7 %collective-permute-start.1 = (bf16[384,128]{1,0:T(8,128)(2,1)S(1)}, bf16[384,128]{1,0:T(8,128)(2,1)S(1)}, u32[]{:S(2)}, u32[]{:S(2)}) collective-permute-start(bf16[384,128]{1,0:T(8,128)(2,1)S(1)} %get-tuple-element.31), channel_id=1, source_target_pairs={{1,2},{3,4},{5,6},{7,8},{9,10},{11,12},{13,14},{15,16},{17,18},{19... | collective-permute-start | bytes 294920 | tf_op jit(solution)/shard_map/ppermute | solution.py:612
  22.1 5.0 %collective-permute-done.1.refs_3_ = bf16[384,128]{1,0:T(8,128)(2,1)S(1)} collective-permute-done((bf16[384,128]{1,0:T(8,128)(2,1)S(1)}, bf16[384,128]{1,0:T(8,128)(2,1)S(1)}, u32[]{:S(2)}, u32[]{:S(2)}) %collective-permute-start.1) | collective-permute-done | bytes 98336 | tf_op jit(solution)/shard_map/ppermute | solution.py:612
  27.1 0.0 copy-start.3
  27.1 12.2 %shard_map.115 = (f32[16,32,256]{2,1,0:T(8,128)}, f32[32,1024]{1,0:T(8,128)}, bf16[128,64,64]{2,1,0:T(8,128)(2,1)}, bf16[8,64,64]{2,1,0:T(8,128)(2,1)}) custom-call(s32[6,16]{1,0:T(8,128)S(1)} %bitcast.16, s32[8,16]{1,0:T(8,128)S(1)} %bitcast.18, bf16[16,32,256]{2,1,0:T(8,128)(2,1)} %get-tuple-element.29.refs_0_, ...), custom_call_target="tpu_custom_call" | custom-call | flops 1000000000 | bytes 16000000 | tf_op jit(solution)/shard_map/pallas_call | solution.py:653
  39.4 0.0 all-to-all-done.gathered_ref
  39.4 0.0 copy-done.3
  39.4 5.7 %shard_map.116 = (bf16[416,128]{1,0:T(8,128)(2,1)S(1)}, bf16[384,128]{1,0:T(8,128)(2,1)S(1)}, bf16[32,128]{1,0:T(8,128)(2,1)S(1)}, bf16[16,32,256]{2,1,0:T(8,128...) custom-call(s32[16]{0:T(128)S(1)} %copy-done.3, ...), custom_call_target="tpu_custom_call" | custom-call | tf_op jit(solution)/shard_map/pallas_call | solution.py:694
  45.1 0.1 collective-permute-start.2
  45.2 1.3 %collective-permute-done.2.ra_ref.refs_2_ = bf16[416,128]{1,0:T(8,128)(2,1)S(1)} collective-permute-done((bf16[416,128]{1,0:T(8,128)(2,1)S(1)}, bf16[416,128]{1,0:T(8,128)(2,1)S(1)}, u32[]{:S(2)}, u32[]{:S(2)}) %collective-permute-start.2) | collective-permute-done | bytes 106528 | tf_op jit(solution)/shard_map/ppermute | solution.py:611
  46.5 1.1 %shard_map.117 = bf16[64,32,128]{2,1,0:T(8,128)(2,1)} custom-call(bf16[32,128]{1,0:T(8,128)(2,1)S(1)} %get-tuple-element.37.own_ref, bf16[416,128]{1,0:T(8,128)(2,1)S(1)} %collective-permute-done.2.ra_ref.refs_2_, bf16[128,64]{1,0:T(8,128)(2,1)S(1)} %get-tuple-element.28.up_ref.pair_ref), custom_call_target="tpu_custom_call" | custom-call | tf_op jit(solution)/shard_map/pallas_call | solution.py:613
  47.6 10.7 %all-to-all-start.1 = ((bf16[64,32,128]{2,1,0:T(8,128)(2,1)}), bf16[64,32,128]{2,1,0:T(8,128)(2,1)S(1)}, u32[]{:S(2)}, u32[]{:S(2)}) async-start(bf16[64,32,128]{2,1,0:T(8,128)(2,1)} %shard_map.117), calls=%async_computation.1 | async-start | bytes 1048576 | tf_op jit(solution)/shard_map/all_to_all | solution.py:621
  58.3 3.7 %collective-permute-start.3 = (bf16[384,128]{1,0:T(8,128)(2,1)S(1)}, bf16[384,128]{1,0:T(8,128)(2,1)S(1)}, u32[]{:S(2)}, u32[]{:S(2)}) collective-permute-start(bf16[384,128]{1,0:T(8,128)(2,1)S(1)} %get-tuple-element.40), channel_id=1, source_target_pairs={{1,2},{3,4},{5,6},{7,8},{9,10},{11,12},{13,14},{15,16},{17,18},{19... | collective-permute-start | bytes 294920 | tf_op jit(solution)/shard_map/ppermute | solution.py:612
  62.0 5.1 %collective-permute-done.3.refs_3_ = bf16[384,128]{1,0:T(8,128)(2,1)S(1)} collective-permute-done((bf16[384,128]{1,0:T(8,128)(2,1)S(1)}, bf16[384,128]{1,0:T(8,128)(2,1)S(1)}, u32[]{:S(2)}, u32[]{:S(2)}) %collective-permute-start.3) | collective-permute-done | bytes 98336 | tf_op jit(solution)/shard_map/ppermute | solution.py:612
  67.1 9.0 %shard_map.118 = (f32[16,32,256]{2,1,0:T(8,128)}, f32[32,1024]{1,0:T(8,128)}) custom-call(s32[6,16]{1,0:T(8,128)S(1)} %bitcast.17, s32[8,16]{1,0:T(8,128)S(1)} %bitcast.19, bf16[16,32,256]{2,1,0:T(8,128)(2,1)} %get-tuple-element.38.refs_0_, bf16[256,128]{1,0:T(8,128)(2,1)} %get-tuple-element.39.refs_1_, ...), custom_call_target="tpu_custom_call" | custom-call | flops 1000000000 | bytes 16000000 | tf_op jit(solution)/shard_map/pallas_call | solution.py:653
  76.1 0.0 all-to-all-done.1.gathered_ref
  76.1 5.0 %shard_map.119 = (f32[16,32,256]{2,1,0:T(8,128)S(1)}, f32[16,32,256]{2,1,0:T(8,128)S(1)}, f32[16,32,256]{2,1,0:T(8,128)S(1)}, f32[128,1,128]{2,1,0:T(1,128)S(1)}, f32[32,128]{1,0:T(8,128)S(1)}) custom-call(s32[16]{0:T(128)S(1)} %copy-done.3, bf16[416,128]{1,0:T(8,128)(2,1)S(1)} %collective-permute-done.2.ra_ref.refs_2_, ...), custom_call_target="tpu_custom_call" | custom-call | tf_op jit(solution)/shard_map/pallas_call | solution.py:716
  81.1 19.0 %all_to_all.15.gathered_ref = f32[128,1,128]{2,1,0:T(1,128)S(1)} all-to-all(f32[128,1,128]{2,1,0:T(1,128)S(1)} %get-tuple-element.49), channel_id=1, replica_groups=mesh['leaf'=128] {'leaf'}, dimensions={0} | all-to-all | bytes 131072 | tf_op jit(solution)/shard_map/all_to_all | solution.py:731
  100.0 1.2 %shard_map.120 = (f32[16,32,256]{2,1,0:T(8,128)}, f32[6,32]{1,0:T(8,128)}) custom-call(f32[16,32,256]{2,1,0:T(8,128)S(1)} %get-tuple-element.45.one_ref, f32[16,32,256]{2,1,0:T(8,128)S(1)} %get-tuple-element.46.two_ref, f32[16,32,256]{2,1,0:T(8,128)S(1)} %get-tuple-element.47.v_ref, f32[32,128]{1,0:T(8,128)S(1)} %get-tuple-element.48.scal_ref, ...), custom_call_target="tpu_custom_call" | custom-call | tf_op jit(solution)/shard_map/pallas_call | solution.py:732
  (5 shorter events, 0.0 us)
Async XLA Ops:
  0.6 26.5 %copy-start = (bf16[16,8,64,64]{3,2,1,0:T(8,128)(2,1)S(1)}, bf16[16,8,64,64]{3,2,1,0:T(8,128)(2,1)}, u32[]{:S(2)}) copy-start(bf16[16,8,64,64]{3,2,1,0:T(8,128)(2,1)} %param.15) | copy-start | bytes 3145732
  0.6 26.5 %copy-start.1 = (s32[16,6]{0,1:T(8,128)S(1)}, s32[16,6]{0,1:T(8,128)}, u32[]{:S(2)}) copy-start(s32[16,6]{0,1:T(8,128)} %param.12) | copy-start | bytes 1156
  0.7 26.5 %copy-start.2 = (s32[16,8]{0,1:T(8,128)S(1)}, s32[16,8]{0,1:T(8,128)}, u32[]{:S(2)}) copy-start(s32[16,8]{0,1:T(8,128)} %param.14) | copy-start | bytes 1540
  3.6 2.4 %collective-permute-start = (bf16[416,128]{1,0:T(8,128)(2,1)S(1)}, bf16[416,128]{1,0:T(8,128)(2,1)S(1)}, u32[]{:S(2)}, u32[]{:S(2)}) collective-permute-start(bf16[416,128]{1,0:T(8,128)(2,1)S(1)} %get-tuple-element.26), channel_id=1, source_target_pairs={{0,1},{1,0},{2,3},{3,2},{4,5},{5,4},{6,7},{7,6},{8,9},{9,8},{10,11... | collective-permute-start | bytes 319496 | tf_op jit(solution)/shard_map/ppermute | solution.py:611
  7.1 32.3 %all-to-all-start = ((bf16[64,32,128]{2,1,0:T(8,128)(2,1)}), bf16[64,32,128]{2,1,0:T(8,128)(2,1)S(1)}, u32[]{:S(2)}, u32[]{:S(2)}) async-start(bf16[64,32,128]{2,1,0:T(8,128)(2,1)} %shard_map.114), calls=%async_computation | async-start | bytes 1048576 | tf_op jit(solution)/shard_map/all_to_all | solution.py:621
  18.4 8.8 %collective-permute-start.1 = (bf16[384,128]{1,0:T(8,128)(2,1)S(1)}, bf16[384,128]{1,0:T(8,128)(2,1)S(1)}, u32[]{:S(2)}, u32[]{:S(2)}) collective-permute-start(bf16[384,128]{1,0:T(8,128)(2,1)S(1)} %get-tuple-element.31), channel_id=1, source_target_pairs={{1,2},{3,4},{5,6},{7,8},{9,10},{11,12},{13,14},{15,16},{17,18},{19... | collective-permute-start | bytes 294920 | tf_op jit(solution)/shard_map/ppermute | solution.py:612
  27.1 12.3 %copy-start.3 = (s32[16]{0:T(128)S(1)}, s32[16]{0:T(128)}, u32[]{:S(2)}) copy-start(s32[16]{0:T(128)} %live_ref.3) | copy-start | bytes 196
  45.1 1.4 %collective-permute-start.2 = (bf16[416,128]{1,0:T(8,128)(2,1)S(1)}, bf16[416,128]{1,0:T(8,128)(2,1)S(1)}, u32[]{:S(2)}, u32[]{:S(2)}) collective-permute-start(bf16[416,128]{1,0:T(8,128)(2,1)S(1)} %get-tuple-element.36), channel_id=1, source_target_pairs={{0,1},{1,0},{2,3},{3,2},{4,5},{5,4},{6,7},{7,6},{8,9},{9,8},{10,11... | collective-permute-start | bytes 319496 | tf_op jit(solution)/shard_map/ppermute | solution.py:611
  47.6 28.5 %all-to-all-start.1 = ((bf16[64,32,128]{2,1,0:T(8,128)(2,1)}), bf16[64,32,128]{2,1,0:T(8,128)(2,1)S(1)}, u32[]{:S(2)}, u32[]{:S(2)}) async-start(bf16[64,32,128]{2,1,0:T(8,128)(2,1)} %shard_map.117), calls=%async_computation.1 | async-start | bytes 1048576 | tf_op jit(solution)/shard_map/all_to_all | solution.py:621
  58.3 8.8 %collective-permute-start.3 = (bf16[384,128]{1,0:T(8,128)(2,1)S(1)}, bf16[384,128]{1,0:T(8,128)(2,1)S(1)}, u32[]{:S(2)}, u32[]{:S(2)}) collective-permute-start(bf16[384,128]{1,0:T(8,128)(2,1)S(1)} %get-tuple-element.40), channel_id=1, source_target_pairs={{1,2},{3,4},{5,6},{7,8},{9,10},{11,12},{13,14},{15,16},{17,18},{19... | collective-permute-start | bytes 294920 | tf_op jit(solution)/shard_map/ppermute | solution.py:612

commit v3 on v2

v3 whole, which is shorter than its diff:
```python
import functools

import jax
import jax.numpy as jnp
from jax import lax
from jax.experimental import pallas as pl
from jax.experimental.pallas import tpu as pltpu
from jax.sharding import PartitionSpec as P


EPSILON = 1e-06
F32 = jnp.float32
BF16 = jnp.bfloat16
NT = (((1,), (1,)), ((), ()))

ANY = pl.BlockSpec(memory_space=pl.ANY)
VMEM = pl.BlockSpec(memory_space=pltpu.VMEM)
HBM = pl.BlockSpec(memory_space=pltpu.HBM)

SLOTS, RHS, POINTS, RANK = 16, 32, 256, 64
REACH = 2
HALF = SLOTS // 2
MOM_ROWS = HALF * RHS
NEAR_ROWS = REACH * 2 * RHS
BOX_AT = MOM_ROWS + NEAR_ROWS
PAIR_ROWS = BOX_AT + RHS
DEVICES = 128
LEVELS = 7
CHIPS = DEVICES // 2
NODES = 254
GROUPS = (4, 4, 4, 2, 2)
COPIES = 8


def dot(a, b):
    return jnp.dot(a, b, preferred_element_type=F32)


def dot_nt(a, b):
    return lax.dot_general(a, b, NT, preferred_element_type=F32)


def row_sum(x):
    return jnp.sum(x, axis=1, keepdims=True)


def lanes(shape=(RHS, 128)):
    return lax.broadcasted_iota(jnp.int32, shape, 1)


def rows(shape=(RHS, 128)):
    return lax.broadcasted_iota(jnp.int32, shape, 0)


def level_start(level):
    return 2 * DEVICES - 2 * (DEVICES >> level)


def three_parts(column):
    high = column.astype(BF16).astype(F32)
    rest = column - high
    middle = rest.astype(BF16).astype(F32)
    low = (rest - middle).astype(BF16).astype(F32)
    return high, middle, low


def sums_block(sums):
    at = lanes()
    block = jnp.zeros((RHS, 128), F32)
    for j, column in enumerate(sums):
        for k, part in enumerate(three_parts(column)):
            block = jnp.where(at == RANK + 3 * j + k, part, block)
    return block


def message(moment, sums):
    wide = jnp.concatenate([moment, jnp.zeros((RHS, 128 - RANK), F32)], axis=1)
    return jnp.where(lanes() < RANK, wide, sums_block(sums)).astype(BF16)


def read_sum(block, j):
    at = lanes()
    first = RANK + 3 * j
    return row_sum(jnp.where((at >= first) & (at < first + 3), block, 0.0))


def pack_out(inputs, moments, box, sums, pa_ref, pb_ref, own_ref):
    block = message(box, sums)
    own_ref[...] = block
    pa_ref[BOX_AT:PAIR_ROWS, :] = block
    for j in range(HALF):
        both = moments[:, j * 128 : (j + 1) * 128]
        pa_ref[j * RHS : (j + 1) * RHS, :] = both
        pb_ref[j * RHS : (j + 1) * RHS, :] = both
    odd = lax.rem(lax.axis_index("leaf"), 2)

    def edge(ref, first):
        for j in range(REACH):
            x = inputs[first + j]
            for half in range(2):
                start = MOM_ROWS + (2 * j + half) * RHS
                ref[start : start + RHS, :] = x[:, half * 128 : (half + 1) * 128]

    @pl.when(odd == 0)
    def _():
        edge(pa_ref, SLOTS - REACH)
        edge(pb_ref, 0)

    @pl.when(odd == 1)
    def _():
        edge(pa_ref, 0)
        edge(pb_ref, SLOTS - REACH)


def block_of_lane():
    return lanes((RHS, 4 * RANK)) // RANK


def up_moments(inputs, basis_ref, transfer_ref):
    block = block_of_lane()
    groups = []
    for q in range(SLOTS // 4):
        four = jnp.concatenate(inputs[4 * q : 4 * q + 4], axis=0)
        crossed = dot_nt(four, basis_ref[4 * q * RANK : 4 * (q + 1) * RANK, :])
        group = crossed[0:RHS, :]
        for j in range(1, 4):
            group = jnp.where(block == j, crossed[j * RHS : (j + 1) * RHS, :], group)
        groups.append(group.astype(BF16))
    moments = jnp.concatenate(groups, axis=1)
    return moments, dot(moments, transfer_ref[...])


def start_copies(sources, targets, sems):
    copies = [
        pltpu.make_async_copy(source, target, sems.at[i])
        for i, (source, target) in enumerate(zip(sources, targets, strict=True))
    ]
    for copy in copies:
        copy.start()
    return copies


def one_hot(count, nodes):
    at, row = lanes((count, NODES)), rows((count, NODES))
    block = jnp.zeros((count, NODES), F32)
    for i, node in enumerate(nodes):
        block = jnp.where((row == i) & (at == node), 1.0, block)
    return block.astype(BF16)


def pick_nodes(nodes, turned_ref, out_ref, rows_ref):
    pick = one_hot(8, nodes)
    for k in range(0, RANK, 4):
        four = dot_nt(pick, turned_ref[k * RANK : (k + 4) * RANK, :])
        for j in range(4):
            rows_ref[pl.ds(k + j, 8, stride=RANK), :] = four[:, j * RANK : (j + 1) * RANK]
    out_ref[...] = rows_ref[...].astype(BF16)


def first_kernel(
    live_hbm,
    rh_hbm,
    basis_hbm,
    transfer_hbm,
    up_hbm,
    couple_hbm,
    pa_ref,
    pb_ref,
    own_ref,
    sb_hbm,
    mom_hbm,
    pair_ref,
    couple_zero_ref,
    out_path_ref,
    down_path_ref,
    live_ref,
    rh_ref,
    basis_ref,
    transfer_ref,
    up_ref,
    couple_ref,
    sb_ref,
    up_nodes_ref,
    couple_nodes_ref,
    up_rows_ref,
    couple_rows_ref,
    sems,
    out_sems,
):
    up_in, couple_in, *copies = start_copies(
        (up_hbm, couple_hbm, live_hbm, rh_hbm, basis_hbm, transfer_hbm),
        (up_ref, couple_ref, live_ref, rh_ref, basis_ref, transfer_ref),
        sems,
    )
    position = lax.axis_index("leaf")
    odd = lax.rem(position, 2)
    path = [level_start(level) + (position >> level) for level in range(1, LEVELS - 1)]
    beside = [level_start(level) + ((position >> level) ^ 1) for level in range(1, LEVELS)]
    up_in.wait()
    pick_nodes((position - odd, position - odd + 1, *path), up_ref, up_nodes_ref, up_rows_ref)
    couple_in.wait()
    pick_nodes((position, *beside), couple_ref, couple_nodes_ref, couple_rows_ref)
    for copy in copies:
        copy.wait()
    inputs = []
    square = jnp.zeros((RHS, POINTS), F32)
    for g in range(SLOTS):
        s = rh_ref[g] * live_ref[g].astype(F32)
        square = square + s * s
        sb = s.astype(BF16)
        sb_ref[g] = sb
        inputs.append(sb)
    sb_out = pltpu.make_async_copy(sb_ref, sb_hbm, out_sems.at[0])
    sb_out.start()
    moments, box = up_moments(inputs, basis_ref, transfer_ref)
    pack_out(inputs, moments, box, [row_sum(square)], pa_ref, pb_ref, own_ref)
    mom_out = pltpu.make_async_copy(pb_ref.at[pl.ds(0, MOM_ROWS)], mom_hbm, out_sems.at[1])
    mom_out.start()
    pair_ref[...] = up_nodes_ref[0 : 2 * RANK, :]
    couple_zero_ref[...] = couple_nodes_ref[0:RANK, :]

    def node(ref, i):
        return ref[i * RANK : (i + 1) * RANK, :]

    up_zero = up_nodes_ref[pl.ds(pl.multiple_of(odd * RANK, RANK), RANK), :]
    chain = None
    outward = []
    for level in range(1, LEVELS):
        to = slice((level - 1) * RANK, level * RANK)
        if chain is None:
            outward.append(node(couple_nodes_ref, level).astype(F32))
            down_path_ref[to, :] = up_zero
            chain = node(up_nodes_ref, 2)
        else:
            outward.append(dot(chain, node(couple_nodes_ref, level)))
            down_path_ref[to, :] = dot(up_zero, chain).astype(BF16)
            if level + 1 < LEVELS:
                chain = dot(chain, node(up_nodes_ref, level + 1)).astype(BF16)
    out_path_ref[...] = jnp.concatenate(outward, axis=1).astype(BF16)
    for copy in (sb_out, mom_out):
        copy.wait()


def pair_kernel(n_sums, own_ref, ra_ref, up_ref, path_ref, out_hbm, block_ref, out_sems):
    position = lax.axis_index("leaf")
    odd = lax.rem(position, 2)
    chip = position >> 1
    own = own_ref[...].astype(F32)
    other = ra_ref[BOX_AT:PAIR_ROWS, :].astype(F32)
    even_side = jnp.where(odd == 0, own, other)
    odd_side = jnp.where(odd == 0, other, own)
    both = own + other
    joined = jnp.concatenate([even_side[:, :RANK], odd_side[:, :RANK]], axis=1).astype(BF16)
    moment = dot(joined, up_ref[...]).astype(BF16)
    levels = dot(moment, path_ref[...])
    sums = sums_block([read_sum(both, j) for j in range(n_sums)])
    low = lanes() < RANK
    outs = []
    at = 0
    for level in range(LEVELS):
        count = 1 if level == 0 else 1 << (level - 1)
        if level == 0:
            block, first = sums, chip
        else:
            group = levels[:, (level - 1) // 2 * 128 : (level + 1) // 2 * 128]
            if level % 2 == 0:
                group = pltpu.roll(group, RANK, 1)
            block = jnp.where(low, group, sums)
            first = ((chip >> (level - 1)) ^ 1) << (level - 1)
        block = block.astype(BF16)
        copies = min(count, COPIES)
        for c in range(copies):
            block_ref[at + c] = block
        for i in range(count // copies):
            out = pltpu.make_async_copy(
                block_ref.at[pl.ds(at, copies)],
                out_hbm.at[pl.ds(first + i * copies, copies)],
                out_sems.at[len(outs)],
            )
            out.start()
            outs.append(out)
        at += copies
    for out in outs:
        out.wait()


def near_far_kernel(
    near_index_hbm,
    far_index_hbm,
    sb_hbm,
    mom_hbm,
    ra_any,
    rb_any,
    tile_hbm,
    couple_ref,
    near_hbm,
    far_ref,
    near_index_ref,
    far_index_ref,
    near_ref,
    x_ref,
    mom_ref,
    ra_ref,
    rb_ref,
    left_ref,
    right_ref,
    tile_ref,
    in_sems,
    tile_sems,
    near_sems,
):
    small = start_copies(
        (mom_hbm, rb_any, ra_any, sb_hbm, near_index_hbm, far_index_hbm),
        (
            mom_ref,
            rb_ref,
            ra_ref,
            x_ref.at[pl.ds(REACH, SLOTS)],
            near_index_ref,
            far_index_ref,
        ),
        in_sems,
    )
    parts = [pl.ds(sum(GROUPS[:i]), size) for i, size in enumerate(GROUPS)]
    tiles = start_copies(
        [tile_hbm.at[part] for part in parts], [tile_ref.at[part] for part in parts], tile_sems
    )
    position = lax.axis_index("leaf")
    odd = lax.rem(position, 2)
    low = lanes() < RANK

    def spread_moments(source, first):
        for j in range(HALF):
            both = source[j * RHS : (j + 1) * RHS, :].astype(F32)
            turned = pltpu.roll(both, RANK, 1)
            left_ref[first + 2 * j] = jnp.where(low, both, 0.0).astype(BF16)
            right_ref[first + 2 * j] = jnp.where(low, 0.0, turned).astype(BF16)
            left_ref[first + 2 * j + 1] = jnp.where(low, turned, 0.0).astype(BF16)
            right_ref[first + 2 * j + 1] = jnp.where(low, 0.0, both).astype(BF16)

    def edges(source, first):
        for j in range(REACH):
            for half in range(2):
                start = MOM_ROWS + (2 * j + half) * RHS
                x_ref[first + j, :, half * 128 : (half + 1) * 128] = source[start : start + RHS, :]

    for copy in small:
        copy.wait()
    spread_moments(mom_ref, SLOTS)
    spread_moments(rb_ref, odd * (2 * SLOTS))
    spread_moments(ra_ref, (1 - odd) * (2 * SLOTS))
    edges(rb_ref, odd * (REACH + SLOTS))
    edges(ra_ref, (1 - odd) * (REACH + SLOTS))
    near_base = position * SLOTS - REACH
    far_base = position * SLOTS - SLOTS
    for g in range(SLOTS):
        pairs = [
            left_ref[far_index_ref[2 * f, g] - far_base]
            + right_ref[far_index_ref[2 * f + 1, g] - far_base]
            for f in range(4)
        ]
        far_ref[:, g * RANK : (g + 1) * RANK] = dot(jnp.concatenate(pairs, axis=1), couple_ref[g])
    outs = []
    for i, part in enumerate(parts):
        tiles[i].wait()
        for g in range(part.start, part.start + part.size):
            columns = [x_ref[near_index_ref[k, g] - near_base] for k in range(6)]
            near_ref[g] = dot(jnp.concatenate(columns, axis=1), tile_ref[g])
        out = pltpu.make_async_copy(near_ref.at[part], near_hbm.at[part], near_sems.at[i])
        out.start()
        outs.append(out)
    for out in outs:
        out.wait()


def tree_sweep(ra_ref, gathered_ref, couple_zero_ref, down_path_ref):
    chip = lax.axis_index("leaf") >> 1
    total = gathered_ref[chip].astype(F32)
    sibling = ra_ref[BOX_AT:PAIR_ROWS, :][:, :RANK]
    downward = dot(sibling, couple_zero_ref[...])
    for level in range(1, LEVELS):
        level_sum = jnp.zeros((RHS, 128), F32)
        for x in range(1 << (level - 1), 1 << level):
            level_sum = level_sum + gathered_ref[chip ^ x].astype(F32)
        total = total + level_sum
        path = down_path_ref[(level - 1) * RANK : level * RANK, :]
        downward = downward + dot_nt(level_sum[:, :RANK].astype(BF16), path)
    return downward.astype(BF16), total


def spread_of(downward, far_ref, basis_ref, transfer_ref):
    block = block_of_lane()
    local_total = far_ref[...] + dot_nt(downward, transfer_ref[...])
    spread = []
    for q in range(SLOTS // 4):
        group = local_total[:, 4 * q * RANK : 4 * (q + 1) * RANK]
        apart = jnp.concatenate(
            [jnp.where(block == j, group, 0.0).astype(BF16) for j in range(4)], axis=0
        )
        four = dot(apart, basis_ref[4 * q * RANK : 4 * (q + 1) * RANK, :])
        spread += [four[j * RHS : (j + 1) * RHS, :] for j in range(4)]
    return spread


def middle_kernel(
    ra_ref,
    gathered_ref,
    couple_zero_ref,
    down_path_ref,
    far_ref,
    *refs,
):
    hbm, refs = refs[:5], refs[5:]
    pa_ref, pb_ref, own_ref, scal_ref, sb_hbm, mom_hbm, image_hbm, *refs = refs
    local, refs = refs[:5], refs[5:]
    sb_ref, image_ref, sems, out_sems, image_sems = refs
    copies = start_copies(hbm, local, sems)
    live_ref, transfer_ref, basis_ref, near_ref, rh_ref = local
    downward, total = tree_sweep(ra_ref, gathered_ref, couple_zero_ref, down_path_ref)
    for copy in copies:
        copy.wait()
    spread = spread_of(downward, far_ref, basis_ref, transfer_ref)
    outs = []
    square = read_sum(total, 0)
    norm = jnp.sqrt(square + EPSILON)
    scal_ref[...] = jnp.where(lanes() == 0, norm, square)
    inputs = []
    inner = jnp.zeros((RHS, POINTS), F32)
    length = jnp.zeros((RHS, POINTS), F32)
    for g in range(SLOTS):
        image = live_ref[g].astype(F32) * (near_ref[g] + spread[g]) / norm
        image_ref[g] = image
        if g % 4 == 3:
            four = pl.ds(g - 3, 4)
            out = pltpu.make_async_copy(
                image_ref.at[four], image_hbm.at[four], image_sems.at[g // 4]
            )
            out.start()
            outs.append(out)
        basis_one = rh_ref[g] * live_ref[g].astype(F32) / norm
        inner = inner + basis_one * image
        length = length + image * image
        sb = image.astype(BF16)
        sb_ref[g] = sb
        inputs.append(sb)
    outs += start_copies((sb_ref,), (sb_hbm,), out_sems)
    moments, box = up_moments(inputs, basis_ref, transfer_ref)
    pack_out(inputs, moments, box, [row_sum(inner), row_sum(length)], pa_ref, pb_ref, own_ref)
    mom_out = pltpu.make_async_copy(pb_ref.at[pl.ds(0, MOM_ROWS)], mom_hbm, out_sems.at[1])
    mom_out.start()
    for out in (*outs, mom_out):
        out.wait()


def as_row(column, shift):
    return jnp.sum(jnp.where(lanes() == rows() + shift, column, 0.0), axis=0, keepdims=True)


def as_column(row, shift):
    return row_sum(jnp.where(lanes() == rows() + shift, row, 0.0))


def last_operator_kernel(
    ra_ref,
    gathered_ref,
    couple_zero_ref,
    down_path_ref,
    scal_in_ref,
    far_ref,
    *refs,
):
    hbm, refs = refs[:6], refs[6:]
    one_ref, two_ref, v_ref, send_ref, scal_ref, *refs = refs
    local, (sems,) = refs[:6], refs[6:]
    copies = start_copies(hbm, local, sems)
    live_ref, transfer_ref, basis_ref, near_ref, rh_ref, image_ref = local
    downward, total = tree_sweep(ra_ref, gathered_ref, couple_zero_ref, down_path_ref)
    for copy in copies:
        copy.wait()
    spread = spread_of(downward, far_ref, basis_ref, transfer_ref)
    norm = scal_in_ref[:, 0:1]
    one_one = (scal_in_ref[:, 1:2] / norm) / norm
    first_inner = read_sum(total, 0)
    image_square = read_sum(total, 1)
    residue = image_square - 2.0 * first_inner * first_inner + first_inner * first_inner * one_one
    residue = jnp.maximum(residue, 0.0)
    first_length = jnp.sqrt(residue + EPSILON)
    one_two = (first_inner - first_inner * one_one) / first_length
    two_two = (residue / first_length) / first_length
    at = lanes()
    scal = jnp.zeros((RHS, 128), F32)
    for j, column in enumerate((norm, first_inner, first_length, one_one, one_two, two_two)):
        scal = jnp.where(at == j, column, scal)
    scal_ref[...] = scal
    cross = jnp.zeros((RHS, POINTS), F32)
    own = jnp.zeros((RHS, POINTS), F32)
    square = jnp.zeros((RHS, POINTS), F32)
    for g in range(SLOTS):
        image = image_ref[g]
        y = live_ref[g].astype(F32) * (near_ref[g] + spread[g])
        basis_one = rh_ref[g] * live_ref[g].astype(F32) / norm
        basis_two = (image - first_inner * basis_one) / first_length
        v = (y - first_inner * image) / first_length
        one_ref[g] = basis_one
        two_ref[g] = basis_two
        v_ref[g] = v
        cross = cross + basis_one * v
        own = own + basis_two * v
        square = square + v * v
    row = as_row(row_sum(cross), 0) + as_row(row_sum(own), 32) + as_row(row_sum(square), 64)
    for d in range(DEVICES):
        send_ref[d] = row


def final_kernel(one_ref, two_ref, v_ref, scal_ref, gathered_ref, next_ref, hess_ref):
    row = jnp.sum(gathered_ref[...], axis=0)
    cross, own, square = as_column(row, 0), as_column(row, 32), as_column(row, 64)
    norm, first_inner, first_length, one_one, one_two, two_two = (
        scal_ref[:, j : j + 1] for j in range(6)
    )
    residue = (
        square
        - 2.0 * cross * cross
        - 2.0 * own * own
        + cross * cross * one_one
        + own * own * two_two
        + 2.0 * cross * own * one_two
    )
    second_length = jnp.sqrt(jnp.maximum(residue, 0.0) + EPSILON)
    for j, column in enumerate((norm, first_inner, first_length, cross, own, second_length)):
        hess_ref[j : j + 1, :] = as_row(column, 0)[:, :RHS]
    for g in range(SLOTS):
        next_ref[g] = (v_ref[g] - cross * one_ref[g] - own * two_ref[g]) / second_length


def shape(dims, dtype):
    return jax.ShapeDtypeStruct(dims, dtype)


FIELD = (SLOTS, RHS, POINTS)
FAR_FIELD = (RHS, SLOTS * RANK)
PACKED = [shape((PAIR_ROWS, 128), BF16), shape((BOX_AT, 128), BF16), shape((RHS, 128), BF16)]
BASIS = (SLOTS * RANK, POINTS)
TRANSFER = (SLOTS * RANK, RANK)
TURNED = (RANK * RANK, NODES)
GATHERED = (CHIPS, RHS, 128)
LEAF_BUFFERS = [(TRANSFER, BF16), (BASIS, BF16), (FIELD, F32), (FIELD, F32)]
PATH = (LEVELS - 1) * RANK
WEIGHTS = [
    shape((2 * RANK, RANK), BF16),
    shape((RANK, RANK), BF16),
    shape((RANK, PATH), BF16),
    shape((PATH, RANK), BF16),
]
MIB = 1 << 20


def vmem(*kinds):
    return [pltpu.VMEM(*kind) for kind in kinds]


def sems(*dims):
    return [pltpu.SemaphoreType.DMA(dim) for dim in dims]


def in_hbm(*arrays):
    return [pltpu.with_memory_space_constraint(array, pltpu.HBM) for array in arrays]


def call(kernel, outs, in_specs, out_specs, scratch, mib, **more):
    return pl.pallas_call(
        kernel,
        out_shape=outs,
        in_specs=in_specs,
        out_specs=out_specs,
        scratch_shapes=scratch,
        compiler_params=pltpu.CompilerParams(vmem_limit_bytes=mib * MIB),
        **more,
    )


def on_device(
    right_hand,
    leaf_live,
    near_index,
    near_tile,
    far_index,
    far_couple,
    leaf_basis,
    leaf_transfer,
    tree_up,
    tree_couple,
):
    up_turned = tree_up.transpose(1, 2, 0).reshape(TURNED)
    couple_turned = tree_couple.transpose(1, 2, 0).reshape(TURNED)
    tiles = near_tile.reshape(SLOTS, 6 * POINTS, POINTS)
    couples = far_couple.reshape(SLOTS, 8 * RANK, RANK)
    indices = (near_index.T, far_index.T)
    leaf_basis = leaf_basis.reshape(BASIS)
    leaf_transfer = leaf_transfer.reshape(TRANSFER)
    same = [(i, i ^ 1) for i in range(DEVICES)]
    across = [(i, i + 1) for i in range(1, DEVICES - 1, 2)]
    across += [(j, i) for i, j in across]
    groups = [[2 * c + core for c in range(CHIPS)] for core in range(2)]

    def exchange(pa, pb, own, pair_up, out_path, n_sums):
        ra = lax.ppermute(pa, "leaf", same)
        rb = lax.ppermute(pb, "leaf", across)
        sent = call(
            functools.partial(pair_kernel, n_sums),
            pltpu.HBM(GATHERED, BF16),
            [VMEM] * 4,
            HBM,
            [*vmem(((4 * COPIES, RHS, 128), BF16)), *sems((11,))],
            4,
        )(own, ra, pair_up, out_path)
        gathered = lax.all_to_all(sent, "leaf", 0, 0, axis_index_groups=groups)
        return ra, rb, gathered

    def near_far(sb, mom, ra, rb):
        return call(
            near_far_kernel,
            [pltpu.HBM(FIELD, F32), shape(FAR_FIELD, F32)],
            [HBM, HBM, HBM, HBM, ANY, ANY, HBM, VMEM],
            [HBM, VMEM],
            [
                pltpu.SMEM((6, SLOTS), jnp.int32),
                pltpu.SMEM((8, SLOTS), jnp.int32),
                *vmem(
                    (FIELD, F32),
                    ((SLOTS + 2 * REACH, RHS, POINTS), BF16),
                    ((MOM_ROWS, 128), BF16),
                    ((PAIR_ROWS, 128), BF16),
                    ((BOX_AT, 128), BF16),
                    ((3 * SLOTS, RHS, 128), BF16),
                    ((3 * SLOTS, RHS, 128), BF16),
                    ((SLOTS, 6 * POINTS, POINTS), BF16),
                ),
                *sems((6,), (len(GROUPS),), (len(GROUPS),)),
            ],
            40,
            cost_estimate=pl.CostEstimate(
                flops=1_000_000_000, bytes_accessed=16_000_000, transcendentals=0
            ),
        )(*in_hbm(*indices, sb, mom), ra, rb, *in_hbm(tiles), couples)

    pa, pb, own, sb, mom, pair_up, couple_zero, out_path, down_path = call(
        first_kernel,
        [*PACKED, pltpu.HBM(FIELD, BF16), pltpu.HBM((MOM_ROWS, 128), BF16), *WEIGHTS],
        [HBM] * 6,
        [VMEM] * 3 + [HBM] * 2 + [VMEM] * 4,
        [
            pltpu.SMEM((SLOTS,), jnp.int32),
            *vmem(
                (FIELD, F32),
                (BASIS, BF16),
                (TRANSFER, BF16),
                (TURNED, BF16),
                (TURNED, BF16),
                (FIELD, BF16),
                ((8 * RANK, RANK), BF16),
                ((8 * RANK, RANK), BF16),
                ((8 * RANK, RANK), F32),
                ((8 * RANK, RANK), F32),
            ),
            *sems((6,), (2,)),
        ],
        16,
    )(*in_hbm(leaf_live, right_hand, leaf_basis, leaf_transfer, up_turned, couple_turned))
    ra, rb, gathered = exchange(pa, pb, own, pair_up, out_path, 1)
    near, far = near_far(sb, mom, ra, rb)
    count = len(LEAF_BUFFERS)
    pa, pb, own, scal, sb, mom, image = call(
        middle_kernel,
        [
            *PACKED,
            shape((RHS, 128), F32),
            pltpu.HBM(FIELD, BF16),
            pltpu.HBM((MOM_ROWS, 128), BF16),
            pltpu.HBM(FIELD, F32),
        ],
        [VMEM] * 5 + [HBM] * (count + 1),
        [VMEM] * 4 + [HBM] * 3,
        [
            pltpu.SMEM((SLOTS,), jnp.int32),
            *vmem(*LEAF_BUFFERS, (FIELD, BF16), (FIELD, F32)),
            *sems((count + 1,), (2,), (4,)),
        ],
        16,
    )(
        ra, gathered, couple_zero, down_path, far,
        *in_hbm(leaf_live, leaf_transfer, leaf_basis, near, right_hand),
    )
    ra, rb, gathered = exchange(pa, pb, own, pair_up, out_path, 2)
    near, far = near_far(sb, mom, ra, rb)
    one, two, v, sent, scal = call(
        last_operator_kernel,
        [shape(FIELD, F32)] * 3 + [shape((DEVICES, 1, 128), F32), shape((RHS, 128), F32)],
        [VMEM] * 6 + [HBM] * (count + 2),
        [VMEM] * 5,
        [
            pltpu.SMEM((SLOTS,), jnp.int32),
            *vmem(*LEAF_BUFFERS, (FIELD, F32)),
            *sems((count + 2,)),
        ],
        16,
    )(
        ra, gathered, couple_zero, down_path, scal, far,
        *in_hbm(leaf_live, leaf_transfer, leaf_basis, near, right_hand, image),
    )
    gathered = lax.all_to_all(sent, "leaf", 0, 0)
    return call(
        final_kernel, [shape(FIELD, F32), shape((6, RHS), F32)], [VMEM] * 5, [VMEM] * 2, [], 8
    )(one, two, v, scal, gathered)


def solution(mesh):
    placed = (
        P("leaf", None, None),
        P("leaf"),
        P("leaf", None),
        P("leaf", None, None, None),
        P("leaf", None),
        P("leaf", None, None, None),
        P("leaf", None, None),
        P("leaf", None, None),
        P(),
        P(),
    )
    return jax.shard_map(
        on_device,
        mesh=mesh,
        in_specs=placed,
        out_specs=(P("leaf", None, None), P()),
        check_vma=False,
    )
```

time: 102 us -> 91.4 us (0.90)
  Pallas kernels: 38.2 us -> 27.9 us
    pallas_call x3, Pallas kernels: 26.9 us -> 17.3 us  [the longest x2 14.3 us: near_far(): call(near_far_kernel, [pltpu.HBM(FIELD, F32), shape(FAR_FIELD, F32)], [HB...]
    pallas_call x1, Pallas kernels: 4.97 us -> 2.35 us  [on_device(): call(last_operator_kernel, [shape(FIELD, F32)] * 3 + [shape((DEVICES, 1,...]
    pallas_call x1, Pallas kernels: 2.94 us -> 4.53 us  [on_device(): call(first_kernel, [*PACKED, pltpu.HBM(FIELD, BF16), pltpu.HBM((MOM_ROWS,...]
  transfers between devices with their start and end apart: 6 -> 6, of which waited for: 4 -> 4; matrix products, arithmetic and copies ran while one was open for 0% -> 0% of each run, Pallas kernels for 21% -> 16%
where the time goes in v3:
time: 91.4 us; the launch traced here: 91 us
  starting transfers between devices  30.7 us (34%)
  Pallas kernels  27.9 us (31%)
  blocking collectives  19 us (21%)
  waiting for transfers between devices  12.5 us (14%)
    all_to_all x2, starting transfers between devices, exchange(): gathered = lax.all_to_all(sent, 'leaf', 0, 0, axis_index_groups=groups)  22 us
    all_to_all x1, blocking collectives, on_device(): gathered = lax.all_to_all(sent, 'leaf', 0, 0)  19 us
    pallas_call x2, Pallas kernels, near_far(): call(near_far_kernel, [pltpu.HBM(FIELD, F32), shape(FAR_FIELD, F32)], [HB...  14.3 us
    ppermute x2, waiting for transfers between devices, exchange(): rb = lax.ppermute(pb, 'leaf', across)  10.3 us
    ppermute x2, starting transfers between devices, exchange(): rb = lax.ppermute(pb, 'leaf', across)  7.24 us
    pallas_call x1, Pallas kernels, on_device(): call(first_kernel, [*PACKED, pltpu.HBM(FIELD, BF16), pltpu.HBM((MOM_ROWS,...  4.53 us
    pallas_call x1, Pallas kernels, on_device(): call(middle_kernel, [*PACKED, shape((RHS, 128), F32), pltpu.HBM(FIELD, BF...  2.91 us
    pallas_call x2, Pallas kernels, exchange(): call(functools.partial(pair_kernel, n_sums), pltpu.HBM(GATHERED, BF16), [...  2.54 us
  transfers between devices with their start and end apart: 6, of which 4 were waited for; matrix products, arithmetic and copies ran while one was open for 0% of the time, Pallas kernels for 16%

profile of v3, /device:TPU:1, one launch (start us, length us, event | category | flops | bytes accessed | tf_op | source)
XLA Modules:
  0.0 91.0 jit_solution(12882687958368786605)
XLA Ops:
  0.6 0.0 copy-start
  0.6 4.5 %shard_map.113 = (bf16[416,128]{1,0:T(8,128)(2,1)S(1)}, bf16[384,128]{1,0:T(8,128)(2,1)S(1)}, bf16[32,128]{1,0:T(8,128)(2,1)S(1)}, bf16[16,32,256]{2,1,0:T(8,128...) custom-call(s32[16]{0:T(128)} %refs_0_.3, ...), custom_call_target="tpu_custom_call" | custom-call | tf_op jit(solution)/shard_map/pallas_call | solution.py:647
  5.2 1.5 %collective-permute-start = (bf16[416,128]{1,0:T(8,128)(2,1)S(1)}, bf16[416,128]{1,0:T(8,128)(2,1)S(1)}, u32[]{:S(2)}, u32[]{:S(2)}) collective-permute-start(bf16[416,128]{1,0:T(8,128)(2,1)S(1)} %get-tuple-element.27), channel_id=1, source_target_pairs={{0,1},{1,0},{2,3},{3,2},{4,5},{5,4},{6,7},{7,6},{8,9},{9,8},{10,11... | collective-permute-start | bytes 319496 | tf_op jit(solution)/shard_map/ppermute | solution.py:607
  6.6 1.0 %collective-permute-done.ra_ref.ra_any = bf16[416,128]{1,0:T(8,128)(2,1)S(1)} collective-permute-done((bf16[416,128]{1,0:T(8,128)(2,1)S(1)}, bf16[416,128]{1,0:T(8,128)(2,1)S(1)}, u32[]{:S(2)}, u32[]{:S(2)}) %collective-permute-start) | collective-permute-done | bytes 106528 | tf_op jit(solution)/shard_map/ppermute | solution.py:607
  7.6 1.3 %shard_map.114 = bf16[64,32,128]{2,1,0:T(8,128)(2,1)} custom-call(bf16[32,128]{1,0:T(8,128)(2,1)S(1)} %get-tuple-element.28.own_ref, bf16[416,128]{1,0:T(8,128)(2,1)S(1)} %collective-permute-done.ra_ref.ra_any, bf16[128,64]{1,0:T(8,128)(2,1)S(1)} %get-tuple-element.29.up_ref, bf16[64,384]{1,0:T(8,128)(2,1)S(1)} %get-tuple-element.30.path_ref), custom_call_target="tpu_custom_call" | custom-call | tf_op jit(solution)/shard_map/pallas_call | solution.py:609
  8.9 11.3 %all-to-all-start = ((bf16[64,32,128]{2,1,0:T(8,128)(2,1)}), bf16[64,32,128]{2,1,0:T(8,128)(2,1)S(1)}, u32[]{:S(2)}, u32[]{:S(2)}) async-start(bf16[64,32,128]{2,1,0:T(8,128)(2,1)} %shard_map.114), calls=%async_computation | async-start | bytes 1048576 | tf_op jit(solution)/shard_map/all_to_all | solution.py:617
  20.1 3.7 %collective-permute-start.1 = (bf16[384,128]{1,0:T(8,128)(2,1)S(1)}, bf16[384,128]{1,0:T(8,128)(2,1)S(1)}, u32[]{:S(2)}, u32[]{:S(2)}) collective-permute-start(bf16[384,128]{1,0:T(8,128)(2,1)S(1)} %get-tuple-element.35), channel_id=1, source_target_pairs={{1,2},{3,4},{5,6},{7,8},{9,10},{11,12},{13,14},{15,16},{17,18},{19... | collective-permute-start | bytes 294920 | tf_op jit(solution)/shard_map/ppermute | solution.py:608
  23.8 5.0 %collective-permute-done.1.rb_any = bf16[384,128]{1,0:T(8,128)(2,1)S(1)} collective-permute-done((bf16[384,128]{1,0:T(8,128)(2,1)S(1)}, bf16[384,128]{1,0:T(8,128)(2,1)S(1)}, u32[]{:S(2)}, u32[]{:S(2)}) %collective-permute-start.1) | collective-permute-done | bytes 98336 | tf_op jit(solution)/shard_map/ppermute | solution.py:608
  28.9 0.0 copy-done
  28.9 7.2 %shard_map.115 = (f32[16,32,256]{2,1,0:T(8,128)}, f32[32,1024]{1,0:T(8,128)S(1)}) custom-call(s32[6,16]{1,0:T(8,128)} %bitcast.24, s32[8,16]{1,0:T(8,128)} %bitcast.26, bf16[16,32,256]{2,1,0:T(8,128)(2,1)} %get-tuple-element.33.sb_hbm, bf16[256,128]{1,0:T(8,128)(2,1)} %get-tuple-element.34.mom_hbm, bf16[416,128]{1,0:T(8,128)(2,1)S(1)} %collective-permute-done.ra_ref.ra_any, ...), custom_call_target="tpu_custom_call" | custom-call | flops 1000000000 | bytes 16000000 | tf_op jit(solution)/shard_map/pallas_call | solution.py:621
  36.1 0.0 all-to-all-done.gathered_ref
  36.1 2.9 %shard_map.116 = (bf16[416,128]{1,0:T(8,128)(2,1)S(1)}, bf16[384,128]{1,0:T(8,128)(2,1)S(1)}, bf16[32,128]{1,0:T(8,128)(2,1)S(1)}, f32[32,128]{1,0:T(8,128)S(1)}...) custom-call(bf16[416,128]{1,0:T(8,128)(2,1)S(1)} %collective-permute-done.ra_ref.ra_any, ...), custom_call_target="tpu_custom_call" | custom-call | tf_op jit(solution)/shard_map/pallas_call | solution.py:673
  39.0 0.1 collective-permute-start.2
  39.1 1.3 %collective-permute-done.2.ra_ref.ra_any = bf16[416,128]{1,0:T(8,128)(2,1)S(1)} collective-permute-done((bf16[416,128]{1,0:T(8,128)(2,1)S(1)}, bf16[416,128]{1,0:T(8,128)(2,1)S(1)}, u32[]{:S(2)}, u32[]{:S(2)}) %collective-permute-start.2) | collective-permute-done | bytes 106528 | tf_op jit(solution)/shard_map/ppermute | solution.py:607
  40.4 1.3 %shard_map.117 = bf16[64,32,128]{2,1,0:T(8,128)(2,1)} custom-call(bf16[32,128]{1,0:T(8,128)(2,1)S(1)} %get-tuple-element.39.own_ref, bf16[416,128]{1,0:T(8,128)(2,1)S(1)} %collective-permute-done.2.ra_ref.ra_any, bf16[128,64]{1,0:T(8,128)(2,1)S(1)} %get-tuple-element.29.up_ref, bf16[64,384]{1,0:T(8,128)(2,1)S(1)} %get-tuple-element.30.path_ref), custom_call_target="tpu_custom_call" | custom-call | tf_op jit(solution)/shard_map/pallas_call | solution.py:609
  41.7 10.7 %all-to-all-start.1 = ((bf16[64,32,128]{2,1,0:T(8,128)(2,1)}), bf16[64,32,128]{2,1,0:T(8,128)(2,1)S(1)}, u32[]{:S(2)}, u32[]{:S(2)}) async-start(bf16[64,32,128]{2,1,0:T(8,128)(2,1)} %shard_map.117), calls=%async_computation.1 | async-start | bytes 1048576 | tf_op jit(solution)/shard_map/all_to_all | solution.py:617
  52.4 3.5 %collective-permute-start.3 = (bf16[384,128]{1,0:T(8,128)(2,1)S(1)}, bf16[384,128]{1,0:T(8,128)(2,1)S(1)}, u32[]{:S(2)}, u32[]{:S(2)}) collective-permute-start(bf16[384,128]{1,0:T(8,128)(2,1)S(1)} %get-tuple-element.43), channel_id=1, source_target_pairs={{1,2},{3,4},{5,6},{7,8},{9,10},{11,12},{13,14},{15,16},{17,18},{19... | collective-permute-start | bytes 294920 | tf_op jit(solution)/shard_map/ppermute | solution.py:608
  55.9 5.2 %collective-permute-done.3.rb_any = bf16[384,128]{1,0:T(8,128)(2,1)S(1)} collective-permute-done((bf16[384,128]{1,0:T(8,128)(2,1)S(1)}, bf16[384,128]{1,0:T(8,128)(2,1)S(1)}, u32[]{:S(2)}, u32[]{:S(2)}) %collective-permute-start.3) | collective-permute-done | bytes 98336 | tf_op jit(solution)/shard_map/ppermute | solution.py:608
  61.2 7.2 %shard_map.118 = (f32[16,32,256]{2,1,0:T(8,128)}, f32[32,1024]{1,0:T(8,128)S(1)}) custom-call(s32[6,16]{1,0:T(8,128)} %bitcast.25, s32[8,16]{1,0:T(8,128)} %bitcast.27, bf16[16,32,256]{2,1,0:T(8,128)(2,1)} %get-tuple-element.41.sb_hbm, bf16[256,128]{1,0:T(8,128)(2,1)} %get-tuple-element.42.mom_hbm, ...), custom_call_target="tpu_custom_call" | custom-call | flops 1000000000 | bytes 16000000 | tf_op jit(solution)/shard_map/pallas_call | solution.py:621
  68.3 0.0 all-to-all-done.1.gathered_ref
  68.4 2.3 %shard_map.119 = (f32[16,32,256]{2,1,0:T(8,128)S(1)}, f32[16,32,256]{2,1,0:T(8,128)S(1)}, f32[16,32,256]{2,1,0:T(8,128)S(1)}, f32[128,1,128]{2,1,0:T(1,128)S(1)}, f32[32,128]{1,0:T(8,128)S(1)}) custom-call(bf16[416,128]{1,0:T(8,128)(2,1)S(1)} %collective-permute-done.2.ra_ref.ra_any, bf16[64,32,128]{2,1,0:T(8,128)(2,1)S(1)} %all-to-all-done.1.gathered_ref, ...), custom_call_target="tpu_custom_call" | custom-call | tf_op jit(solution)/shard_map/pallas_call | solution.py:696
  70.7 19.0 %all_to_all.15.gathered_ref = f32[128,1,128]{2,1,0:T(1,128)S(1)} all-to-all(f32[128,1,128]{2,1,0:T(1,128)S(1)} %get-tuple-element.51), channel_id=1, replica_groups=mesh['leaf'=128] {'leaf'}, dimensions={0} | all-to-all | bytes 131072 | tf_op jit(solution)/shard_map/all_to_all | solution.py:711
  89.7 1.2 %shard_map.120 = (f32[16,32,256]{2,1,0:T(8,128)}, f32[6,32]{1,0:T(8,128)}) custom-call(f32[16,32,256]{2,1,0:T(8,128)S(1)} %get-tuple-element.47.one_ref, f32[16,32,256]{2,1,0:T(8,128)S(1)} %get-tuple-element.48.two_ref, f32[16,32,256]{2,1,0:T(8,128)S(1)} %get-tuple-element.49.v_ref, f32[32,128]{1,0:T(8,128)S(1)} %get-tuple-element.50.scal_ref, ...), custom_call_target="tpu_custom_call" | custom-call | tf_op jit(solution)/shard_map/pallas_call | solution.py:712
Async XLA Ops:
  0.6 28.3 %copy-start = (bf16[16,8,64,64]{3,2,1,0:T(8,128)(2,1)S(1)}, bf16[16,8,64,64]{3,2,1,0:T(8,128)(2,1)}, u32[]{:S(2)}) copy-start(bf16[16,8,64,64]{3,2,1,0:T(8,128)(2,1)} %param.15) | copy-start | bytes 3145732
  5.2 2.4 %collective-permute-start = (bf16[416,128]{1,0:T(8,128)(2,1)S(1)}, bf16[416,128]{1,0:T(8,128)(2,1)S(1)}, u32[]{:S(2)}, u32[]{:S(2)}) collective-permute-start(bf16[416,128]{1,0:T(8,128)(2,1)S(1)} %get-tuple-element.27), channel_id=1, source_target_pairs={{0,1},{1,0},{2,3},{3,2},{4,5},{5,4},{6,7},{7,6},{8,9},{9,8},{10,11... | collective-permute-start | bytes 319496 | tf_op jit(solution)/shard_map/ppermute | solution.py:607
  8.9 27.2 %all-to-all-start = ((bf16[64,32,128]{2,1,0:T(8,128)(2,1)}), bf16[64,32,128]{2,1,0:T(8,128)(2,1)S(1)}, u32[]{:S(2)}, u32[]{:S(2)}) async-start(bf16[64,32,128]{2,1,0:T(8,128)(2,1)} %shard_map.114), calls=%async_computation | async-start | bytes 1048576 | tf_op jit(solution)/shard_map/all_to_all | solution.py:617
  20.1 8.8 %collective-permute-start.1 = (bf16[384,128]{1,0:T(8,128)(2,1)S(1)}, bf16[384,128]{1,0:T(8,128)(2,1)S(1)}, u32[]{:S(2)}, u32[]{:S(2)}) collective-permute-start(bf16[384,128]{1,0:T(8,128)(2,1)S(1)} %get-tuple-element.35), channel_id=1, source_target_pairs={{1,2},{3,4},{5,6},{7,8},{9,10},{11,12},{13,14},{15,16},{17,18},{19... | collective-permute-start | bytes 294920 | tf_op jit(solution)/shard_map/ppermute | solution.py:608
  39.0 1.4 %collective-permute-start.2 = (bf16[416,128]{1,0:T(8,128)(2,1)S(1)}, bf16[416,128]{1,0:T(8,128)(2,1)S(1)}, u32[]{:S(2)}, u32[]{:S(2)}) collective-permute-start(bf16[416,128]{1,0:T(8,128)(2,1)S(1)} %get-tuple-element.38), channel_id=1, source_target_pairs={{0,1},{1,0},{2,3},{3,2},{4,5},{5,4},{6,7},{7,6},{8,9},{9,8},{10,11... | collective-permute-start | bytes 319496 | tf_op jit(solution)/shard_map/ppermute | solution.py:607
  41.7 26.7 %all-to-all-start.1 = ((bf16[64,32,128]{2,1,0:T(8,128)(2,1)}), bf16[64,32,128]{2,1,0:T(8,128)(2,1)S(1)}, u32[]{:S(2)}, u32[]{:S(2)}) async-start(bf16[64,32,128]{2,1,0:T(8,128)(2,1)} %shard_map.117), calls=%async_computation.1 | async-start | bytes 1048576 | tf_op jit(solution)/shard_map/all_to_all | solution.py:617
  52.4 8.8 %collective-permute-start.3 = (bf16[384,128]{1,0:T(8,128)(2,1)S(1)}, bf16[384,128]{1,0:T(8,128)(2,1)S(1)}, u32[]{:S(2)}, u32[]{:S(2)}) collective-permute-start(bf16[384,128]{1,0:T(8,128)(2,1)S(1)} %get-tuple-element.43), channel_id=1, source_target_pairs={{1,2},{3,4},{5,6},{7,8},{9,10},{11,12},{13,14},{15,16},{17,18},{19... | collective-permute-start | bytes 294920 | tf_op jit(solution)/shard_map/ppermute | solution.py:608

commit v4 on v3

--- a/solution.py
+++ b/solution.py
@@ -168,7 +168,6 @@
     pb_ref,
     own_ref,
     sb_hbm,
-    mom_hbm,
     pair_ref,
     couple_zero_ref,
     out_path_ref,
@@ -185,7 +184,7 @@
     up_rows_ref,
     couple_rows_ref,
     sems,
-    out_sems,
+    out_sem,
 ):
     up_in, couple_in, *copies = start_copies(
         (up_hbm, couple_hbm, live_hbm, rh_hbm, basis_hbm, transfer_hbm),
@@ -210,12 +209,10 @@
         sb = s.astype(BF16)
         sb_ref[g] = sb
         inputs.append(sb)
-    sb_out = pltpu.make_async_copy(sb_ref, sb_hbm, out_sems.at[0])
+    sb_out = pltpu.make_async_copy(sb_ref, sb_hbm, out_sem)
     sb_out.start()
     moments, box = up_moments(inputs, basis_ref, transfer_ref)
     pack_out(inputs, moments, box, [row_sum(square)], pa_ref, pb_ref, own_ref)
-    mom_out = pltpu.make_async_copy(pb_ref.at[pl.ds(0, MOM_ROWS)], mom_hbm, out_sems.at[1])
-    mom_out.start()
     pair_ref[...] = up_nodes_ref[0 : 2 * RANK, :]
     couple_zero_ref[...] = couple_nodes_ref[0:RANK, :]
 
@@ -237,8 +234,7 @@
             if level + 1 < LEVELS:
                 chain = dot(chain, node(up_nodes_ref, level + 1)).astype(BF16)
     out_path_ref[...] = jnp.concatenate(outward, axis=1).astype(BF16)
-    for copy in (sb_out, mom_out):
-        copy.wait()
+    sb_out.wait()
 
 
 def pair_kernel(n_sums, own_ref, ra_ref, up_ref, path_ref, out_hbm, block_ref, out_sems):
@@ -288,7 +284,7 @@
     near_index_hbm,
     far_index_hbm,
     sb_hbm,
-    mom_hbm,
+    mom_ref,
     ra_any,
     rb_any,
     tile_hbm,
@@ -299,7 +295,6 @@
     far_index_ref,
     near_ref,
     x_ref,
-    mom_ref,
     ra_ref,
     rb_ref,
     left_ref,
@@ -310,9 +305,8 @@
     near_sems,
 ):
     small = start_copies(
-        (mom_hbm, rb_any, ra_any, sb_hbm, near_index_hbm, far_index_hbm),
+        (rb_any, ra_any, sb_hbm, near_index_hbm, far_index_hbm),
         (
-            mom_ref,
             rb_ref,
             ra_ref,
             x_ref.at[pl.ds(REACH, SLOTS)],
@@ -344,9 +338,9 @@
                 start = MOM_ROWS + (2 * j + half) * RHS
                 x_ref[first + j, :, half * 128 : (half + 1) * 128] = source[start : start + RHS, :]
 
+    spread_moments(mom_ref, SLOTS)
     for copy in small:
         copy.wait()
-    spread_moments(mom_ref, SLOTS)
     spread_moments(rb_ref, odd * (2 * SLOTS))
     spread_moments(ra_ref, (1 - odd) * (2 * SLOTS))
     edges(rb_ref, odd * (REACH + SLOTS))
@@ -411,7 +405,7 @@
     *refs,
 ):
     hbm, refs = refs[:5], refs[5:]
-    pa_ref, pb_ref, own_ref, scal_ref, sb_hbm, mom_hbm, image_hbm, *refs = refs
+    pa_ref, pb_ref, own_ref, scal_ref, sb_hbm, image_hbm, *refs = refs
     local, refs = refs[:5], refs[5:]
     sb_ref, image_ref, sems, out_sems, image_sems = refs
     copies = start_copies(hbm, local, sems)
@@ -446,9 +440,7 @@
     outs += start_copies((sb_ref,), (sb_hbm,), out_sems)
     moments, box = up_moments(inputs, basis_ref, transfer_ref)
     pack_out(inputs, moments, box, [row_sum(inner), row_sum(length)], pa_ref, pb_ref, own_ref)
-    mom_out = pltpu.make_async_copy(pb_ref.at[pl.ds(0, MOM_ROWS)], mom_hbm, out_sems.at[1])
-    mom_out.start()
-    for out in (*outs, mom_out):
+    for out in outs:
         out.wait()
 
 
@@ -599,7 +591,7 @@
     leaf_basis = leaf_basis.reshape(BASIS)
     leaf_transfer = leaf_transfer.reshape(TRANSFER)
     same = [(i, i ^ 1) for i in range(DEVICES)]
-    across = [(i, i + 1) for i in range(1, DEVICES - 1, 2)]
+    across = [(i, (i + 1) % DEVICES) for i in range(1, DEVICES, 2)]
     across += [(j, i) for i, j in across]
     groups = [[2 * c + core for c in range(CHIPS)] for core in range(2)]
 
@@ -617,11 +609,11 @@
         gathered = lax.all_to_all(sent, "leaf", 0, 0, axis_index_groups=groups)
         return ra, rb, gathered
 
-    def near_far(sb, mom, ra, rb):
+    def near_far(sb, pb, ra, rb):
         return call(
             near_far_kernel,
             [pltpu.HBM(FIELD, F32), shape(FAR_FIELD, F32)],
-            [HBM, HBM, HBM, HBM, ANY, ANY, HBM, VMEM],
+            [HBM, HBM, HBM, VMEM, ANY, ANY, HBM, VMEM],
             [HBM, VMEM],
             [
                 pltpu.SMEM((6, SLOTS), jnp.int32),
@@ -629,26 +621,25 @@
                 *vmem(
                     (FIELD, F32),
                     ((SLOTS + 2 * REACH, RHS, POINTS), BF16),
-                    ((MOM_ROWS, 128), BF16),
                     ((PAIR_ROWS, 128), BF16),
                     ((BOX_AT, 128), BF16),
                     ((3 * SLOTS, RHS, 128), BF16),
                     ((3 * SLOTS, RHS, 128), BF16),
                     ((SLOTS, 6 * POINTS, POINTS), BF16),
                 ),
-                *sems((6,), (len(GROUPS),), (len(GROUPS),)),
+                *sems((5,), (len(GROUPS),), (len(GROUPS),)),
             ],
             40,
             cost_estimate=pl.CostEstimate(
                 flops=1_000_000_000, bytes_accessed=16_000_000, transcendentals=0
             ),
-        )(*in_hbm(*indices, sb, mom), ra, rb, *in_hbm(tiles), couples)
-
-    pa, pb, own, sb, mom, pair_up, couple_zero, out_path, down_path = call(
+        )(*in_hbm(*indices, sb), pb, ra, rb, *in_hbm(tiles), couples)
+
+    pa, pb, own, sb, pair_up, couple_zero, out_path, down_path = call(
         first_kernel,
-        [*PACKED, pltpu.HBM(FIELD, BF16), pltpu.HBM((MOM_ROWS, 128), BF16), *WEIGHTS],
+        [*PACKED, pltpu.HBM(FIELD, BF16), *WEIGHTS],
         [HBM] * 6,
-        [VMEM] * 3 + [HBM] * 2 + [VMEM] * 4,
+        [VMEM] * 3 + [HBM] + [VMEM] * 4,
         [
             pltpu.SMEM((SLOTS,), jnp.int32),
             *vmem(
@@ -663,28 +654,28 @@
                 ((8 * RANK, RANK), F32),
                 ((8 * RANK, RANK), F32),
             ),
-            *sems((6,), (2,)),
+            *sems((6,)),
+            pltpu.SemaphoreType.DMA,
         ],
         16,
     )(*in_hbm(leaf_live, right_hand, leaf_basis, leaf_transfer, up_turned, couple_turned))
     ra, rb, gathered = exchange(pa, pb, own, pair_up, out_path, 1)
-    near, far = near_far(sb, mom, ra, rb)
+    near, far = near_far(sb, pb, ra, rb)
     count = len(LEAF_BUFFERS)
-    pa, pb, own, scal, sb, mom, image = call(
+    pa, pb, own, scal, sb, image = call(
         middle_kernel,
         [
             *PACKED,
             shape((RHS, 128), F32),
             pltpu.HBM(FIELD, BF16),
-            pltpu.HBM((MOM_ROWS, 128), BF16),
             pltpu.HBM(FIELD, F32),
         ],
         [VMEM] * 5 + [HBM] * (count + 1),
-        [VMEM] * 4 + [HBM] * 3,
+        [VMEM] * 4 + [HBM] * 2,
         [
             pltpu.SMEM((SLOTS,), jnp.int32),
             *vmem(*LEAF_BUFFERS, (FIELD, BF16), (FIELD, F32)),
-            *sems((count + 1,), (2,), (4,)),
+            *sems((count + 1,), (1,), (4,)),
         ],
         16,
     )(
@@ -692,7 +683,7 @@
         *in_hbm(leaf_live, leaf_transfer, leaf_basis, near, right_hand),
     )
     ra, rb, gathered = exchange(pa, pb, own, pair_up, out_path, 2)
-    near, far = near_far(sb, mom, ra, rb)
+    near, far = near_far(sb, pb, ra, rb)
     one, two, v, sent, scal = call(
         last_operator_kernel,
         [shape(FIELD, F32)] * 3 + [shape((DEVICES, 1, 128), F32), shape((RHS, 128), F32)],

time: 91.4 us -> 90.4 us (0.989)
  starting transfers between devices: 30.7 us -> 26.9 us
  waiting for transfers between devices: 12.5 us -> 15.9 us
    all_to_all x2, starting transfers between devices: 22 us -> 15.9 us  [exchange(): gathered = lax.all_to_all(sent, 'leaf', 0, 0, axis_index_groups=groups)]
    ppermute x2, starting transfers between devices: 1.54 us -> 7.59 us  [exchange(): ra = lax.ppermute(pa, 'leaf', same)]
    ppermute x2, starting transfers between devices: 7.24 us -> 3.4 us  [exchange(): rb = lax.ppermute(pb, 'leaf', across)]
    ppermute x2, waiting for transfers between devices: 10.3 us -> 14 us  [exchange(): rb = lax.ppermute(pb, 'leaf', across)]
where the time goes in v4:
time: 90.4 us; the launch traced here: 90.1 us
  Pallas kernels  27.7 us (31%)
  starting transfers between devices  26.9 us (30%)
  blocking collectives  18.8 us (21%)
  waiting for transfers between devices  15.9 us (18%)
    all_to_all x1, blocking collectives, on_device(): gathered = lax.all_to_all(sent, 'leaf', 0, 0)  18.8 us
    all_to_all x2, starting transfers between devices, exchange(): gathered = lax.all_to_all(sent, 'leaf', 0, 0, axis_index_groups=groups)  15.9 us
    pallas_call x2, Pallas kernels, near_far(): call(near_far_kernel, [pltpu.HBM(FIELD, F32), shape(FAR_FIELD, F32)], [HB...  14.3 us
    ppermute x2, waiting for transfers between devices, exchange(): rb = lax.ppermute(pb, 'leaf', across)  14 us
    ppermute x2, starting transfers between devices, exchange(): ra = lax.ppermute(pa, 'leaf', same)  7.59 us
    pallas_call x1, Pallas kernels, on_device(): call(first_kernel, [*PACKED, pltpu.HBM(FIELD, BF16), *WEIGHTS], [HBM] * 6...  4.52 us
    ppermute x2, starting transfers between devices, exchange(): rb = lax.ppermute(pb, 'leaf', across)  3.4 us
    pallas_call x1, Pallas kernels, on_device(): call(middle_kernel, [*PACKED, shape((RHS, 128), F32), pltpu.HBM(FIELD, BF...  2.79 us
  transfers between devices with their start and end apart: 6, of which 4 were waited for; matrix products, arithmetic and copies ran while one was open for 0% of the time, Pallas kernels for 16%

profile of v4, /device:TPU:1, one launch (start us, length us, event | category | flops | bytes accessed | tf_op | source)
XLA Modules:
  0.0 90.1 jit_solution(3576731810516781234)
XLA Ops:
  0.6 0.0 copy-start
  0.6 4.5 %shard_map.113 = (bf16[416,128]{1,0:T(8,128)(2,1)S(1)}, bf16[384,128]{1,0:T(8,128)(2,1)S(1)}, bf16[32,128]{1,0:T(8,128)(2,1)S(1)}, bf16[16,32,256]{2,1,0:T(8,128...) custom-call(s32[16]{0:T(128)} %refs_0_.3, ...), custom_call_target="tpu_custom_call" | custom-call | tf_op jit(solution)/shard_map/pallas_call | solution.py:638
  5.2 1.5 %collective-permute-start = (bf16[416,128]{1,0:T(8,128)(2,1)S(1)}, bf16[416,128]{1,0:T(8,128)(2,1)S(1)}, u32[]{:S(2)}, u32[]{:S(2)}) collective-permute-start(bf16[416,128]{1,0:T(8,128)(2,1)S(1)} %get-tuple-element.25), channel_id=1, source_target_pairs={{0,1},{1,0},{2,3},{3,2},{4,5},{5,4},{6,7},{7,6},{8,9},{9,8},{10,11... | collective-permute-start | bytes 319496 | tf_op jit(solution)/shard_map/ppermute | solution.py:599
  6.6 1.0 %collective-permute-done.ra_ref.ra_any = bf16[416,128]{1,0:T(8,128)(2,1)S(1)} collective-permute-done((bf16[416,128]{1,0:T(8,128)(2,1)S(1)}, bf16[416,128]{1,0:T(8,128)(2,1)S(1)}, u32[]{:S(2)}, u32[]{:S(2)}) %collective-permute-start) | collective-permute-done | bytes 106528 | tf_op jit(solution)/shard_map/ppermute | solution.py:599
  7.6 1.3 %shard_map.114 = bf16[64,32,128]{2,1,0:T(8,128)(2,1)} custom-call(bf16[32,128]{1,0:T(8,128)(2,1)S(1)} %get-tuple-element.26.own_ref, bf16[416,128]{1,0:T(8,128)(2,1)S(1)} %collective-permute-done.ra_ref.ra_any, bf16[128,64]{1,0:T(8,128)(2,1)S(1)} %get-tuple-element.27.up_ref, bf16[64,384]{1,0:T(8,128)(2,1)S(1)} %get-tuple-element.28.path_ref), custom_call_target="tpu_custom_call" | custom-call | tf_op jit(solution)/shard_map/pallas_call | solution.py:601
  8.8 11.3 %all-to-all-start = ((bf16[64,32,128]{2,1,0:T(8,128)(2,1)}), bf16[64,32,128]{2,1,0:T(8,128)(2,1)S(1)}, u32[]{:S(2)}, u32[]{:S(2)}) async-start(bf16[64,32,128]{2,1,0:T(8,128)(2,1)} %shard_map.114), calls=%async_computation | async-start | bytes 1048576 | tf_op jit(solution)/shard_map/all_to_all | solution.py:609
  20.1 1.9 %collective-permute-start.1 = (bf16[384,128]{1,0:T(8,128)(2,1)S(1)}, bf16[384,128]{1,0:T(8,128)(2,1)S(1)}, u32[]{:S(2)}, u32[]{:S(2)}) collective-permute-start(bf16[384,128]{1,0:T(8,128)(2,1)S(1)} %get-tuple-element.32.mom_ref), channel_id=1, source_target_pairs={{1,2},{3,4},{5,6},{7,8},{9,10},{11,12},{13,14},{15,16},{17,18},{19... | collective-permute-start | bytes 294920 | tf_op jit(solution)/shard_map/ppermute | solution.py:600
  22.0 6.9 %collective-permute-done.1.rb_any = bf16[384,128]{1,0:T(8,128)(2,1)S(1)} collective-permute-done((bf16[384,128]{1,0:T(8,128)(2,1)S(1)}, bf16[384,128]{1,0:T(8,128)(2,1)S(1)}, u32[]{:S(2)}, u32[]{:S(2)}) %collective-permute-start.1) | collective-permute-done | bytes 98336 | tf_op jit(solution)/shard_map/ppermute | solution.py:600
  28.9 0.0 copy-done
  28.9 7.1 %shard_map.115 = (f32[16,32,256]{2,1,0:T(8,128)}, f32[32,1024]{1,0:T(8,128)S(1)}) custom-call(s32[6,16]{1,0:T(8,128)} %bitcast.24, s32[8,16]{1,0:T(8,128)} %bitcast.26, bf16[16,32,256]{2,1,0:T(8,128)(2,1)} %get-tuple-element.31.sb_hbm, bf16[384,128]{1,0:T(8,128)(2,1)S(1)} %get-tuple-element.32.mom_ref, ...), custom_call_target="tpu_custom_call" | custom-call | flops 1000000000 | bytes 16000000 | tf_op jit(solution)/shard_map/pallas_call | solution.py:613
  36.0 0.0 all-to-all-done.gathered_ref
  36.0 2.8 %shard_map.116 = (bf16[416,128]{1,0:T(8,128)(2,1)S(1)}, bf16[384,128]{1,0:T(8,128)(2,1)S(1)}, bf16[32,128]{1,0:T(8,128)(2,1)S(1)}, f32[32,128]{1,0:T(8,128)S(1)}...) custom-call(bf16[416,128]{1,0:T(8,128)(2,1)S(1)} %collective-permute-done.ra_ref.ra_any, ...), custom_call_target="tpu_custom_call" | custom-call | tf_op jit(solution)/shard_map/pallas_call | solution.py:665
  38.8 6.1 %collective-permute-start.2 = (bf16[416,128]{1,0:T(8,128)(2,1)S(1)}, bf16[416,128]{1,0:T(8,128)(2,1)S(1)}, u32[]{:S(2)}, u32[]{:S(2)}) collective-permute-start(bf16[416,128]{1,0:T(8,128)(2,1)S(1)} %get-tuple-element.35), channel_id=1, source_target_pairs={{0,1},{1,0},{2,3},{3,2},{4,5},{5,4},{6,7},{7,6},{8,9},{9,8},{10,11... | collective-permute-start | bytes 319496 | tf_op jit(solution)/shard_map/ppermute | solution.py:599
  45.0 1.0 %collective-permute-done.2.ra_ref.ra_any = bf16[416,128]{1,0:T(8,128)(2,1)S(1)} collective-permute-done((bf16[416,128]{1,0:T(8,128)(2,1)S(1)}, bf16[416,128]{1,0:T(8,128)(2,1)S(1)}, u32[]{:S(2)}, u32[]{:S(2)}) %collective-permute-start.2) | collective-permute-done | bytes 106528 | tf_op jit(solution)/shard_map/ppermute | solution.py:599
  45.9 1.3 %shard_map.117 = bf16[64,32,128]{2,1,0:T(8,128)(2,1)} custom-call(bf16[32,128]{1,0:T(8,128)(2,1)S(1)} %get-tuple-element.36.own_ref, bf16[416,128]{1,0:T(8,128)(2,1)S(1)} %collective-permute-done.2.ra_ref.ra_any, bf16[128,64]{1,0:T(8,128)(2,1)S(1)} %get-tuple-element.27.up_ref, bf16[64,384]{1,0:T(8,128)(2,1)S(1)} %get-tuple-element.28.path_ref), custom_call_target="tpu_custom_call" | custom-call | tf_op jit(solution)/shard_map/pallas_call | solution.py:601
  47.2 4.6 %all-to-all-start.1 = ((bf16[64,32,128]{2,1,0:T(8,128)(2,1)}), bf16[64,32,128]{2,1,0:T(8,128)(2,1)S(1)}, u32[]{:S(2)}, u32[]{:S(2)}) async-start(bf16[64,32,128]{2,1,0:T(8,128)(2,1)} %shard_map.117), calls=%async_computation.1 | async-start | bytes 1048576 | tf_op jit(solution)/shard_map/all_to_all | solution.py:609
  51.9 1.5 %collective-permute-start.3 = (bf16[384,128]{1,0:T(8,128)(2,1)S(1)}, bf16[384,128]{1,0:T(8,128)(2,1)S(1)}, u32[]{:S(2)}, u32[]{:S(2)}) collective-permute-start(bf16[384,128]{1,0:T(8,128)(2,1)S(1)} %get-tuple-element.39.mom_ref), channel_id=1, source_target_pairs={{1,2},{3,4},{5,6},{7,8},{9,10},{11,12},{13,14},{15,16},{17,18},{19... | collective-permute-start | bytes 294920 | tf_op jit(solution)/shard_map/ppermute | solution.py:600
  53.4 7.2 %collective-permute-done.3.rb_any = bf16[384,128]{1,0:T(8,128)(2,1)S(1)} collective-permute-done((bf16[384,128]{1,0:T(8,128)(2,1)S(1)}, bf16[384,128]{1,0:T(8,128)(2,1)S(1)}, u32[]{:S(2)}, u32[]{:S(2)}) %collective-permute-start.3) | collective-permute-done | bytes 98336 | tf_op jit(solution)/shard_map/ppermute | solution.py:600
  60.5 7.1 %shard_map.118 = (f32[16,32,256]{2,1,0:T(8,128)}, f32[32,1024]{1,0:T(8,128)S(1)}) custom-call(s32[6,16]{1,0:T(8,128)} %bitcast.25, s32[8,16]{1,0:T(8,128)} %bitcast.27, bf16[16,32,256]{2,1,0:T(8,128)(2,1)} %get-tuple-element.38.sb_hbm, bf16[384,128]{1,0:T(8,128)(2,1)S(1)} %get-tuple-element.39.mom_ref, ...), custom_call_target="tpu_custom_call" | custom-call | flops 1000000000 | bytes 16000000 | tf_op jit(solution)/shard_map/pallas_call | solution.py:613
  67.7 0.0 all-to-all-done.1.gathered_ref
  67.7 2.3 %shard_map.119 = (f32[16,32,256]{2,1,0:T(8,128)S(1)}, f32[16,32,256]{2,1,0:T(8,128)S(1)}, f32[16,32,256]{2,1,0:T(8,128)S(1)}, f32[128,1,128]{2,1,0:T(1,128)S(1)}, f32[32,128]{1,0:T(8,128)S(1)}) custom-call(bf16[416,128]{1,0:T(8,128)(2,1)S(1)} %collective-permute-done.2.ra_ref.ra_any, bf16[64,32,128]{2,1,0:T(8,128)(2,1)S(1)} %all-to-all-done.1.gathered_ref, ...), custom_call_target="tpu_custom_call" | custom-call | tf_op jit(solution)/shard_map/pallas_call | solution.py:687
  70.0 18.8 %all_to_all.15.gathered_ref = f32[128,1,128]{2,1,0:T(1,128)S(1)} all-to-all(f32[128,1,128]{2,1,0:T(1,128)S(1)} %get-tuple-element.47), channel_id=1, replica_groups=mesh['leaf'=128] {'leaf'}, dimensions={0} | all-to-all | bytes 131072 | tf_op jit(solution)/shard_map/all_to_all | solution.py:702
  88.8 1.2 %shard_map.120 = (f32[16,32,256]{2,1,0:T(8,128)}, f32[6,32]{1,0:T(8,128)}) custom-call(f32[16,32,256]{2,1,0:T(8,128)S(1)} %get-tuple-element.43.one_ref, f32[16,32,256]{2,1,0:T(8,128)S(1)} %get-tuple-element.44.two_ref, f32[16,32,256]{2,1,0:T(8,128)S(1)} %get-tuple-element.45.v_ref, f32[32,128]{1,0:T(8,128)S(1)} %get-tuple-element.46.scal_ref, ...), custom_call_target="tpu_custom_call" | custom-call | tf_op jit(solution)/shard_map/pallas_call | solution.py:703
Async XLA Ops:
  0.6 28.2 %copy-start = (bf16[16,8,64,64]{3,2,1,0:T(8,128)(2,1)S(1)}, bf16[16,8,64,64]{3,2,1,0:T(8,128)(2,1)}, u32[]{:S(2)}) copy-start(bf16[16,8,64,64]{3,2,1,0:T(8,128)(2,1)} %param.15) | copy-start | bytes 3145732
  5.2 2.4 %collective-permute-start = (bf16[416,128]{1,0:T(8,128)(2,1)S(1)}, bf16[416,128]{1,0:T(8,128)(2,1)S(1)}, u32[]{:S(2)}, u32[]{:S(2)}) collective-permute-start(bf16[416,128]{1,0:T(8,128)(2,1)S(1)} %get-tuple-element.25), channel_id=1, source_target_pairs={{0,1},{1,0},{2,3},{3,2},{4,5},{5,4},{6,7},{7,6},{8,9},{9,8},{10,11... | collective-permute-start | bytes 319496 | tf_op jit(solution)/shard_map/ppermute | solution.py:599
  8.8 27.2 %all-to-all-start = ((bf16[64,32,128]{2,1,0:T(8,128)(2,1)}), bf16[64,32,128]{2,1,0:T(8,128)(2,1)S(1)}, u32[]{:S(2)}, u32[]{:S(2)}) async-start(bf16[64,32,128]{2,1,0:T(8,128)(2,1)} %shard_map.114), calls=%async_computation | async-start | bytes 1048576 | tf_op jit(solution)/shard_map/all_to_all | solution.py:609
  20.1 8.8 %collective-permute-start.1 = (bf16[384,128]{1,0:T(8,128)(2,1)S(1)}, bf16[384,128]{1,0:T(8,128)(2,1)S(1)}, u32[]{:S(2)}, u32[]{:S(2)}) collective-permute-start(bf16[384,128]{1,0:T(8,128)(2,1)S(1)} %get-tuple-element.32.mom_ref), channel_id=1, source_target_pairs={{1,2},{3,4},{5,6},{7,8},{9,10},{11,12},{13,14},{15,16},{17,18},{19... | collective-permute-start | bytes 294920 | tf_op jit(solution)/shard_map/ppermute | solution.py:600
  38.8 7.1 %collective-permute-start.2 = (bf16[416,128]{1,0:T(8,128)(2,1)S(1)}, bf16[416,128]{1,0:T(8,128)(2,1)S(1)}, u32[]{:S(2)}, u32[]{:S(2)}) collective-permute-start(bf16[416,128]{1,0:T(8,128)(2,1)S(1)} %get-tuple-element.35), channel_id=1, source_target_pairs={{0,1},{1,0},{2,3},{3,2},{4,5},{5,4},{6,7},{7,6},{8,9},{9,8},{10,11... | collective-permute-start | bytes 319496 | tf_op jit(solution)/shard_map/ppermute | solution.py:599
  47.2 20.4 %all-to-all-start.1 = ((bf16[64,32,128]{2,1,0:T(8,128)(2,1)}), bf16[64,32,128]{2,1,0:T(8,128)(2,1)S(1)}, u32[]{:S(2)}, u32[]{:S(2)}) async-start(bf16[64,32,128]{2,1,0:T(8,128)(2,1)} %shard_map.117), calls=%async_computation.1 | async-start | bytes 1048576 | tf_op jit(solution)/shard_map/all_to_all | solution.py:609
  51.9 8.7 %collective-permute-start.3 = (bf16[384,128]{1,0:T(8,128)(2,1)S(1)}, bf16[384,128]{1,0:T(8,128)(2,1)S(1)}, u32[]{:S(2)}, u32[]{:S(2)}) collective-permute-start(bf16[384,128]{1,0:T(8,128)(2,1)S(1)} %get-tuple-element.39.mom_ref), channel_id=1, source_target_pairs={{1,2},{3,4},{5,6},{7,8},{9,10},{11,12},{13,14},{15,16},{17,18},{19... | collective-permute-start | bytes 294920 | tf_op jit(solution)/shard_map/ppermute | solution.py:600

commit v5 on v4

--- a/solution.py
+++ b/solution.py
@@ -249,21 +249,26 @@
     joined = jnp.concatenate([even_side[:, :RANK], odd_side[:, :RANK]], axis=1).astype(BF16)
     moment = dot(joined, up_ref[...]).astype(BF16)
     levels = dot(moment, path_ref[...])
-    sums = sums_block([read_sum(both, j) for j in range(n_sums)])
-    low = lanes() < RANK
+    parts = [part for j in range(n_sums) for part in three_parts(read_sum(both, j))]
+    sums = jnp.zeros((8, 128), F32)
+    for p, part in enumerate(parts):
+        sums = jnp.where(rows((8, 128)) == p, as_row(part, 0), sums)
+    half = RHS // 2
+    low = lanes((half, 128)) < RANK
     outs = []
     at = 0
     for level in range(LEVELS):
         count = 1 if level == 0 else 1 << (level - 1)
         if level == 0:
-            block, first = sums, chip
+            packed, first = jnp.zeros((half, 128), F32), chip
         else:
             group = levels[:, (level - 1) // 2 * 128 : (level + 1) // 2 * 128]
+            turned = pltpu.roll(group, RANK, 1)
             if level % 2 == 0:
-                group = pltpu.roll(group, RANK, 1)
-            block = jnp.where(low, group, sums)
+                group, turned = turned, group
+            packed = jnp.where(low, group[:half], turned[half:])
             first = ((chip >> (level - 1)) ^ 1) << (level - 1)
-        block = block.astype(BF16)
+        block = jnp.concatenate([packed, sums], axis=0).astype(BF16)
         copies = min(count, COPIES)
         for c in range(copies):
             block_ref[at + c] = block
@@ -373,13 +378,21 @@
     sibling = ra_ref[BOX_AT:PAIR_ROWS, :][:, :RANK]
     downward = dot(sibling, couple_zero_ref[...])
     for level in range(1, LEVELS):
-        level_sum = jnp.zeros((RHS, 128), F32)
+        level_sum = jnp.zeros(GATHERED[1:], F32)
         for x in range(1 << (level - 1), 1 << level):
             level_sum = level_sum + gathered_ref[chip ^ x].astype(F32)
         total = total + level_sum
         path = down_path_ref[(level - 1) * RANK : level * RANK, :]
-        downward = downward + dot_nt(level_sum[:, :RANK].astype(BF16), path)
+        packed = level_sum[: RHS // 2]
+        local = jnp.concatenate([packed[:, :RANK], packed[:, RANK:]], axis=0)
+        downward = downward + dot_nt(local.astype(BF16), path)
     return downward.astype(BF16), total
+
+
+def gathered_sum(total, j):
+    row = rows((8, 128))
+    parts = jnp.where((row >= 3 * j) & (row < 3 * j + 3), total[RHS // 2 :], 0.0)
+    return as_column(jnp.sum(parts, axis=0, keepdims=True), 0)
 
 
 def spread_of(downward, far_ref, basis_ref, transfer_ref):
@@ -415,7 +428,7 @@
         copy.wait()
     spread = spread_of(downward, far_ref, basis_ref, transfer_ref)
     outs = []
-    square = read_sum(total, 0)
+    square = gathered_sum(total, 0)
     norm = jnp.sqrt(square + EPSILON)
     scal_ref[...] = jnp.where(lanes() == 0, norm, square)
     inputs = []
@@ -472,8 +485,8 @@
     spread = spread_of(downward, far_ref, basis_ref, transfer_ref)
     norm = scal_in_ref[:, 0:1]
     one_one = (scal_in_ref[:, 1:2] / norm) / norm
-    first_inner = read_sum(total, 0)
-    image_square = read_sum(total, 1)
+    first_inner = gathered_sum(total, 0)
+    image_square = gathered_sum(total, 1)
     residue = image_square - 2.0 * first_inner * first_inner + first_inner * first_inner * one_one
     residue = jnp.maximum(residue, 0.0)
     first_length = jnp.sqrt(residue + EPSILON)
@@ -535,7 +548,7 @@
 BASIS = (SLOTS * RANK, POINTS)
 TRANSFER = (SLOTS * RANK, RANK)
 TURNED = (RANK * RANK, NODES)
-GATHERED = (CHIPS, RHS, 128)
+GATHERED = (CHIPS, RHS // 2 + 8, 128)
 LEAF_BUFFERS = [(TRANSFER, BF16), (BASIS, BF16), (FIELD, F32), (FIELD, F32)]
 PATH = (LEVELS - 1) * RANK
 WEIGHTS = [
@@ -603,7 +616,7 @@
             pltpu.HBM(GATHERED, BF16),
             [VMEM] * 4,
             HBM,
-            [*vmem(((4 * COPIES, RHS, 128), BF16)), *sems((11,))],
+            [*vmem(((4 * COPIES, *GATHERED[1:]), BF16)), *sems((11,))],
             4,
         )(own, ra, pair_up, out_path)
         gathered = lax.all_to_all(sent, "leaf", 0, 0, axis_index_groups=groups)

time: 90.4 us -> 89.3 us (0.988)
  waiting for transfers between devices: 15.9 us -> 13.1 us
  starting transfers between devices: 26.9 us -> 28 us
    ppermute x2, waiting for transfers between devices: 14 us -> 11.1 us  [exchange(): rb = lax.ppermute(pb, 'leaf', across)]
    all_to_all x2, starting transfers between devices: 15.9 us -> 16.9 us  [exchange(): gathered = lax.all_to_all(sent, 'leaf', 0, 0, axis_index_groups=groups)]
where the time goes in v5:
time: 89.3 us; the launch traced here: 89 us
  starting transfers between devices  28 us (31%)
  Pallas kernels  27.7 us (31%)
  blocking collectives  19.5 us (22%)
  waiting for transfers between devices  13.1 us (15%)
    all_to_all x1, blocking collectives, on_device(): gathered = lax.all_to_all(sent, 'leaf', 0, 0)  19.5 us
    all_to_all x2, starting transfers between devices, exchange(): gathered = lax.all_to_all(sent, 'leaf', 0, 0, axis_index_groups=groups)  16.9 us
    pallas_call x2, Pallas kernels, near_far(): call(near_far_kernel, [pltpu.HBM(FIELD, F32), shape(FAR_FIELD, F32)], [HB...  14.3 us
    ppermute x2, waiting for transfers between devices, exchange(): rb = lax.ppermute(pb, 'leaf', across)  11.1 us
    ppermute x2, starting transfers between devices, exchange(): ra = lax.ppermute(pa, 'leaf', same)  7.55 us
    pallas_call x1, Pallas kernels, on_device(): call(first_kernel, [*PACKED, pltpu.HBM(FIELD, BF16), *WEIGHTS], [HBM] * 6...  4.52 us
    ppermute x2, starting transfers between devices, exchange(): rb = lax.ppermute(pb, 'leaf', across)  3.58 us
    pallas_call x1, Pallas kernels, on_device(): call(middle_kernel, [*PACKED, shape((RHS, 128), F32), pltpu.HBM(FIELD, BF...  2.81 us
  transfers between devices with their start and end apart: 6, of which 4 were waited for; matrix products, arithmetic and copies ran while one was open for 0% of the time, Pallas kernels for 16%

profile of v5, /device:TPU:1, one launch (start us, length us, event | category | flops | bytes accessed | tf_op | source)
XLA Modules:
  0.0 89.0 jit_solution(7154530979977154190)
XLA Ops:
  0.6 0.0 copy-start
  0.6 4.5 %shard_map.113 = (bf16[416,128]{1,0:T(8,128)(2,1)S(1)}, bf16[384,128]{1,0:T(8,128)(2,1)S(1)}, bf16[32,128]{1,0:T(8,128)(2,1)S(1)}, bf16[16,32,256]{2,1,0:T(8,128...) custom-call(s32[16]{0:T(128)} %refs_0_.3, ...), custom_call_target="tpu_custom_call" | custom-call | tf_op jit(solution)/shard_map/pallas_call | solution.py:651
  5.2 1.5 %collective-permute-start = (bf16[416,128]{1,0:T(8,128)(2,1)S(1)}, bf16[416,128]{1,0:T(8,128)(2,1)S(1)}, u32[]{:S(2)}, u32[]{:S(2)}) collective-permute-start(bf16[416,128]{1,0:T(8,128)(2,1)S(1)} %get-tuple-element.25), channel_id=1, source_target_pairs={{0,1},{1,0},{2,3},{3,2},{4,5},{5,4},{6,7},{7,6},{8,9},{9,8},{10,11... | collective-permute-start | bytes 319496 | tf_op jit(solution)/shard_map/ppermute | solution.py:612
  6.6 1.0 %collective-permute-done.ra_ref.ra_any = bf16[416,128]{1,0:T(8,128)(2,1)S(1)} collective-permute-done((bf16[416,128]{1,0:T(8,128)(2,1)S(1)}, bf16[416,128]{1,0:T(8,128)(2,1)S(1)}, u32[]{:S(2)}, u32[]{:S(2)}) %collective-permute-start) | collective-permute-done | bytes 106528 | tf_op jit(solution)/shard_map/ppermute | solution.py:612
  7.6 1.2 %shard_map.114 = bf16[64,24,128]{2,1,0:T(8,128)(2,1)} custom-call(bf16[32,128]{1,0:T(8,128)(2,1)S(1)} %get-tuple-element.26.own_ref, bf16[416,128]{1,0:T(8,128)(2,1)S(1)} %collective-permute-done.ra_ref.ra_any, bf16[128,64]{1,0:T(8,128)(2,1)S(1)} %get-tuple-element.27.up_ref, bf16[64,384]{1,0:T(8,128)(2,1)S(1)} %get-tuple-element.28.path_ref), custom_call_target="tpu_custom_call" | custom-call | tf_op jit(solution)/shard_map/pallas_call | solution.py:614
  8.8 11.3 %all-to-all-start = ((bf16[64,24,128]{2,1,0:T(8,128)(2,1)}), bf16[64,24,128]{2,1,0:T(8,128)(2,1)S(1)}, u32[]{:S(2)}, u32[]{:S(2)}) async-start(bf16[64,24,128]{2,1,0:T(8,128)(2,1)} %shard_map.114), calls=%async_computation | async-start | bytes 786432 | tf_op jit(solution)/shard_map/all_to_all | solution.py:622
  20.1 1.9 %collective-permute-start.1 = (bf16[384,128]{1,0:T(8,128)(2,1)S(1)}, bf16[384,128]{1,0:T(8,128)(2,1)S(1)}, u32[]{:S(2)}, u32[]{:S(2)}) collective-permute-start(bf16[384,128]{1,0:T(8,128)(2,1)S(1)} %get-tuple-element.32.mom_ref), channel_id=1, source_target_pairs={{1,2},{3,4},{5,6},{7,8},{9,10},{11,12},{13,14},{15,16},{17,18},{19... | collective-permute-start | bytes 294920 | tf_op jit(solution)/shard_map/ppermute | solution.py:613
  22.0 5.5 %collective-permute-done.1.rb_any = bf16[384,128]{1,0:T(8,128)(2,1)S(1)} collective-permute-done((bf16[384,128]{1,0:T(8,128)(2,1)S(1)}, bf16[384,128]{1,0:T(8,128)(2,1)S(1)}, u32[]{:S(2)}, u32[]{:S(2)}) %collective-permute-start.1) | collective-permute-done | bytes 98336 | tf_op jit(solution)/shard_map/ppermute | solution.py:613
  27.5 0.0 copy-done
  27.5 7.1 %shard_map.115 = (f32[16,32,256]{2,1,0:T(8,128)}, f32[32,1024]{1,0:T(8,128)S(1)}) custom-call(s32[6,16]{1,0:T(8,128)} %bitcast.24, s32[8,16]{1,0:T(8,128)} %bitcast.26, bf16[16,32,256]{2,1,0:T(8,128)(2,1)} %get-tuple-element.31.sb_hbm, bf16[384,128]{1,0:T(8,128)(2,1)S(1)} %get-tuple-element.32.mom_ref, ...), custom_call_target="tpu_custom_call" | custom-call | flops 1000000000 | bytes 16000000 | tf_op jit(solution)/shard_map/pallas_call | solution.py:626
  34.6 0.0 all-to-all-done.gathered_ref
  34.6 2.8 %shard_map.116 = (bf16[416,128]{1,0:T(8,128)(2,1)S(1)}, bf16[384,128]{1,0:T(8,128)(2,1)S(1)}, bf16[32,128]{1,0:T(8,128)(2,1)S(1)}, f32[32,128]{1,0:T(8,128)S(1)}...) custom-call(bf16[416,128]{1,0:T(8,128)(2,1)S(1)} %collective-permute-done.ra_ref.ra_any, ...), custom_call_target="tpu_custom_call" | custom-call | tf_op jit(solution)/shard_map/pallas_call | solution.py:678
  37.4 6.1 %collective-permute-start.2 = (bf16[416,128]{1,0:T(8,128)(2,1)S(1)}, bf16[416,128]{1,0:T(8,128)(2,1)S(1)}, u32[]{:S(2)}, u32[]{:S(2)}) collective-permute-start(bf16[416,128]{1,0:T(8,128)(2,1)S(1)} %get-tuple-element.35), channel_id=1, source_target_pairs={{0,1},{1,0},{2,3},{3,2},{4,5},{5,4},{6,7},{7,6},{8,9},{9,8},{10,11... | collective-permute-start | bytes 319496 | tf_op jit(solution)/shard_map/ppermute | solution.py:612
  43.5 1.0 %collective-permute-done.2.ra_ref.ra_any = bf16[416,128]{1,0:T(8,128)(2,1)S(1)} collective-permute-done((bf16[416,128]{1,0:T(8,128)(2,1)S(1)}, bf16[416,128]{1,0:T(8,128)(2,1)S(1)}, u32[]{:S(2)}, u32[]{:S(2)}) %collective-permute-start.2) | collective-permute-done | bytes 106528 | tf_op jit(solution)/shard_map/ppermute | solution.py:612
  44.5 1.2 %shard_map.117 = bf16[64,24,128]{2,1,0:T(8,128)(2,1)} custom-call(bf16[32,128]{1,0:T(8,128)(2,1)S(1)} %get-tuple-element.36.own_ref, bf16[416,128]{1,0:T(8,128)(2,1)S(1)} %collective-permute-done.2.ra_ref.ra_any, bf16[128,64]{1,0:T(8,128)(2,1)S(1)} %get-tuple-element.27.up_ref, bf16[64,384]{1,0:T(8,128)(2,1)S(1)} %get-tuple-element.28.path_ref), custom_call_target="tpu_custom_call" | custom-call | tf_op jit(solution)/shard_map/pallas_call | solution.py:614
  45.7 5.6 %all-to-all-start.1 = ((bf16[64,24,128]{2,1,0:T(8,128)(2,1)}), bf16[64,24,128]{2,1,0:T(8,128)(2,1)S(1)}, u32[]{:S(2)}, u32[]{:S(2)}) async-start(bf16[64,24,128]{2,1,0:T(8,128)(2,1)} %shard_map.117), calls=%async_computation.1 | async-start | bytes 786432 | tf_op jit(solution)/shard_map/all_to_all | solution.py:622
  51.3 1.7 %collective-permute-start.3 = (bf16[384,128]{1,0:T(8,128)(2,1)S(1)}, bf16[384,128]{1,0:T(8,128)(2,1)S(1)}, u32[]{:S(2)}, u32[]{:S(2)}) collective-permute-start(bf16[384,128]{1,0:T(8,128)(2,1)S(1)} %get-tuple-element.39.mom_ref), channel_id=1, source_target_pairs={{1,2},{3,4},{5,6},{7,8},{9,10},{11,12},{13,14},{15,16},{17,18},{19... | collective-permute-start | bytes 294920 | tf_op jit(solution)/shard_map/ppermute | solution.py:613
  53.0 5.7 %collective-permute-done.3.rb_any = bf16[384,128]{1,0:T(8,128)(2,1)S(1)} collective-permute-done((bf16[384,128]{1,0:T(8,128)(2,1)S(1)}, bf16[384,128]{1,0:T(8,128)(2,1)S(1)}, u32[]{:S(2)}, u32[]{:S(2)}) %collective-permute-start.3) | collective-permute-done | bytes 98336 | tf_op jit(solution)/shard_map/ppermute | solution.py:613
  58.7 7.1 %shard_map.118 = (f32[16,32,256]{2,1,0:T(8,128)}, f32[32,1024]{1,0:T(8,128)S(1)}) custom-call(s32[6,16]{1,0:T(8,128)} %bitcast.25, s32[8,16]{1,0:T(8,128)} %bitcast.27, bf16[16,32,256]{2,1,0:T(8,128)(2,1)} %get-tuple-element.38.sb_hbm, bf16[384,128]{1,0:T(8,128)(2,1)S(1)} %get-tuple-element.39.mom_ref, ...), custom_call_target="tpu_custom_call" | custom-call | flops 1000000000 | bytes 16000000 | tf_op jit(solution)/shard_map/pallas_call | solution.py:626
  65.8 0.0 all-to-all-done.1.gathered_ref
  65.9 2.3 %shard_map.119 = (f32[16,32,256]{2,1,0:T(8,128)S(1)}, f32[16,32,256]{2,1,0:T(8,128)S(1)}, f32[16,32,256]{2,1,0:T(8,128)S(1)}, f32[128,1,128]{2,1,0:T(1,128)S(1)}, f32[32,128]{1,0:T(8,128)S(1)}) custom-call(bf16[416,128]{1,0:T(8,128)(2,1)S(1)} %collective-permute-done.2.ra_ref.ra_any, bf16[64,24,128]{2,1,0:T(8,128)(2,1)S(1)} %all-to-all-done.1.gathered_ref, ...), custom_call_target="tpu_custom_call" | custom-call | tf_op jit(solution)/shard_map/pallas_call | solution.py:700
  68.2 19.5 %all_to_all.15.gathered_ref = f32[128,1,128]{2,1,0:T(1,128)S(1)} all-to-all(f32[128,1,128]{2,1,0:T(1,128)S(1)} %get-tuple-element.47), channel_id=1, replica_groups=mesh['leaf'=128] {'leaf'}, dimensions={0} | all-to-all | bytes 131072 | tf_op jit(solution)/shard_map/all_to_all | solution.py:715
  87.7 1.2 %shard_map.120 = (f32[16,32,256]{2,1,0:T(8,128)}, f32[6,32]{1,0:T(8,128)}) custom-call(f32[16,32,256]{2,1,0:T(8,128)S(1)} %get-tuple-element.43.one_ref, f32[16,32,256]{2,1,0:T(8,128)S(1)} %get-tuple-element.44.two_ref, f32[16,32,256]{2,1,0:T(8,128)S(1)} %get-tuple-element.45.v_ref, f32[32,128]{1,0:T(8,128)S(1)} %get-tuple-element.46.scal_ref, ...), custom_call_target="tpu_custom_call" | custom-call | tf_op jit(solution)/shard_map/pallas_call | solution.py:716
Async XLA Ops:
  0.6 26.8 %copy-start = (bf16[16,8,64,64]{3,2,1,0:T(8,128)(2,1)S(1)}, bf16[16,8,64,64]{3,2,1,0:T(8,128)(2,1)}, u32[]{:S(2)}) copy-start(bf16[16,8,64,64]{3,2,1,0:T(8,128)(2,1)} %param.15) | copy-start | bytes 3145732
  5.2 2.4 %collective-permute-start = (bf16[416,128]{1,0:T(8,128)(2,1)S(1)}, bf16[416,128]{1,0:T(8,128)(2,1)S(1)}, u32[]{:S(2)}, u32[]{:S(2)}) collective-permute-start(bf16[416,128]{1,0:T(8,128)(2,1)S(1)} %get-tuple-element.25), channel_id=1, source_target_pairs={{0,1},{1,0},{2,3},{3,2},{4,5},{5,4},{6,7},{7,6},{8,9},{9,8},{10,11... | collective-permute-start | bytes 319496 | tf_op jit(solution)/shard_map/ppermute | solution.py:612
  8.8 25.8 %all-to-all-start = ((bf16[64,24,128]{2,1,0:T(8,128)(2,1)}), bf16[64,24,128]{2,1,0:T(8,128)(2,1)S(1)}, u32[]{:S(2)}, u32[]{:S(2)}) async-start(bf16[64,24,128]{2,1,0:T(8,128)(2,1)} %shard_map.114), calls=%async_computation | async-start | bytes 786432 | tf_op jit(solution)/shard_map/all_to_all | solution.py:622
  20.1 7.4 %collective-permute-start.1 = (bf16[384,128]{1,0:T(8,128)(2,1)S(1)}, bf16[384,128]{1,0:T(8,128)(2,1)S(1)}, u32[]{:S(2)}, u32[]{:S(2)}) collective-permute-start(bf16[384,128]{1,0:T(8,128)(2,1)S(1)} %get-tuple-element.32.mom_ref), channel_id=1, source_target_pairs={{1,2},{3,4},{5,6},{7,8},{9,10},{11,12},{13,14},{15,16},{17,18},{19... | collective-permute-start | bytes 294920 | tf_op jit(solution)/shard_map/ppermute | solution.py:613
  37.4 7.0 %collective-permute-start.2 = (bf16[416,128]{1,0:T(8,128)(2,1)S(1)}, bf16[416,128]{1,0:T(8,128)(2,1)S(1)}, u32[]{:S(2)}, u32[]{:S(2)}) collective-permute-start(bf16[416,128]{1,0:T(8,128)(2,1)S(1)} %get-tuple-element.35), channel_id=1, source_target_pairs={{0,1},{1,0},{2,3},{3,2},{4,5},{5,4},{6,7},{7,6},{8,9},{9,8},{10,11... | collective-permute-start | bytes 319496 | tf_op jit(solution)/shard_map/ppermute | solution.py:612
  45.7 20.1 %all-to-all-start.1 = ((bf16[64,24,128]{2,1,0:T(8,128)(2,1)}), bf16[64,24,128]{2,1,0:T(8,128)(2,1)S(1)}, u32[]{:S(2)}, u32[]{:S(2)}) async-start(bf16[64,24,128]{2,1,0:T(8,128)(2,1)} %shard_map.117), calls=%async_computation.1 | async-start | bytes 786432 | tf_op jit(solution)/shard_map/all_to_all | solution.py:622
  51.3 7.4 %collective-permute-start.3 = (bf16[384,128]{1,0:T(8,128)(2,1)S(1)}, bf16[384,128]{1,0:T(8,128)(2,1)S(1)}, u32[]{:S(2)}, u32[]{:S(2)}) collective-permute-start(bf16[384,128]{1,0:T(8,128)(2,1)S(1)} %get-tuple-element.39.mom_ref), channel_id=1, source_target_pairs={{1,2},{3,4},{5,6},{7,8},{9,10},{11,12},{13,14},{15,16},{17,18},{19... | collective-permute-start | bytes 294920 | tf_op jit(solution)/shard_map/ppermute | solution.py:613
